TPU v7x, 512 devices: a whole 4x4x16 slice. The times are simulated.
512 devices in a mesh: sta: 16 (over z), grp: 8 (over y, core), hr: 4 (over x).
Axes of the slice: x: 4, y: 4, z: 16, core: 2. Of those that a mesh axis runs over, the one named last changes fastest.
Arguments:
- spectra: bfloat16 [4, 128, 6, 8192], P('hr', 'sta'), may hold values from -6 to 6
- pair_source: int32 [2048], P(('sta', 'grp')), may hold values from 0 to 7
- pair_owner: int32 [2048, 1], P(('sta', 'grp')), may hold values from 0 to 15; in each aligned block of 16 rows (0 to 15, 16 to 31, ...) at most 2 rows name the same one
- pair_row: int32 [2048], P(('sta', 'grp')), may hold values from 0 to 7
Outputs:
- stacked: float32 [2048, 9, 1024], P(('sta', 'grp'))
Inputs may be any that keep to these rules, and one draw needn't show every extreme that they name: `pair_owner`: in each aligned block of 16 pairs (the pairs of one device) no value is named by more than 2 pairs, and in some block one value is named by exactly 2 pairs.
All inputs are finite; a program needn't handle non-finite values.
Results may differ from a plain program's by a relative error of at most 0.0032.
Values may be sent and summed in bfloat16 or wider, within the bound.
No kernel may reach another device: no remote copies, remote signals or barrier semaphores. Data moves between devices by JAX's collectives and lax.ppermute only.
A program may use at most 128 MiB of HBM per device.

v0:
```python
import math

import jax
import jax.numpy as jnp
from jax import lax
from jax.sharding import PartitionSpec as P

LAGS = 1024


two_pi = 2.0 * math.pi


def lag_table(start_bin, block_size, num_bins):
    bin_index = start_bin + jnp.arange(block_size, dtype=jnp.int32)
    lag_shift = jnp.arange(LAGS, dtype=jnp.int32) - LAGS // 2
    period = 2 * num_bins
    angles = jnp.mod(bin_index[:, None] * lag_shift[None, :], period).astype(jnp.float32) * (
        two_pi / period
    )
    return jnp.concatenate([jnp.cos(angles), -jnp.sin(angles)], axis=0).astype(jnp.bfloat16)


def cross_block(src_blk, rcv_blk):
    source_part = src_blk.astype(jnp.float32)
    recv_part = rcv_blk.astype(jnp.float32)
    src_re = source_part[..., 0:3, :][..., :, None, :]
    src_im = source_part[..., 3:6, :][..., :, None, :]
    rcv_re = recv_part[..., 0:3, :][..., None, :, :]
    rcv_im = recv_part[..., 3:6, :][..., None, :, :]
    cross_re = src_re * rcv_re + src_im * rcv_im
    cross_im = src_re * rcv_im - src_im * rcv_re
    return jnp.concatenate([cross_re, cross_im], axis=-1).astype(jnp.bfloat16)


def window_taper():
    lag_pos = jnp.arange(LAGS, dtype=jnp.float32)
    return 0.75 - 0.25 * jnp.cos(two_pi * (lag_pos + 0.5) / LAGS)


def slot_layout(owners, pair_row, peer_count, slot_cap):
    onehot = (owners[:, None] == jnp.arange(peer_count, dtype=jnp.int32)[None, :]).astype(jnp.int32)
    before = jnp.cumsum(onehot, axis=0) - onehot
    slot_rank = jnp.sum(before * onehot, axis=1)
    slot_index = owners * slot_cap + slot_rank
    request_table = jnp.zeros((peer_count * slot_cap,), jnp.int32).at[slot_index].set(pair_row)
    return (slot_index, request_table)


def body(spectra, pair_source, pair_owner, pair_row):
    hours_dev, sta_dev, comp_rows, num_bins = spectra.shape
    pair_count = pair_source.shape[0]
    owners = pair_owner[:, 0]
    peer_count = lax.axis_size("sta")
    slot_cap = 2 * pair_count // peer_count
    slot_index, request_table = slot_layout(owners, pair_row, peer_count, slot_cap)
    slot_owner = jnp.arange(peer_count * slot_cap, dtype=jnp.int32) // slot_cap
    wanted_station = slot_owner * sta_dev + request_table
    picked = jnp.take(lax.all_gather(spectra, "sta", axis=1, tiled=True), wanted_station, axis=1)
    receivers = jnp.take(picked, slot_index, axis=1)
    sources = jnp.take(spectra, pair_source, axis=1)
    block_size = min(512, num_bins)
    row_count = hours_dev * pair_count * 9

    def add_block(block_index, running):
        start_bin = (block_index * block_size).astype(jnp.int32)
        src_blk = lax.dynamic_slice_in_dim(sources, start_bin, block_size, 3)
        rcv_blk = lax.dynamic_slice_in_dim(receivers, start_bin, block_size, 3)
        cross = cross_block(src_blk, rcv_blk).reshape(row_count, 2 * block_size)
        table = lag_table(start_bin, block_size, num_bins)
        return running + jnp.dot(cross, table, preferred_element_type=jnp.float32)

    running = lax.fori_loop(
        0, num_bins // block_size, add_block, jnp.zeros((row_count, LAGS), jnp.float32)
    )
    local_sum = jnp.sum(running.reshape(hours_dev, pair_count, 9, LAGS), axis=0)
    stacked_sum = lax.psum(local_sum, "hr")
    hour_total = hours_dev * lax.axis_size("hr")
    return stacked_sum * window_taper()[None, None, :] / (hour_total * math.sqrt(num_bins))


def solution(mesh):
    placed = (
        P("hr", "sta", None, None),
        P(("sta", "grp")),
        P(("sta", "grp"), None),
        P(("sta", "grp")),
    )
    return jax.shard_map(
        body, mesh=mesh, in_specs=placed, out_specs=P(("sta", "grp"), None, None), check_vma=False
    )
```

profile of v0, /device:TPU:8, one launch (start us, length us, event | category | flops | bytes accessed | tf_op | source)
XLA Modules:
  0.0 459.1 jit_solution(4330169677160378186)
XLA Ops:
  10.8 151.2 %all-gather.2.cloned.1.call-done = bf16[1,128,6,8192]{3,1,2,0:T(8,128)(2,1)} async-done(((bf16[1,8,6,8192]{3,1,2,0:T(8,128)(2,1)}), bf16[1,128,6,8192]{3,1,2,0:T(8,128)(2,1)}) %all-gather.2.cloned.1.call-update) | async-done | bytes 12582928 | tf_op jit(solution)/shard_map/all_gather | solution.py:59
  161.9 13.8 %copy.16 = bf16[1,128,6,8192]{3,2,1,0:T(8,128)(2,1)} copy(bf16[1,128,6,8192]{3,1,2,0:T(8,128)(2,1)} %all-gather.2.cloned.1.call-done) | data formatting | bytes 25165824 | tf_op jit(solution)/shard_map/all_gather | solution.py:59
  175.7 8.5 %gather_fusion.1 = bf16[32,6,8192]{2,1,0:T(8,128)(2,1)} fusion(bf16[128,6,8192]{2,1,0:T(8,128)(2,1)} %bitcast.37, s32[1024]{0:T(1024)S(1)} %pad_clamp_fusion.1), kind=kCustom, calls=%fused_computation.1 | custom fusion | bytes 6291584 | tf_op jit(solution)/shard_map/jit(_take)/gather | solution.py:59
  184.2 4.7 %fusion.14 = bf16[32,6,8192]{2,1,0:T(8,128)(2,1)} fusion(bf16[32,6,8192]{2,1,0:T(8,128)(2,1)} %gather_fusion.1, pred[32]{0:T(512)(128)(4,1)S(1)} %get-tuple-element.143), kind=kLoop, calls=%fused_computation.35 | loop fusion | flops 1572864 | bytes 6291488 | tf_op jit(solution)/shard_map/jit(_take)/select_n | solution.py:59
  188.9 4.2 gather_fusion.2
  193.1 4.2 bitcast_select_fusion.1
  197.3 193.9 %while.16 = (s32[]{:T(128)}, f32[144,1024]{1,0:T(8,128)}, bf16[1,16,6,8192]{3,2,1,0:T(8,128)(2,1)}, bf16[1,16,6,8192]{3,2,1,0:T(8,128)(2,1)}, s32[]{:T(128)}, /*index=5*/s32[]{:T(128)}, s32[]{:T(128)}, s32[]{:T(128)}) while((s32[]{:T(128)}, f32[144,1024]{1,0:T(8,128)}, bf16[1,16,6,8192]{3,2,1,0:T(8,128)(2,1)}, ...), condition=%wide.region_4.5_spmd.clone, body=%wide.region_3.4_spmd.clone.sunk | while | flops 316671488 | bytes 13054157 | solution.py:73
  198.9 9.0 %cosine_convert_fusion.2 = (bf16[512,1024]{1,0:T(8,128)(2,1)S(1)}, bf16[512,1024]{1,0:T(8,128)(2,1)S(1)}) fusion(s32[1024]{0:T(1024)S(1)} %iota_add_fusion.4, s32[512]{0:T(512)S(1)} %iota_add_fusion.5), kind=kLoop, calls=%fused_computation.17.clone.1 | loop fusion | flops 8912896 | bytes 2103296 | tf_op jit(solution)/shard_map/convert
  211.1 9.0 %cosine_convert_fusion.2 = (bf16[512,1024]{1,0:T(8,128)(2,1)S(1)}, bf16[512,1024]{1,0:T(8,128)(2,1)S(1)}) fusion(s32[1024]{0:T(1024)S(1)} %iota_add_fusion.4, s32[512]{0:T(512)S(1)} %iota_add_fusion.5), kind=kLoop, calls=%fused_computation.17.clone.1 | loop fusion | flops 8912896 | bytes 2103296 | tf_op jit(solution)/shard_map/convert
  223.2 9.0 %cosine_convert_fusion.2 = (bf16[512,1024]{1,0:T(8,128)(2,1)S(1)}, bf16[512,1024]{1,0:T(8,128)(2,1)S(1)}) fusion(s32[1024]{0:T(1024)S(1)} %iota_add_fusion.4, s32[512]{0:T(512)S(1)} %iota_add_fusion.5), kind=kLoop, calls=%fused_computation.17.clone.1 | loop fusion | flops 8912896 | bytes 2103296 | tf_op jit(solution)/shard_map/convert
  235.3 9.0 %cosine_convert_fusion.2 = (bf16[512,1024]{1,0:T(8,128)(2,1)S(1)}, bf16[512,1024]{1,0:T(8,128)(2,1)S(1)}) fusion(s32[1024]{0:T(1024)S(1)} %iota_add_fusion.4, s32[512]{0:T(512)S(1)} %iota_add_fusion.5), kind=kLoop, calls=%fused_computation.17.clone.1 | loop fusion | flops 8912896 | bytes 2103296 | tf_op jit(solution)/shard_map/convert
  247.4 9.0 %cosine_convert_fusion.2 = (bf16[512,1024]{1,0:T(8,128)(2,1)S(1)}, bf16[512,1024]{1,0:T(8,128)(2,1)S(1)}) fusion(s32[1024]{0:T(1024)S(1)} %iota_add_fusion.4, s32[512]{0:T(512)S(1)} %iota_add_fusion.5), kind=kLoop, calls=%fused_computation.17.clone.1 | loop fusion | flops 8912896 | bytes 2103296 | tf_op jit(solution)/shard_map/convert
  259.5 9.0 %cosine_convert_fusion.2 = (bf16[512,1024]{1,0:T(8,128)(2,1)S(1)}, bf16[512,1024]{1,0:T(8,128)(2,1)S(1)}) fusion(s32[1024]{0:T(1024)S(1)} %iota_add_fusion.4, s32[512]{0:T(512)S(1)} %iota_add_fusion.5), kind=kLoop, calls=%fused_computation.17.clone.1 | loop fusion | flops 8912896 | bytes 2103296 | tf_op jit(solution)/shard_map/convert
  271.6 9.0 %cosine_convert_fusion.2 = (bf16[512,1024]{1,0:T(8,128)(2,1)S(1)}, bf16[512,1024]{1,0:T(8,128)(2,1)S(1)}) fusion(s32[1024]{0:T(1024)S(1)} %iota_add_fusion.4, s32[512]{0:T(512)S(1)} %iota_add_fusion.5), kind=kLoop, calls=%fused_computation.17.clone.1 | loop fusion | flops 8912896 | bytes 2103296 | tf_op jit(solution)/shard_map/convert
  283.8 9.0 %cosine_convert_fusion.2 = (bf16[512,1024]{1,0:T(8,128)(2,1)S(1)}, bf16[512,1024]{1,0:T(8,128)(2,1)S(1)}) fusion(s32[1024]{0:T(1024)S(1)} %iota_add_fusion.4, s32[512]{0:T(512)S(1)} %iota_add_fusion.5), kind=kLoop, calls=%fused_computation.17.clone.1 | loop fusion | flops 8912896 | bytes 2103296 | tf_op jit(solution)/shard_map/convert
  295.9 9.0 %cosine_convert_fusion.2 = (bf16[512,1024]{1,0:T(8,128)(2,1)S(1)}, bf16[512,1024]{1,0:T(8,128)(2,1)S(1)}) fusion(s32[1024]{0:T(1024)S(1)} %iota_add_fusion.4, s32[512]{0:T(512)S(1)} %iota_add_fusion.5), kind=kLoop, calls=%fused_computation.17.clone.1 | loop fusion | flops 8912896 | bytes 2103296 | tf_op jit(solution)/shard_map/convert
  308.0 9.0 %cosine_convert_fusion.2 = (bf16[512,1024]{1,0:T(8,128)(2,1)S(1)}, bf16[512,1024]{1,0:T(8,128)(2,1)S(1)}) fusion(s32[1024]{0:T(1024)S(1)} %iota_add_fusion.4, s32[512]{0:T(512)S(1)} %iota_add_fusion.5), kind=kLoop, calls=%fused_computation.17.clone.1 | loop fusion | flops 8912896 | bytes 2103296 | tf_op jit(solution)/shard_map/convert
  320.1 9.0 %cosine_convert_fusion.2 = (bf16[512,1024]{1,0:T(8,128)(2,1)S(1)}, bf16[512,1024]{1,0:T(8,128)(2,1)S(1)}) fusion(s32[1024]{0:T(1024)S(1)} %iota_add_fusion.4, s32[512]{0:T(512)S(1)} %iota_add_fusion.5), kind=kLoop, calls=%fused_computation.17.clone.1 | loop fusion | flops 8912896 | bytes 2103296 | tf_op jit(solution)/shard_map/convert
  332.2 9.0 %cosine_convert_fusion.2 = (bf16[512,1024]{1,0:T(8,128)(2,1)S(1)}, bf16[512,1024]{1,0:T(8,128)(2,1)S(1)}) fusion(s32[1024]{0:T(1024)S(1)} %iota_add_fusion.4, s32[512]{0:T(512)S(1)} %iota_add_fusion.5), kind=kLoop, calls=%fused_computation.17.clone.1 | loop fusion | flops 8912896 | bytes 2103296 | tf_op jit(solution)/shard_map/convert
  344.4 9.0 %cosine_convert_fusion.2 = (bf16[512,1024]{1,0:T(8,128)(2,1)S(1)}, bf16[512,1024]{1,0:T(8,128)(2,1)S(1)}) fusion(s32[1024]{0:T(1024)S(1)} %iota_add_fusion.4, s32[512]{0:T(512)S(1)} %iota_add_fusion.5), kind=kLoop, calls=%fused_computation.17.clone.1 | loop fusion | flops 8912896 | bytes 2103296 | tf_op jit(solution)/shard_map/convert
  356.5 9.0 %cosine_convert_fusion.2 = (bf16[512,1024]{1,0:T(8,128)(2,1)S(1)}, bf16[512,1024]{1,0:T(8,128)(2,1)S(1)}) fusion(s32[1024]{0:T(1024)S(1)} %iota_add_fusion.4, s32[512]{0:T(512)S(1)} %iota_add_fusion.5), kind=kLoop, calls=%fused_computation.17.clone.1 | loop fusion | flops 8912896 | bytes 2103296 | tf_op jit(solution)/shard_map/convert
  368.6 9.0 %cosine_convert_fusion.2 = (bf16[512,1024]{1,0:T(8,128)(2,1)S(1)}, bf16[512,1024]{1,0:T(8,128)(2,1)S(1)}) fusion(s32[1024]{0:T(1024)S(1)} %iota_add_fusion.4, s32[512]{0:T(512)S(1)} %iota_add_fusion.5), kind=kLoop, calls=%fused_computation.17.clone.1 | loop fusion | flops 8912896 | bytes 2103296 | tf_op jit(solution)/shard_map/convert
  380.7 9.0 %cosine_convert_fusion.2 = (bf16[512,1024]{1,0:T(8,128)(2,1)S(1)}, bf16[512,1024]{1,0:T(8,128)(2,1)S(1)}) fusion(s32[1024]{0:T(1024)S(1)} %iota_add_fusion.4, s32[512]{0:T(512)S(1)} %iota_add_fusion.5), kind=kLoop, calls=%fused_computation.17.clone.1 | loop fusion | flops 8912896 | bytes 2103296 | tf_op jit(solution)/shard_map/convert
  393.6 56.8 %all-reduce.2.cloned.1.call-done = f32[16,9,1024]{2,0,1:T(8,128)} async-done(((f32[16,9,1024]{2,0,1:T(8,128)}), f32[16,9,1024]{2,0,1:T(8,128)}) %all-reduce.2.cloned.1.call-update) | async-done | bytes 589840 | tf_op jit(solution)/shard_map/psum | solution.py:77
  (234 shorter events, 56.3 us)
Async XLA Ops:
  6.5 2.4 copy-start.2
  6.5 3.4 copy-start.3
  6.5 155.4 %all-gather.2.cloned.1.call-start = ((), (), s32[]{:S(2)}) async-start(), calls=%async_computation | async-start | bytes 13369344 | tf_op jit(solution)/shard_map/all_gather | solution.py:59
  7.3 443.1 %all-reduce.2.cloned.1.call-start = ((), (), s32[]{:S(2)}) async-start(), calls=%async_computation.1 | async-start | bytes 1179648 | tf_op jit(solution)/shard_map/psum | solution.py:77
  198.4 9.6 %copy-start = (f32[144,1024]{1,0:T(8,128)S(1)}, f32[144,1024]{1,0:T(8,128)}, u32[]{:S(2)}) copy-start(f32[144,1024]{1,0:T(8,128)} %get-tuple-element.211) | copy-start | bytes 1769476 | tf_op jit(solution)/shard_map/while
  210.5 9.6 %copy-start = (f32[144,1024]{1,0:T(8,128)S(1)}, f32[144,1024]{1,0:T(8,128)}, u32[]{:S(2)}) copy-start(f32[144,1024]{1,0:T(8,128)} %get-tuple-element.211) | copy-start | bytes 1769476 | tf_op jit(solution)/shard_map/while
  220.7 0.8 copy-start.1
  222.6 9.6 %copy-start = (f32[144,1024]{1,0:T(8,128)S(1)}, f32[144,1024]{1,0:T(8,128)}, u32[]{:S(2)}) copy-start(f32[144,1024]{1,0:T(8,128)} %get-tuple-element.211) | copy-start | bytes 1769476 | tf_op jit(solution)/shard_map/while
  234.7 9.6 %copy-start = (f32[144,1024]{1,0:T(8,128)S(1)}, f32[144,1024]{1,0:T(8,128)}, u32[]{:S(2)}) copy-start(f32[144,1024]{1,0:T(8,128)} %get-tuple-element.211) | copy-start | bytes 1769476 | tf_op jit(solution)/shard_map/while
  246.8 9.6 %copy-start = (f32[144,1024]{1,0:T(8,128)S(1)}, f32[144,1024]{1,0:T(8,128)}, u32[]{:S(2)}) copy-start(f32[144,1024]{1,0:T(8,128)} %get-tuple-element.211) | copy-start | bytes 1769476 | tf_op jit(solution)/shard_map/while
  257.0 0.8 copy-start.1
  259.0 9.6 %copy-start = (f32[144,1024]{1,0:T(8,128)S(1)}, f32[144,1024]{1,0:T(8,128)}, u32[]{:S(2)}) copy-start(f32[144,1024]{1,0:T(8,128)} %get-tuple-element.211) | copy-start | bytes 1769476 | tf_op jit(solution)/shard_map/while
  269.2 0.8 copy-start.1
  271.1 9.6 %copy-start = (f32[144,1024]{1,0:T(8,128)S(1)}, f32[144,1024]{1,0:T(8,128)}, u32[]{:S(2)}) copy-start(f32[144,1024]{1,0:T(8,128)} %get-tuple-element.211) | copy-start | bytes 1769476 | tf_op jit(solution)/shard_map/while
  283.2 9.6 %copy-start = (f32[144,1024]{1,0:T(8,128)S(1)}, f32[144,1024]{1,0:T(8,128)}, u32[]{:S(2)}) copy-start(f32[144,1024]{1,0:T(8,128)} %get-tuple-element.211) | copy-start | bytes 1769476 | tf_op jit(solution)/shard_map/while
  295.3 9.6 %copy-start = (f32[144,1024]{1,0:T(8,128)S(1)}, f32[144,1024]{1,0:T(8,128)}, u32[]{:S(2)}) copy-start(f32[144,1024]{1,0:T(8,128)} %get-tuple-element.211) | copy-start | bytes 1769476 | tf_op jit(solution)/shard_map/while
  305.5 0.8 copy-start.1
  307.4 9.6 %copy-start = (f32[144,1024]{1,0:T(8,128)S(1)}, f32[144,1024]{1,0:T(8,128)}, u32[]{:S(2)}) copy-start(f32[144,1024]{1,0:T(8,128)} %get-tuple-element.211) | copy-start | bytes 1769476 | tf_op jit(solution)/shard_map/while
  319.5 9.6 %copy-start = (f32[144,1024]{1,0:T(8,128)S(1)}, f32[144,1024]{1,0:T(8,128)}, u32[]{:S(2)}) copy-start(f32[144,1024]{1,0:T(8,128)} %get-tuple-element.211) | copy-start | bytes 1769476 | tf_op jit(solution)/shard_map/while
  331.7 9.6 %copy-start = (f32[144,1024]{1,0:T(8,128)S(1)}, f32[144,1024]{1,0:T(8,128)}, u32[]{:S(2)}) copy-start(f32[144,1024]{1,0:T(8,128)} %get-tuple-element.211) | copy-start | bytes 1769476 | tf_op jit(solution)/shard_map/while
  343.8 9.6 %copy-start = (f32[144,1024]{1,0:T(8,128)S(1)}, f32[144,1024]{1,0:T(8,128)}, u32[]{:S(2)}) copy-start(f32[144,1024]{1,0:T(8,128)} %get-tuple-element.211) | copy-start | bytes 1769476 | tf_op jit(solution)/shard_map/while
  355.9 9.6 %copy-start = (f32[144,1024]{1,0:T(8,128)S(1)}, f32[144,1024]{1,0:T(8,128)}, u32[]{:S(2)}) copy-start(f32[144,1024]{1,0:T(8,128)} %get-tuple-element.211) | copy-start | bytes 1769476 | tf_op jit(solution)/shard_map/while
  368.0 9.6 %copy-start = (f32[144,1024]{1,0:T(8,128)S(1)}, f32[144,1024]{1,0:T(8,128)}, u32[]{:S(2)}) copy-start(f32[144,1024]{1,0:T(8,128)} %get-tuple-element.211) | copy-start | bytes 1769476 | tf_op jit(solution)/shard_map/while
  380.1 9.6 %copy-start = (f32[144,1024]{1,0:T(8,128)S(1)}, f32[144,1024]{1,0:T(8,128)}, u32[]{:S(2)}) copy-start(f32[144,1024]{1,0:T(8,128)} %get-tuple-element.211) | copy-start | bytes 1769476 | tf_op jit(solution)/shard_map/while
  (12 other events, 9.8 us)
Sparse Core Ops, SparseCore 0:
  9.4 152.4 all-gather.1
  393.6 56.6 all-reduce.1
where the time goes:
time: 460 us; the launch traced here: 459 us
  waiting for transfers between devices  209 us (45%)
  other arithmetic  176 us (38%)
  local copies, waits for them, and re-layouts  50.5 us (11%)
  between operations  13.5 us (3%)
  matrix products  9.22 us (2%)
    all_gather x1, waiting for transfers between devices, body(): lax.all_gather(spectra, 'sta', axis=1, tiled=True)  151 us
    another operation x32, other arithmetic  148 us
    psum x1, waiting for transfers between devices, body(): stacked_sum = lax.psum(local_sum, 'hr')  56.8 us
    convert_element_type x16, other arithmetic, cross_block(): recv_part = rcv_blk.astype(jnp.float32)  16.4 us
    all_gather x1, local copies, waits for them, and re-layouts, body(): lax.all_gather(spectra, 'sta', axis=1, tiled=True)  13.8 us
    while x64, local copies, waits for them, and re-layouts  13 us
    dot_general x16, matrix products, add_block(): return running + jnp.dot(cross, table, preferred_element_type=jnp.float32)  9.22 us
  transfers between devices with their start and end apart: 2, of which 2 were waited for; matrix products, arithmetic and copies ran while one was open for 1% of the time, Pallas kernels for 0%

commit v1 on v0

v1 whole, which is shorter than its diff:
```python
import math

import jax
import jax.numpy as jnp
from jax import lax
from jax.experimental import pallas as pl
from jax.experimental.pallas import tpu as pltpu
from jax.sharding import PartitionSpec as P

LAGS = 1024
NZ, NG, NY, NC, NX = 16, 8, 4, 2, 4
SD, PD, NB = 8, 16, 8192
W = NB // NG
WA = 512
FINE = 32
ROWS = NG * PD
CH = 128
TWO_PI = 2.0 * math.pi


def phases(bins):
    lag = jnp.arange(LAGS, dtype=jnp.int32) - LAGS // 2
    ang = jnp.mod(bins[:, None] * lag[None, :], 2 * NB).astype(jnp.float32) * (TWO_PI / (2 * NB))
    return jnp.cos(ang), jnp.sin(ang)


def correlate(ridx_ref, sidx_ref, xa_ref, xb_ref, hc_ref, hs_ref, lc_ref, ls_ref, keep_ref, send_ref, cross, table):
    lc, ls = lc_ref[...], ls_ref[...]

    def fill(i, carry):
        hc, hs = hc_ref[pl.ds(i, 1), :], hs_ref[pl.ds(i, 1), :]
        row = pl.multiple_of(i * FINE, FINE)
        table[pl.ds(row, FINE), :] = (hc * lc - hs * ls).astype(jnp.bfloat16)
        table[pl.ds(W + row, FINE), :] = (-(hs * lc + hc * ls)).astype(jnp.bfloat16)
        return carry

    lax.fori_loop(0, W // FINE, fill, 0)

    station = lax.broadcasted_iota(jnp.int32, (ROWS, NZ * SD), 1)
    pick_r = (station == ridx_ref[...]).astype(jnp.float32).astype(jnp.bfloat16)
    pick_s = (station == sidx_ref[...]).astype(jnp.float32).astype(jnp.bfloat16)
    for k in range(W // CH):
        at = k * CH
        ref, lo = (xa_ref, at) if at < WA else (xb_ref, at - WA)
        rcv, src = [], []
        for comp in range(6):
            x = ref[:, comp, :, lo : lo + CH].astype(jnp.float32).reshape(NZ * SD, CH).astype(jnp.bfloat16)
            rcv.append(jnp.dot(pick_r, x, preferred_element_type=jnp.float32))
            src.append(jnp.dot(pick_s, x, preferred_element_type=jnp.float32))
        for a in range(3):
            for b in range(3):
                r0 = (3 * a + b) * ROWS
                re = src[a] * rcv[b] + src[3 + a] * rcv[3 + b]
                im = src[a] * rcv[3 + b] - src[3 + a] * rcv[b]
                cross[r0 : r0 + ROWS, at : at + CH] = re.astype(jnp.bfloat16)
                cross[r0 : r0 + ROWS, W + at : W + at + CH] = im.astype(jnp.bfloat16)

    half = ROWS // 2
    for n in range(0, LAGS, 256):
        for a in range(3):
            out = jnp.dot(
                cross[a * 3 * ROWS : (a + 1) * 3 * ROWS, :], table[:, n : n + 256], preferred_element_type=jnp.float32
            )
            for b in range(3):
                for k in range(NY):
                    r0 = b * ROWS + k * PD
                    keep_ref[k, 3 * a + b, :, n : n + 256] = out[r0 : r0 + PD]
                    send_ref[k, 3 * a + b, :, n : n + 256] = out[half + r0 : half + r0 + PD].astype(jnp.bfloat16)


def body(spectra, pair_source, pair_owner, pair_row):
    s, g = lax.axis_index("sta"), lax.axis_index("grp")
    y, core = g // NC, g % NC

    code = (pair_owner[:, 0] * SD + pair_row) * (NZ * SD) + s * SD + pair_source
    code = lax.all_to_all(jnp.broadcast_to(code[None], (NG, PD)), "grp", 0, 0, tiled=True).reshape(NY, NC, PD)

    mine = lax.dynamic_slice_in_dim(spectra[0], g * W, W, 2).transpose(1, 0, 2)
    xa = lax.all_gather(mine[:, :, :WA], "sta", axis=0)
    xb = lax.all_gather(mine[:, :, WA:], "sta", axis=0)

    code = lax.dynamic_slice_in_dim(jnp.concatenate([code, code], axis=0), y, NY, 0)
    code = jnp.where(core == 0, code, code[:, ::-1]).transpose(1, 0, 2).reshape(ROWS, 1)
    hc, hs = phases(g * W + FINE * jnp.arange(W // FINE, dtype=jnp.int32))
    lc, ls = phases(jnp.arange(FINE, dtype=jnp.int32))
    shape = (NY, 9, PD, LAGS)
    keep, send = pl.pallas_call(
        correlate,
        out_shape=(jax.ShapeDtypeStruct(shape, jnp.float32), jax.ShapeDtypeStruct(shape, jnp.bfloat16)),
        in_specs=[pl.BlockSpec(memory_space=pltpu.VMEM)] * 8,
        out_specs=(pl.BlockSpec(memory_space=pltpu.VMEM),) * 2,
        scratch_shapes=[pltpu.VMEM((9 * ROWS, 2 * W), jnp.bfloat16), pltpu.VMEM((2 * W, LAGS), jnp.bfloat16)],
        compiler_params=pltpu.CompilerParams(vmem_limit_bytes=48 * 1024 * 1024),
        name="correlate",
    )(code // (NZ * SD), code % (NZ * SD), xa, xb, hc, hs, lc, ls)

    part = keep + lax.ppermute(send, "grp", [(i, i ^ 1) for i in range(NG)]).astype(jnp.float32)
    total = part[0]
    for k in range(1, NY):
        perm = [(i, (i + NC * k) % NG) for i in range(NG)]
        total = total + lax.ppermute(part[k].astype(jnp.bfloat16), "grp", perm).astype(jnp.float32)
    hours = jnp.broadcast_to(total.astype(jnp.bfloat16)[None], (NX, 9, PD, LAGS))
    hours = lax.all_to_all(hours, "hr", 0, 0, tiled=True).astype(jnp.float32)
    stacked = (hours[0] + hours[1] + (hours[2] + hours[3])).transpose(1, 0, 2)
    pos = jnp.arange(LAGS, dtype=jnp.float32)
    taper = 0.75 - 0.25 * jnp.cos(TWO_PI * (pos + 0.5) / LAGS)
    return stacked * (taper / (NX * math.sqrt(NB)))[None, None, :]


def solution(mesh):
    placed = (
        P("hr", "sta", None, None),
        P(("sta", "grp")),
        P(("sta", "grp"), None),
        P(("sta", "grp")),
    )
    return jax.shard_map(
        body, mesh=mesh, in_specs=placed, out_specs=P(("sta", "grp"), None, None), check_vma=False
    )
```

time: 460 us -> 139 us (0.30)
  the two profiles are of different devices: /device:TPU:8 before, /device:TPU:40 now
where the time goes in v1:
time: 139 us
  blocking collectives  71 us (51%)
  waiting for transfers between devices  30.9 us (22%)
  starting transfers between devices  21.6 us (16%)
  Pallas kernels  8.82 us (6%)
  other arithmetic  4.13 us (3%)
  local copies, waits for them, and re-layouts  2.01 us (1%)
    all_gather x1, blocking collectives, body(): xa = lax.all_gather(mine[:, :, :WA], 'sta', axis=0)  38 us
    all_gather x1, blocking collectives, body(): xb = lax.all_gather(mine[:, :, WA:], 'sta', axis=0)  33 us
    all_to_all x1, waiting for transfers between devices, body(): hours = lax.all_to_all(hours, 'hr', 0, 0, tiled=True).astype(jnp.float32)  16.6 us
    ppermute x3, waiting for transfers between devices, body(): lax.ppermute(part[k].astype(jnp.bfloat16), 'grp', perm).astype(jnp.float32)  11.4 us
    ppermute x3, starting transfers between devices, body(): lax.ppermute(part[k].astype(jnp.bfloat16), 'grp', perm).astype(jnp.float32)  10.4 us
    pallas_call x1, Pallas kernels, body(): pl.pallas_call(correlate, out_shape=(jax.ShapeDtypeStruct(shape, jnp.floa...  8.82 us
    all_to_all x1, starting transfers between devices, body(): lax.all_to_all(jnp.broadcast_to(code[None], (NG, PD)), 'grp', 0, 0, tiled...  4.92 us
    all_to_all x1, starting transfers between devices, body(): hours = lax.all_to_all(hours, 'hr', 0, 0, tiled=True).astype(jnp.float32)  4.28 us
  transfers between devices with their start and end apart: 6, of which 5 were waited for; matrix products, arithmetic and copies ran while one was open for 1% of the time, Pallas kernels for 0%

profile of v1, /device:TPU:40, one launch (start us, length us, event | category | flops | bytes accessed | tf_op | source)
XLA Modules:
  0.0 138.6 jit_solution(5450107061878170679)
XLA Ops:
  0.0 0.8 fusion.26
  0.8 0.6 broadcast_in_dim.4
  1.4 4.9 %all-to-all-start = ((s32[8,1,16]{2,1,0:T(1,128)}), s32[8,1,16]{2,1,0:T(1,128)S(1)}, u32[]{:S(2)}, u32[]{:S(2)}) async-start(s32[8,1,16]{2,1,0:T(1,128)} %broadcast_in_dim.4), calls=%async_computation | async-start | bytes 8192 | tf_op jit(solution)/shard_map/all_to_all | solution.py:76
  6.4 38.0 %all-gather = bf16[96,8,512]{2,1,0:T(8,128)(2,1)S(1)} all-gather(bf16[6,8,512]{2,1,0:T(8,128)(2,1)S(1)} %get-tuple-element.15), channel_id=2, replica_groups=mesh['sta'=16,'grp'=8,'hr'=4] {'sta'}, dimensions={0}, use_global_device_ids=true | all-gather | bytes 835584 | tf_op jit(solution)/shard_map/all_gather | solution.py:79
  44.4 33.0 %all-gather.1 = bf16[96,8,512]{2,1,0:T(8,128)(2,1)S(1)} all-gather(bf16[6,8,512]{2,1,0:T(8,128)(2,1)S(1)} %get-tuple-element.14), channel_id=3, replica_groups=mesh['sta'=16,'grp'=8,'hr'=4] {'sta'}, dimensions={0}, use_global_device_ids=true | all-gather | bytes 835584 | tf_op jit(solution)/shard_map/all_gather | solution.py:80
  77.4 1.1 fusion.19
  78.5 0.1 reshape.185
  78.7 8.8 %correlate.1 = (f32[4,9,16,1024]{3,2,1,0:T(8,128)S(1)}, bf16[4,9,16,1024]{3,2,1,0:T(8,128)(2,1)S(1)}) custom-call(s32[128,1]{1,0:T(8,128)S(1)} %get-tuple-element.17.ridx_ref, s32[128,1]{1,0:T(8,128)S(1)} %get-tuple-element.16.sidx_ref, bf16[16,6,8,512]{3,2,1,0:T(8,128)(2,1)S(1)} %bitcast.41, bf16[16,6,8,512]{3,2,1,0:T(8,128)(2,1)S(1)} %bitcast.42, ...), custom_call_target="tpu_custom_call" | custom-call | tf_op jit(solution)/shard_map/correlate/pallas_call | solution.py:87
  87.5 1.9 %collective-permute-start = (bf16[4,9,16,1024]{3,2,1,0:T(8,128)(2,1)S(1)}, bf16[4,9,16,1024]{3,2,1,0:T(8,128)(2,1)S(1)}, u32[]{:S(2)}, u32[]{:S(2)}) collective-permute-start(bf16[4,9,16,1024]{3,2,1,0:T(8,128)(2,1)S(1)} %get-tuple-element.8), channel_id=1, source_target_pairs={{0,4},{4,0},{8,12},{12,8},{16,20},{20,16},{24,28},{28,24},{1,5},{5... | collective-permute-start | bytes 3538952 | tf_op jit(solution)/shard_map/ppermute | solution.py:97
  89.5 2.8 %collective-permute-done = bf16[4,9,16,1024]{3,2,1,0:T(8,128)(2,1)S(1)} collective-permute-done((bf16[4,9,16,1024]{3,2,1,0:T(8,128)(2,1)S(1)}, bf16[4,9,16,1024]{3,2,1,0:T(8,128)(2,1)S(1)}, u32[]{:S(2)}, u32[]{:S(2)}) %collective-permute-start) | collective-permute-done | bytes 1179680 | tf_op jit(solution)/shard_map/ppermute | solution.py:97
  92.3 0.7 fusion.27
  92.9 0.1 slice_bitcast_fusion.3
  93.0 3.4 %collective-permute-start.1 = (bf16[9,16,1024]{2,1,0:T(8,128)(2,1)S(1)}, bf16[9,16,1024]{2,1,0:T(8,128)(2,1)S(1)}, u32[]{:S(2)}, u32[]{:S(2)}) collective-permute-start(bf16[9,16,1024]{2,1,0:T(8,128)(2,1)S(1)} %get-tuple-element.11), channel_id=1, source_target_pairs={{0,8},{4,12},{8,16},{12,20},{16,24},{20,28},{24,0},{28,4},{1,9},{5... | collective-permute-start | bytes 884744 | tf_op jit(solution)/shard_map/ppermute | solution.py:101
  96.4 2.5 %collective-permute-start.2 = (bf16[9,16,1024]{2,1,0:T(8,128)(2,1)S(1)}, bf16[9,16,1024]{2,1,0:T(8,128)(2,1)S(1)}, u32[]{:S(2)}, u32[]{:S(2)}) collective-permute-start(bf16[9,16,1024]{2,1,0:T(8,128)(2,1)S(1)} %get-tuple-element.13), channel_id=1, source_target_pairs={{0,16},{4,20},{8,24},{12,28},{16,0},{20,4},{24,8},{28,12},{1,17},{... | collective-permute-start | bytes 884744 | tf_op jit(solution)/shard_map/ppermute | solution.py:101
  98.9 4.5 %collective-permute-start.3 = (bf16[9,16,1024]{2,1,0:T(8,128)(2,1)S(1)}, bf16[9,16,1024]{2,1,0:T(8,128)(2,1)S(1)}, u32[]{:S(2)}, u32[]{:S(2)}) collective-permute-start(bf16[9,16,1024]{2,1,0:T(8,128)(2,1)S(1)} %get-tuple-element.12), channel_id=1, source_target_pairs={{0,24},{4,28},{8,0},{12,4},{16,8},{20,12},{24,16},{28,20},{1,25},{... | collective-permute-start | bytes 884744 | tf_op jit(solution)/shard_map/ppermute | solution.py:101
  103.5 1.3 collective-permute-done.1
  104.8 5.0 %collective-permute-done.2 = bf16[9,16,1024]{2,1,0:T(8,128)(2,1)S(1)} collective-permute-done((bf16[9,16,1024]{2,1,0:T(8,128)(2,1)S(1)}, bf16[9,16,1024]{2,1,0:T(8,128)(2,1)S(1)}, u32[]{:S(2)}, u32[]{:S(2)}) %collective-permute-start.2) | collective-permute-done | bytes 294944 | tf_op jit(solution)/shard_map/ppermute | solution.py:101
  109.8 5.2 %collective-permute-done.3 = bf16[9,16,1024]{2,1,0:T(8,128)(2,1)S(1)} collective-permute-done((bf16[9,16,1024]{2,1,0:T(8,128)(2,1)S(1)}, bf16[9,16,1024]{2,1,0:T(8,128)(2,1)S(1)}, u32[]{:S(2)}, u32[]{:S(2)}) %collective-permute-start.3) | collective-permute-done | bytes 294944 | tf_op jit(solution)/shard_map/ppermute | solution.py:101
  114.9 0.2 fusion.7
  115.1 1.2 broadcast_in_dim.5
  116.3 4.3 %all-to-all-start.1 = ((bf16[4,9,16,1024]{3,2,1,0:T(8,128)(2,1)}), bf16[4,9,16,1024]{3,2,1,0:T(8,128)(2,1)S(1)}, u32[]{:S(2)}, u32[]{:S(2)}) async-start(bf16[4,9,16,1024]{3,2,1,0:T(8,128)(2,1)} %broadcast_in_dim.5), calls=%async_computation.1 | async-start | bytes 2359296 | tf_op jit(solution)/shard_map/all_to_all | solution.py:103
  120.6 16.6 %all-to-all-done.1 = bf16[4,9,16,1024]{3,2,1,0:T(8,128)(2,1)S(1)} async-done(((bf16[4,9,16,1024]{3,2,1,0:T(8,128)(2,1)}), bf16[4,9,16,1024]{3,2,1,0:T(8,128)(2,1)S(1)}, u32[]{:S(2)}, u32[]{:S(2)}) %all-to-all-start.1) | async-done | bytes 1179680 | tf_op jit(solution)/shard_map/all_to_all | solution.py:103
  137.2 0.3 convert_element_type.48
  137.5 1.0 fusion.3
  (13 shorter events, 0.2 us)
Async XLA Ops:
  0.0 6.3 %copy-start = (bf16[1,8,6,8192]{3,1,2,0:T(8,128)(2,1)S(1)}, bf16[1,8,6,8192]{3,1,2,0:T(8,128)(2,1)}, u32[]{:S(2)}) copy-start(bf16[1,8,6,8192]{3,1,2,0:T(8,128)(2,1)} %param.4) | copy-start | bytes 2359300
  1.4 77.1 %all-to-all-start = ((s32[8,1,16]{2,1,0:T(1,128)}), s32[8,1,16]{2,1,0:T(1,128)S(1)}, u32[]{:S(2)}, u32[]{:S(2)}) async-start(s32[8,1,16]{2,1,0:T(1,128)} %broadcast_in_dim.4), calls=%async_computation | async-start | bytes 8192 | tf_op jit(solution)/shard_map/all_to_all | solution.py:76
  87.5 4.7 %collective-permute-start = (bf16[4,9,16,1024]{3,2,1,0:T(8,128)(2,1)S(1)}, bf16[4,9,16,1024]{3,2,1,0:T(8,128)(2,1)S(1)}, u32[]{:S(2)}, u32[]{:S(2)}) collective-permute-start(bf16[4,9,16,1024]{3,2,1,0:T(8,128)(2,1)S(1)} %get-tuple-element.8), channel_id=1, source_target_pairs={{0,4},{4,0},{8,12},{12,8},{16,20},{20,16},{24,28},{28,24},{1,5},{5... | collective-permute-start | bytes 3538952 | tf_op jit(solution)/shard_map/ppermute | solution.py:97
  93.0 11.7 %collective-permute-start.1 = (bf16[9,16,1024]{2,1,0:T(8,128)(2,1)S(1)}, bf16[9,16,1024]{2,1,0:T(8,128)(2,1)S(1)}, u32[]{:S(2)}, u32[]{:S(2)}) collective-permute-start(bf16[9,16,1024]{2,1,0:T(8,128)(2,1)S(1)} %get-tuple-element.11), channel_id=1, source_target_pairs={{0,8},{4,12},{8,16},{12,20},{16,24},{20,28},{24,0},{28,4},{1,9},{5... | collective-permute-start | bytes 884744 | tf_op jit(solution)/shard_map/ppermute | solution.py:101
  96.4 13.3 %collective-permute-start.2 = (bf16[9,16,1024]{2,1,0:T(8,128)(2,1)S(1)}, bf16[9,16,1024]{2,1,0:T(8,128)(2,1)S(1)}, u32[]{:S(2)}, u32[]{:S(2)}) collective-permute-start(bf16[9,16,1024]{2,1,0:T(8,128)(2,1)S(1)} %get-tuple-element.13), channel_id=1, source_target_pairs={{0,16},{4,20},{8,24},{12,28},{16,0},{20,4},{24,8},{28,12},{1,17},{... | collective-permute-start | bytes 884744 | tf_op jit(solution)/shard_map/ppermute | solution.py:101
  98.9 16.0 %collective-permute-start.3 = (bf16[9,16,1024]{2,1,0:T(8,128)(2,1)S(1)}, bf16[9,16,1024]{2,1,0:T(8,128)(2,1)S(1)}, u32[]{:S(2)}, u32[]{:S(2)}) collective-permute-start(bf16[9,16,1024]{2,1,0:T(8,128)(2,1)S(1)} %get-tuple-element.12), channel_id=1, source_target_pairs={{0,24},{4,28},{8,0},{12,4},{16,8},{20,12},{24,16},{28,20},{1,25},{... | collective-permute-start | bytes 884744 | tf_op jit(solution)/shard_map/ppermute | solution.py:101
  116.3 21.0 %all-to-all-start.1 = ((bf16[4,9,16,1024]{3,2,1,0:T(8,128)(2,1)}), bf16[4,9,16,1024]{3,2,1,0:T(8,128)(2,1)S(1)}, u32[]{:S(2)}, u32[]{:S(2)}) async-start(bf16[4,9,16,1024]{3,2,1,0:T(8,128)(2,1)} %broadcast_in_dim.5), calls=%async_computation.1 | async-start | bytes 2359296 | tf_op jit(solution)/shard_map/all_to_all | solution.py:103

commit v2 on v1

v2 whole, which is shorter than its diff:
```python
import math

import jax
import jax.numpy as jnp
from jax import lax
from jax.experimental import pallas as pl
from jax.experimental.pallas import tpu as pltpu
from jax.sharding import PartitionSpec as P

LAGS = 1024
NZ, NG, NY, NC, NX = 16, 8, 4, 2, 4
SD, PD, NB = 8, 16, 8192
W = NB // NG
FINE = 32
ROWS = NG * PD
CH = 128
TW = LAGS // NX
TWO_PI = 2.0 * math.pi
VMEM_LIMIT = 48 * 1024 * 1024


def phases(bins):
    lag = jnp.arange(LAGS, dtype=jnp.int32) - LAGS // 2
    ang = jnp.mod(bins[:, None] * lag[None, :], 2 * NB).astype(jnp.float32) * (TWO_PI / (2 * NB))
    return jnp.cos(ang), jnp.sin(ang)


def one_hot(index, count):
    column = lax.broadcasted_iota(jnp.int32, (ROWS, count), 1)
    return (column == index).astype(jnp.float32).astype(jnp.bfloat16)


def prepare(sidx_ref, mine_ref, hc_ref, hs_ref, lc_ref, ls_ref, table, src):
    lc, ls = lc_ref[...], ls_ref[...]

    def fill(i, carry):
        hc, hs = hc_ref[pl.ds(i, 1), :], hs_ref[pl.ds(i, 1), :]
        row = pl.multiple_of(i * FINE, FINE)
        table[pl.ds(row, FINE), :] = (hc * lc - hs * ls).astype(jnp.bfloat16)
        table[pl.ds(W + row, FINE), :] = (-(hs * lc + hc * ls)).astype(jnp.bfloat16)
        return carry

    lax.fori_loop(0, W // FINE, fill, 0)
    pick = one_hot(sidx_ref[...], SD)
    for comp in range(6):
        src[comp] = jnp.dot(pick, mine_ref[comp], preferred_element_type=jnp.float32).astype(jnp.bfloat16)


def correlate(ridx_ref, near_ref, left_ref, right_ref, table, src, keep_ref, send_ref, cross):
    pick = one_hot(ridx_ref[...], NZ * SD)
    for k in range(W // CH):
        at = k * CH
        rcv = []
        for comp in range(6):
            x = [
                ref[:, comp, :, at : at + CH].astype(jnp.float32).reshape(-1, CH)
                for ref in (near_ref, left_ref, right_ref)
            ]
            x = jnp.concatenate(x, axis=0).astype(jnp.bfloat16)
            rcv.append(jnp.dot(pick, x, preferred_element_type=jnp.float32))
        s = [src[comp, :, at : at + CH].astype(jnp.float32) for comp in range(6)]
        for a in range(3):
            for b in range(3):
                r0 = (3 * a + b) * ROWS
                re = s[a] * rcv[b] + s[3 + a] * rcv[3 + b]
                im = s[a] * rcv[3 + b] - s[3 + a] * rcv[b]
                cross[r0 : r0 + ROWS, at : at + CH] = re.astype(jnp.bfloat16)
                cross[r0 : r0 + ROWS, W + at : W + at + CH] = im.astype(jnp.bfloat16)

    half = ROWS // 2
    for n in range(NX):
        for a in range(3):
            out = jnp.dot(
                cross[a * 3 * ROWS : (a + 1) * 3 * ROWS, :],
                table[:, n * TW : (n + 1) * TW],
                preferred_element_type=jnp.float32,
            )
            for b in range(3):
                for k in range(NY):
                    r0 = b * ROWS + k * PD
                    keep_ref[k, n, 3 * a + b] = out[r0 : r0 + PD]
                    send_ref[k, n, 3 * a + b] = out[half + r0 : half + r0 + PD].astype(jnp.bfloat16)


def vmem(n):
    return [pl.BlockSpec(memory_space=pltpu.VMEM)] * n


def body(spectra, pair_source, pair_owner, pair_row):
    s, g = lax.axis_index("sta"), lax.axis_index("grp")
    core, parity = g % NC, s % 2

    mine = lax.dynamic_slice_in_dim(spectra[0], g * W, W, 2).transpose(1, 0, 2)
    planes = [list(range(p, NZ, 2)) for p in range(2)]
    near = lax.all_gather(mine, "sta", axis=0, axis_index_groups=planes)
    left = lax.ppermute(near[: NZ // 4], "sta", [(i, (i + 1) % NZ) for i in range(NZ)])
    right = lax.ppermute(near[NZ // 4 :], "sta", [(i, (i - 1) % NZ) for i in range(NZ)])

    owner = pair_owner[:, 0]
    slot = jnp.where(owner % 2 == parity, 0, NZ // 2) + owner // 2
    code = (slot * SD + pair_row) * SD + pair_source
    code = jnp.broadcast_to(code[None], (NG, PD))
    code, near = lax.optimization_barrier((code, near))
    code = lax.all_to_all(code, "grp", 0, 0, tiled=True).reshape(NY, NC, PD)
    code = jnp.where(core == 0, code, code[:, ::-1]).transpose(1, 0, 2).reshape(ROWS, 1)

    hc, hs = phases(g * W + FINE * jnp.arange(W // FINE, dtype=jnp.int32))
    lc, ls = phases(jnp.arange(FINE, dtype=jnp.int32))
    params = pltpu.CompilerParams(vmem_limit_bytes=VMEM_LIMIT)
    table, src = pl.pallas_call(
        prepare,
        out_shape=(
            jax.ShapeDtypeStruct((2 * W, LAGS), jnp.bfloat16),
            jax.ShapeDtypeStruct((6, ROWS, W), jnp.bfloat16),
        ),
        in_specs=vmem(6),
        out_specs=tuple(vmem(2)),
        compiler_params=params,
        name="prepare",
    )(code % SD, mine, hc, hs, lc, ls)
    shape = (NY, NX, 9, PD, TW)
    keep, send = pl.pallas_call(
        correlate,
        out_shape=(jax.ShapeDtypeStruct(shape, jnp.float32), jax.ShapeDtypeStruct(shape, jnp.bfloat16)),
        in_specs=vmem(6),
        out_specs=tuple(vmem(2)),
        scratch_shapes=[pltpu.VMEM((9 * ROWS, 2 * W), jnp.bfloat16)],
        compiler_params=params,
        name="correlate",
    )(code // SD, near, left, right, table, src)

    part = keep + lax.ppermute(send, "grp", [(i, i ^ 1) for i in range(NG)]).astype(jnp.float32)
    part = part.astype(jnp.bfloat16).reshape(NY * NX, 9, PD, TW)
    chips = [[(NC * y + c) * NX + x for y in range(NY) for x in range(NX)] for c in range(NC)]
    part = lax.all_to_all(part, ("grp", "hr"), 0, 0, axis_index_groups=chips, tiled=True)
    total = jnp.sum(part.astype(jnp.float32), axis=0)
    pos = lax.axis_index("hr") * TW + jnp.arange(TW, dtype=jnp.int32)
    taper = 0.75 - 0.25 * jnp.cos(TWO_PI * (pos.astype(jnp.float32) + 0.5) / LAGS)
    total = total * (taper / (NX * math.sqrt(NB)))
    return lax.all_gather(total, "hr", axis=2, tiled=True).transpose(1, 0, 2)


def solution(mesh):
    placed = (
        P("hr", "sta", None, None),
        P(("sta", "grp")),
        P(("sta", "grp"), None),
        P(("sta", "grp")),
    )
    return jax.shard_map(
        body, mesh=mesh, in_specs=placed, out_specs=P(("sta", "grp"), None, None), check_vma=False
    )
```

time: 139 us -> 121 us (0.87)
  the two profiles are of different devices: /device:TPU:40 before, /device:TPU:96 now
where the time goes in v2:
time: 121 us
  blocking collectives  48.8 us (40%)
  waiting for transfers between devices  29.9 us (25%)
  starting transfers between devices  19.2 us (16%)
  Pallas kernels  13.9 us (11%)
  other arithmetic  5.15 us (4%)
  local copies, waits for them, and re-layouts  3.47 us (3%)
    all_gather x1, blocking collectives, body(): near = lax.all_gather(mine, 'sta', axis=0, axis_index_groups=planes)  35.8 us
    all_to_all x1, waiting for transfers between devices, body(): lax.all_to_all(part, ('grp', 'hr'), 0, 0, axis_index_groups=chips, tiled=...  19.6 us
    all_gather x1, blocking collectives, body(): return lax.all_gather(total, 'hr', axis=2, tiled=True).transpose(1, 0, 2)  12.9 us
    pallas_call x1, Pallas kernels, body(): pl.pallas_call(correlate, out_shape=(jax.ShapeDtypeStruct(shape, jnp.floa...  10.4 us
    all_to_all x1, starting transfers between devices, body(): lax.all_to_all(part, ('grp', 'hr'), 0, 0, axis_index_groups=chips, tiled=...  7.01 us
    ppermute x1, waiting for transfers between devices, body(): lax.ppermute(near[NZ // 4:], 'sta', [(i, (i - 1) % NZ) for i in range(NZ)])  4.59 us
    all_to_all x1, starting transfers between devices, body(): code = lax.all_to_all(code, 'grp', 0, 0, tiled=True).reshape(NY, NC, PD)  4.47 us
    ppermute x1, starting transfers between devices, body(): lax.ppermute(near[:NZ // 4], 'sta', [(i, (i + 1) % NZ) for i in range(NZ)])  3.85 us
  transfers between devices with their start and end apart: 5, of which 4 were waited for; matrix products, arithmetic and copies ran while one was open for 2% of the time, Pallas kernels for 3%

profile of v2, /device:TPU:96, one launch (start us, length us, event | category | flops | bytes accessed | tf_op | source)
XLA Modules:
  0.0 120.6 jit_solution(14644801611698623879)
XLA Ops:
  0.0 1.1 copy-done
  1.1 35.8 %all-gather = bf16[48,8,1024]{2,1,0:T(8,128)(2,1)S(1)} all-gather(bf16[6,8,1024]{2,1,0:T(8,128)(2,1)S(1)} %dynamic-slice_bitcast_fusion.mine_ref), channel_id=2, replica_groups={{0,64,128,192,256,320,384,448},{32,96,160,224,288,352,416,480},{1,65,12..., dimensions={0}, use_global_device_ids=true | all-gather | bytes 884736 | tf_op jit(solution)/shard_map/all_gather | solution.py:95
  37.0 0.7 multiply_add_fusion.1
  37.7 0.6 broadcast_in_dim.9
  38.3 4.5 %all-to-all-start = ((s32[8,1,16]{2,1,0:T(1,128)}), s32[8,1,16]{2,1,0:T(1,128)S(1)}, u32[]{:S(2)}, u32[]{:S(2)}) async-start(s32[8,1,16]{2,1,0:T(1,128)} %bitcast.5), calls=%async_computation | async-start | bytes 8192 | tf_op jit(solution)/shard_map/all_to_all | solution.py:104
  42.8 0.8 fusion.16
  43.5 3.8 %collective-permute-start = (bf16[4,6,8,1024]{3,2,1,0:T(8,128)(2,1)}, bf16[4,6,8,1024]{3,2,1,0:T(8,128)(2,1)S(1)}, u32[]{:S(2)}, u32[]{:S(2)}) collective-permute-start(bf16[4,6,8,1024]{3,2,1,0:T(8,128)(2,1)} %bitcast.8), channel_id=1, source_target_pairs={{0,32},{32,64},{64,96},{96,128},{128,160},{160,192},{192,224},{224... | collective-permute-start | bytes 1179656 | tf_op jit(solution)/shard_map/ppermute | solution.py:96
  47.4 2.0 %collective-permute-start.1 = (bf16[4,6,8,1024]{3,2,1,0:T(8,128)(2,1)S(1)}, bf16[4,6,8,1024]{3,2,1,0:T(8,128)(2,1)S(1)}, u32[]{:S(2)}, u32[]{:S(2)}) collective-permute-start(bf16[4,6,8,1024]{3,2,1,0:T(8,128)(2,1)S(1)} %bitcast.32), channel_id=1, source_target_pairs={{0,480},{32,0},{64,32},{96,64},{128,96},{160,128},{192,160},{224,1... | collective-permute-start | bytes 1179656 | tf_op jit(solution)/shard_map/ppermute | solution.py:97
  49.4 1.1 fusion.11
  50.5 0.0 all-to-all-done
  50.5 0.1 reshape.180
  50.6 0.1 add_select_fusion.2
  50.7 3.5 %prepare.1 = (bf16[2048,1024]{1,0:T(8,128)(2,1)}, bf16[6,128,1024]{2,1,0:T(8,128)(2,1)S(1)}) custom-call(s32[128,1]{1,0:T(8,128)S(1)} %get-tuple-element.19.sidx_ref, bf16[6,8,1024]{2,1,0:T(8,128)(2,1)S(1)} %dynamic-slice_bitcast_fusion.mine_ref, f32[32,1024]{1,0:T(8,128)S(1)} %get-tuple-element.22.hc_ref, f32[32,1024]{1,0:T(8,128)S(1)} %get-tuple-element.21.hs_ref, ...), custom_call_target="tpu_custom_call" | custom-call | tf_op jit(solution)/shard_map/prepare/pallas_call | solution.py:110
  54.2 2.9 %collective-permute-done.left_ref = bf16[4,6,8,1024]{3,2,1,0:T(8,128)(2,1)S(1)} collective-permute-done((bf16[4,6,8,1024]{3,2,1,0:T(8,128)(2,1)}, bf16[4,6,8,1024]{3,2,1,0:T(8,128)(2,1)S(1)}, u32[]{:S(2)}, u32[]{:S(2)}) %collective-permute-start) | collective-permute-done | bytes 393248 | tf_op jit(solution)/shard_map/ppermute | solution.py:96
  57.2 4.6 %collective-permute-done.1.right_ref = bf16[4,6,8,1024]{3,2,1,0:T(8,128)(2,1)S(1)} collective-permute-done((bf16[4,6,8,1024]{3,2,1,0:T(8,128)(2,1)S(1)}, bf16[4,6,8,1024]{3,2,1,0:T(8,128)(2,1)S(1)}, u32[]{:S(2)}, u32[]{:S(2)}) %collective-permute-start.1) | collective-permute-done | bytes 393248 | tf_op jit(solution)/shard_map/ppermute | solution.py:97
  61.8 10.4 %correlate.1 = (f32[4,4,9,16,256]{4,3,2,1,0:T(8,128)}, bf16[4,4,9,16,256]{4,3,2,1,0:T(8,128)(2,1)S(1)}) custom-call(s32[128,1]{1,0:T(8,128)S(1)} %get-tuple-element.20.ridx_ref, bf16[8,6,8,1024]{3,2,1,0:T(8,128)(2,1)S(1)} %bitcast.30, bf16[4,6,8,1024]{3,2,1,0:T(8,128)(2,1)S(1)} %collective-permute-done.left_ref, ...), custom_call_target="tpu_custom_call" | custom-call | tf_op jit(solution)/shard_map/correlate/pallas_call | solution.py:122
  72.1 1.9 %collective-permute-start.2 = (bf16[4,4,9,16,256]{4,3,2,1,0:T(8,128)(2,1)S(1)}, bf16[4,4,9,16,256]{4,3,2,1,0:T(8,128)(2,1)S(1)}, u32[]{:S(2)}, u32[]{:S(2)}) collective-permute-start(bf16[4,4,9,16,256]{4,3,2,1,0:T(8,128)(2,1)S(1)} %get-tuple-element.16), channel_id=1, source_target_pairs={{0,4},{4,0},{8,12},{12,8},{16,20},{20,16},{24,28},{28,24},{1,5},{5... | collective-permute-start | bytes 3538952 | tf_op jit(solution)/shard_map/ppermute | solution.py:132
  74.1 2.8 %collective-permute-done.2 = bf16[4,4,9,16,256]{4,3,2,1,0:T(8,128)(2,1)S(1)} collective-permute-done((bf16[4,4,9,16,256]{4,3,2,1,0:T(8,128)(2,1)S(1)}, bf16[4,4,9,16,256]{4,3,2,1,0:T(8,128)(2,1)S(1)}, u32[]{:S(2)}, u32[]{:S(2)}) %collective-permute-start.2) | collective-permute-done | bytes 1179680 | tf_op jit(solution)/shard_map/ppermute | solution.py:132
  76.9 3.1 %add_convert_fusion = bf16[4,4,9,16,256]{4,3,2,1,0:T(8,128)(2,1)} fusion(f32[4,4,9,16,256]{4,3,2,1,0:T(8,128)} %get-tuple-element.15, bf16[4,4,9,16,256]{4,3,2,1,0:T(8,128)(2,1)S(1)} %collective-permute-done.2), kind=kLoop, calls=%fused_computation.1 | loop fusion | flops 1769472 | bytes 4718592 | tf_op jit(solution)/shard_map/convert_element_type | solution.py:133
  80.0 7.0 %all-to-all-start.1 = ((bf16[16,9,16,256]{3,2,1,0:T(8,128)(2,1)}), bf16[16,9,16,256]{3,2,1,0:T(8,128)(2,1)S(1)}, u32[]{:S(2)}, u32[]{:S(2)}) async-start(bf16[16,9,16,256]{3,2,1,0:T(8,128)(2,1)} %bitcast.11), calls=%async_computation.1 | async-start | bytes 2359296 | tf_op jit(solution)/shard_map/all_to_all | solution.py:135
  87.0 19.6 %all-to-all-done.1 = bf16[16,9,16,256]{3,2,1,0:T(8,128)(2,1)S(1)} async-done(((bf16[16,9,16,256]{3,2,1,0:T(8,128)(2,1)}), bf16[16,9,16,256]{3,2,1,0:T(8,128)(2,1)S(1)}, u32[]{:S(2)}, u32[]{:S(2)}) %all-to-all-start.1) | async-done | bytes 1179680 | tf_op jit(solution)/shard_map/all_to_all | solution.py:135
  106.6 0.2 convert_reduce_fusion
  106.8 12.9 %all_gather.11 = f32[9,16,1024]{2,1,0:T(8,128)S(1)} all-gather(f32[9,16,256]{2,1,0:T(8,128)S(1)} %broadcast_multiply_fusion), channel_id=1, replica_groups=mesh['sta'=16,'grp'=8,'hr'=4] {'hr'}, dimensions={2}, use_global_device_ids=true | all-gather | bytes 737280 | tf_op jit(solution)/shard_map/all_gather | solution.py:140
  119.7 0.8 copy.17
  (9 shorter events, 0.1 us)
Async XLA Ops:
  0.0 1.1 copy-start
  38.3 12.2 %all-to-all-start = ((s32[8,1,16]{2,1,0:T(1,128)}), s32[8,1,16]{2,1,0:T(1,128)S(1)}, u32[]{:S(2)}, u32[]{:S(2)}) async-start(s32[8,1,16]{2,1,0:T(1,128)} %bitcast.5), calls=%async_computation | async-start | bytes 8192 | tf_op jit(solution)/shard_map/all_to_all | solution.py:104
  43.5 13.6 %collective-permute-start = (bf16[4,6,8,1024]{3,2,1,0:T(8,128)(2,1)}, bf16[4,6,8,1024]{3,2,1,0:T(8,128)(2,1)S(1)}, u32[]{:S(2)}, u32[]{:S(2)}) collective-permute-start(bf16[4,6,8,1024]{3,2,1,0:T(8,128)(2,1)} %bitcast.8), channel_id=1, source_target_pairs={{0,32},{32,64},{64,96},{96,128},{128,160},{160,192},{192,224},{224... | collective-permute-start | bytes 1179656 | tf_op jit(solution)/shard_map/ppermute | solution.py:96
  47.4 14.3 %collective-permute-start.1 = (bf16[4,6,8,1024]{3,2,1,0:T(8,128)(2,1)S(1)}, bf16[4,6,8,1024]{3,2,1,0:T(8,128)(2,1)S(1)}, u32[]{:S(2)}, u32[]{:S(2)}) collective-permute-start(bf16[4,6,8,1024]{3,2,1,0:T(8,128)(2,1)S(1)} %bitcast.32), channel_id=1, source_target_pairs={{0,480},{32,0},{64,32},{96,64},{128,96},{160,128},{192,160},{224,1... | collective-permute-start | bytes 1179656 | tf_op jit(solution)/shard_map/ppermute | solution.py:97
  72.1 4.7 %collective-permute-start.2 = (bf16[4,4,9,16,256]{4,3,2,1,0:T(8,128)(2,1)S(1)}, bf16[4,4,9,16,256]{4,3,2,1,0:T(8,128)(2,1)S(1)}, u32[]{:S(2)}, u32[]{:S(2)}) collective-permute-start(bf16[4,4,9,16,256]{4,3,2,1,0:T(8,128)(2,1)S(1)} %get-tuple-element.16), channel_id=1, source_target_pairs={{0,4},{4,0},{8,12},{12,8},{16,20},{20,16},{24,28},{28,24},{1,5},{5... | collective-permute-start | bytes 3538952 | tf_op jit(solution)/shard_map/ppermute | solution.py:132
  80.0 26.7 %all-to-all-start.1 = ((bf16[16,9,16,256]{3,2,1,0:T(8,128)(2,1)}), bf16[16,9,16,256]{3,2,1,0:T(8,128)(2,1)S(1)}, u32[]{:S(2)}, u32[]{:S(2)}) async-start(bf16[16,9,16,256]{3,2,1,0:T(8,128)(2,1)} %bitcast.11), calls=%async_computation.1 | async-start | bytes 2359296 | tf_op jit(solution)/shard_map/all_to_all | solution.py:135

commit v3 on v2

v3 whole, which is shorter than its diff:
```python
import functools
import math

import jax
import jax.numpy as jnp
from jax import lax
from jax.experimental import pallas as pl
from jax.experimental.pallas import tpu as pltpu
from jax.sharding import PartitionSpec as P

LAGS = 1024
NZ, NG, NY, NC, NX = 16, 8, 4, 2, 4
SD, PD, NB = 8, 16, 8192
W = NB // NG
FINE = 32
HALF = NY * PD
CH = 128
TW = LAGS // NX
TWO_PI = 2.0 * math.pi
VMEM_LIMIT = 24 * 1024 * 1024


def phases(bins):
    lag = jnp.arange(LAGS, dtype=jnp.int32) - LAGS // 2
    ang = jnp.mod(bins[:, None] * lag[None, :], 2 * NB).astype(jnp.float32) * (TWO_PI / (2 * NB))
    return jnp.cos(ang), jnp.sin(ang)


def one_hot(index, count):
    column = lax.broadcasted_iota(jnp.int32, (HALF, count), 1)
    return (column == index).astype(jnp.float32).astype(jnp.bfloat16)


def lag_table(hc_ref, hs_ref, lc_ref, ls_ref, table):
    lc, ls = lc_ref[...], ls_ref[...]

    def fill(i, carry):
        hc, hs = hc_ref[pl.ds(i, 1), :], hs_ref[pl.ds(i, 1), :]
        row = pl.multiple_of(i * FINE, FINE)
        table[pl.ds(row, FINE), :] = (hc * lc - hs * ls).astype(jnp.bfloat16)
        table[pl.ds(W + row, FINE), :] = (-(hs * lc + hc * ls)).astype(jnp.bfloat16)
        return carry

    lax.fori_loop(0, W // FINE, fill, 0)


def correlate(half, ridx_ref, sidx_ref, mine_ref, near_ref, left_ref, right_ref, table, out_ref, cross):
    pick_r = one_hot(ridx_ref[half * HALF : (half + 1) * HALF], NZ * SD)
    pick_s = one_hot(sidx_ref[half * HALF : (half + 1) * HALF], SD)
    for k in range(W // CH):
        at = k * CH
        r, s = [], []
        for comp in range(6):
            x = [
                ref[:, comp, :, at : at + CH].astype(jnp.float32).reshape(-1, CH)
                for ref in (near_ref, left_ref, right_ref)
            ]
            x = jnp.concatenate(x, axis=0).astype(jnp.bfloat16)
            r.append(jnp.dot(pick_r, x, preferred_element_type=jnp.float32))
            s.append(jnp.dot(pick_s, mine_ref[comp, :, at : at + CH], preferred_element_type=jnp.float32))
        for a in range(3):
            for b in range(3):
                r0 = (3 * a + b) * HALF
                re = s[a] * r[b] + s[3 + a] * r[3 + b]
                im = s[a] * r[3 + b] - s[3 + a] * r[b]
                cross[r0 : r0 + HALF, at : at + CH] = re.astype(jnp.bfloat16)
                cross[r0 : r0 + HALF, W + at : W + at + CH] = im.astype(jnp.bfloat16)

    for n in range(NX):
        out = jnp.dot(cross[...], table[:, n * TW : (n + 1) * TW], preferred_element_type=jnp.float32)
        for c in range(9):
            for k in range(NY):
                r0 = c * HALF + k * PD
                out_ref[k, n, c] = out[r0 : r0 + PD].astype(out_ref.dtype)


def correlate_first(ridx, sidx, mine, near, left, right, hc, hs, lc, ls, out_ref, table, cross):
    lag_table(hc, hs, lc, ls, table)
    correlate(0, ridx, sidx, mine, near, left, right, table, out_ref, cross)


def vmem(n):
    return [pl.BlockSpec(memory_space=pltpu.VMEM)] * n


def body(spectra, pair_source, pair_owner, pair_row):
    s, g = lax.axis_index("sta"), lax.axis_index("grp")
    core, parity = g % NC, s % 2

    slot = jnp.where(pair_owner[:, 0] % 2 == parity, 0, NZ // 2) + pair_owner[:, 0] // 2
    code = ((slot * SD + pair_row) * SD + pair_source) * NG
    code = code[None] + lax.broadcasted_iota(jnp.int32, (NG, PD), 0)
    code = lax.all_to_all(code, "grp", 0, 0, tiled=True).reshape(NY, NC, PD) // NG
    code = jnp.where(core == 0, code[:, ::-1], code).transpose(1, 0, 2).reshape(NC * HALF, 1)

    mine = lax.dynamic_slice_in_dim(spectra[0], g * W, W, 2).transpose(1, 0, 2)
    planes = [list(range(p, NZ, 2)) for p in range(2)]
    near = lax.all_gather(mine, "sta", axis=0, axis_index_groups=planes)
    left = lax.ppermute(near[: NZ // 4], "sta", [(i, (i + 1) % NZ) for i in range(NZ)])
    right = lax.ppermute(near[NZ // 4 :], "sta", [(i, (i - 1) % NZ) for i in range(NZ)])

    pos = lax.axis_index("hr") * TW + jnp.arange(TW, dtype=jnp.int32)
    taper = 0.75 - 0.25 * jnp.cos(TWO_PI * (pos.astype(jnp.float32) + 0.5) / LAGS)
    scale = taper / (NX * math.sqrt(NB))
    hc, hs = phases(g * W + FINE * jnp.arange(W // FINE, dtype=jnp.int32))
    lc, ls = phases(jnp.arange(FINE, dtype=jnp.int32))

    ridx, sidx = code // SD, code % SD
    ridx, sidx, scale = lax.optimization_barrier((ridx, sidx, scale))

    shape = (NY, NX, 9, PD, TW)
    scratch = [pltpu.VMEM((9 * HALF, 2 * W), jnp.bfloat16)]
    params = pltpu.CompilerParams(vmem_limit_bytes=VMEM_LIMIT)
    send, table = pl.pallas_call(
        correlate_first,
        out_shape=(jax.ShapeDtypeStruct(shape, jnp.bfloat16), jax.ShapeDtypeStruct((2 * W, LAGS), jnp.bfloat16)),
        in_specs=vmem(10),
        out_specs=tuple(vmem(2)),
        scratch_shapes=scratch,
        compiler_params=params,
        name="correlate_first",
    )(ridx, sidx, mine, near, left, right, hc, hs, lc, ls)
    keep = pl.pallas_call(
        functools.partial(correlate, 1),
        out_shape=jax.ShapeDtypeStruct(shape, jnp.float32),
        in_specs=vmem(7),
        out_specs=vmem(1)[0],
        scratch_shapes=scratch,
        compiler_params=params,
        name="correlate",
    )(ridx, sidx, mine, near, left, right, table)

    part = keep + lax.ppermute(send, "grp", [(i, i ^ 1) for i in range(NG)]).astype(jnp.float32)
    part = part.astype(jnp.bfloat16).reshape(NY * NX, 9, PD, TW)
    chips = [[(NC * y + c) * NX + x for y in range(NY) for x in range(NX)] for c in range(NC)]
    part = lax.all_to_all(part, ("grp", "hr"), 0, 0, axis_index_groups=chips, tiled=True)
    total = jnp.sum(part.astype(jnp.float32), axis=0)
    return lax.all_gather(total * scale, "hr", axis=2, tiled=True).transpose(1, 0, 2)


def solution(mesh):
    placed = (
        P("hr", "sta", None, None),
        P(("sta", "grp")),
        P(("sta", "grp"), None),
        P(("sta", "grp")),
    )
    return jax.shard_map(
        body, mesh=mesh, in_specs=placed, out_specs=P(("sta", "grp"), None, None), check_vma=False
    )
```

time: 121 us -> 110 us (0.909)
  the two profiles are of different devices: /device:TPU:96 before, /device:TPU:32 now
where the time goes in v3:
time: 110 us
  blocking collectives  78.4 us (71%)
  starting transfers between devices  12.2 us (11%)
  Pallas kernels  8.87 us (8%)
  waiting for transfers between devices  5.65 us (5%)
  other arithmetic  3.15 us (3%)
  local copies, waits for them, and re-layouts  1.75 us (2%)
    all_gather x1, blocking collectives, body(): near = lax.all_gather(mine, 'sta', axis=0, axis_index_groups=planes)  39.3 us
    all_to_all x1, blocking collectives, body(): lax.all_to_all(part, ('grp', 'hr'), 0, 0, axis_index_groups=chips, tiled=...  25.5 us
    all_gather x1, blocking collectives, body(): lax.all_gather(total * scale, 'hr', axis=2, tiled=True).transpose(1, 0, 2)  13.6 us
    pallas_call x1, Pallas kernels, body(): pl.pallas_call(correlate_first, out_shape=(jax.ShapeDtypeStruct(shape, jn...  5.22 us
    all_to_all x1, starting transfers between devices, body(): lax.all_to_all(code, 'grp', 0, 0, tiled=True).reshape(NY, NC, PD) // NG  4.47 us
    pallas_call x1, Pallas kernels, body(): pl.pallas_call(functools.partial(correlate, 1), out_shape=jax.ShapeDtypeS...  3.65 us
    ppermute x1, starting transfers between devices, body(): lax.ppermute(near[:NZ // 4], 'sta', [(i, (i + 1) % NZ) for i in range(NZ)])  3.22 us
    ppermute x1, waiting for transfers between devices, body(): lax.ppermute(near[NZ // 4:], 'sta', [(i, (i - 1) % NZ) for i in range(NZ)])  3.02 us
  transfers between devices with their start and end apart: 4, of which 2 were waited for; matrix products, arithmetic and copies ran while one was open for 2% of the time, Pallas kernels for 3%

profile of v3, /device:TPU:32, one launch (start us, length us, event | category | flops | bytes accessed | tf_op | source)
XLA Modules:
  0.0 110.2 jit_solution(17131366008025004600)
XLA Ops:
  0.0 0.0 copy-start
  0.0 0.8 add_multiply_fusion
  0.8 0.6 iota_add_fusion.1
  1.4 4.5 %all-to-all-start = ((s32[8,1,16]{2,1,0:T(1,128)}), s32[8,1,16]{2,1,0:T(1,128)S(1)}, u32[]{:S(2)}, u32[]{:S(2)}) async-start(s32[8,1,16]{2,1,0:T(1,128)} %iota_add_fusion.1), calls=%async_computation | async-start | bytes 8192 | tf_op jit(solution)/shard_map/all_to_all | solution.py:93
  5.8 0.0 copy-done
  5.9 39.3 %all-gather = bf16[48,8,1024]{2,1,0:T(8,128)(2,1)S(1)} all-gather(bf16[6,8,1024]{2,1,0:T(8,128)(2,1)S(1)} %dynamic-slice_bitcast_fusion.mine.mine_ref), channel_id=2, replica_groups={{0,64,128,192,256,320,384,448},{32,96,160,224,288,352,416,480},{1,65,12..., dimensions={0}, use_global_device_ids=true | all-gather | bytes 884736 | tf_op jit(solution)/shard_map/all_gather | solution.py:98
  45.2 0.8 fusion.16
  46.0 3.2 %collective-permute-start = (bf16[4,6,8,1024]{3,2,1,0:T(8,128)(2,1)}, bf16[4,6,8,1024]{3,2,1,0:T(8,128)(2,1)S(1)}, u32[]{:S(2)}, u32[]{:S(2)}) collective-permute-start(bf16[4,6,8,1024]{3,2,1,0:T(8,128)(2,1)} %bitcast.7), channel_id=1, source_target_pairs={{0,32},{32,64},{64,96},{96,128},{128,160},{160,192},{192,224},{224... | collective-permute-start | bytes 1179656 | tf_op jit(solution)/shard_map/ppermute | solution.py:99
  49.2 2.6 %collective-permute-start.1 = (bf16[4,6,8,1024]{3,2,1,0:T(8,128)(2,1)S(1)}, bf16[4,6,8,1024]{3,2,1,0:T(8,128)(2,1)S(1)}, u32[]{:S(2)}, u32[]{:S(2)}) collective-permute-start(bf16[4,6,8,1024]{3,2,1,0:T(8,128)(2,1)S(1)} %bitcast.31), channel_id=1, source_target_pairs={{0,480},{32,0},{64,32},{96,64},{128,96},{160,128},{192,160},{224,1... | collective-permute-start | bytes 1179656 | tf_op jit(solution)/shard_map/ppermute | solution.py:100
  51.9 1.1 fusion.11
  53.0 0.0 all-to-all-done
  53.1 0.1 reshape.194
  53.2 0.1 add_select_fusion.2
  53.2 2.6 %collective-permute-done.left.left_ref = bf16[4,6,8,1024]{3,2,1,0:T(8,128)(2,1)S(1)} collective-permute-done((bf16[4,6,8,1024]{3,2,1,0:T(8,128)(2,1)}, bf16[4,6,8,1024]{3,2,1,0:T(8,128)(2,1)S(1)}, u32[]{:S(2)}, u32[]{:S(2)}) %collective-permute-start) | collective-permute-done | bytes 393248 | tf_op jit(solution)/shard_map/ppermute | solution.py:99
  55.9 3.0 %collective-permute-done.1.right.right_ref = bf16[4,6,8,1024]{3,2,1,0:T(8,128)(2,1)S(1)} collective-permute-done((bf16[4,6,8,1024]{3,2,1,0:T(8,128)(2,1)S(1)}, bf16[4,6,8,1024]{3,2,1,0:T(8,128)(2,1)S(1)}, u32[]{:S(2)}, u32[]{:S(2)}) %collective-permute-start.1) | collective-permute-done | bytes 393248 | tf_op jit(solution)/shard_map/ppermute | solution.py:100
  58.9 5.2 %correlate_first.1 = (bf16[4,4,9,16,256]{4,3,2,1,0:T(8,128)(2,1)S(1)}, bf16[2048,1024]{1,0:T(8,128)(2,1)S(1)}) custom-call(s32[128,1]{1,0:T(8,128)S(1)} %get-tuple-element.10.ridx.ridx_ref, s32[128,1]{1,0:T(8,128)S(1)} %get-tuple-element.11.sidx.sidx_ref, bf16[6,8,1024]{2,1,0:T(8,128)(2,1)S(1)} %dynamic-slice_bitcast_fusion.mine.mine_ref, ...), custom_call_target="tpu_custom_call" | custom-call | tf_op jit(solution)/shard_map/correlate_first/pallas_call | solution.py:114
  64.1 1.9 %collective-permute-start.2 = (bf16[4,4,9,16,256]{4,3,2,1,0:T(8,128)(2,1)S(1)}, bf16[4,4,9,16,256]{4,3,2,1,0:T(8,128)(2,1)S(1)}, u32[]{:S(2)}, u32[]{:S(2)}) collective-permute-start(bf16[4,4,9,16,256]{4,3,2,1,0:T(8,128)(2,1)S(1)} %get-tuple-element.13), channel_id=1, source_target_pairs={{0,4},{4,0},{8,12},{12,8},{16,20},{20,16},{24,28},{28,24},{1,5},{5... | collective-permute-start | bytes 3538952 | tf_op jit(solution)/shard_map/ppermute | solution.py:133
  66.0 3.7 %correlate.1 = f32[4,4,9,16,256]{4,3,2,1,0:T(8,128)S(1)} custom-call(s32[128,1]{1,0:T(8,128)S(1)} %get-tuple-element.10.ridx.ridx_ref, s32[128,1]{1,0:T(8,128)S(1)} %get-tuple-element.11.sidx.sidx_ref, bf16[6,8,1024]{2,1,0:T(8,128)(2,1)S(1)} %dynamic-slice_bitcast_fusion.mine.mine_ref, bf16[8,6,8,1024]{3,2,1,0:T(8,128)(2,1)S(1)} %bitcast.28, ...), custom_call_target="tpu_custom_call" | custom-call | tf_op jit(solution)/shard_map/correlate/pallas_call | solution.py:123
  69.7 0.0 collective-permute-done.2
  69.7 0.4 add_convert_fusion
  70.1 25.5 %all_to_all.11 = bf16[16,9,16,256]{3,2,1,0:T(8,128)(2,1)S(1)} all-to-all(bf16[16,9,16,256]{3,2,1,0:T(8,128)(2,1)S(1)} %bitcast.29), channel_id=1, replica_groups={{0,1,2,3,8,9,10,11,16,17,18,19,24,25,26,27},{4,5,6,7,12,13,14,15,20,21,..., dimensions={0} | all-to-all | bytes 2359296 | tf_op jit(solution)/shard_map/all_to_all | solution.py:136
  95.6 0.2 convert_reduce_fusion
  95.8 13.6 %all_gather.11 = f32[9,16,1024]{2,1,0:T(8,128)S(1)} all-gather(f32[9,16,256]{2,1,0:T(8,128)S(1)} %broadcast_multiply_fusion), channel_id=1, replica_groups=mesh['sta'=16,'grp'=8,'hr'=4] {'hr'}, dimensions={2}, use_global_device_ids=true | all-gather | bytes 737280 | tf_op jit(solution)/shard_map/all_gather | solution.py:138
  109.4 0.8 copy.16
  (9 shorter events, 0.1 us)
Async XLA Ops:
  0.0 5.8 %copy-start = (bf16[1,8,6,8192]{3,1,2,0:T(8,128)(2,1)S(1)}, bf16[1,8,6,8192]{3,1,2,0:T(8,128)(2,1)}, u32[]{:S(2)}) copy-start(bf16[1,8,6,8192]{3,1,2,0:T(8,128)(2,1)} %param.4) | copy-start | bytes 2359300
  1.4 51.6 %all-to-all-start = ((s32[8,1,16]{2,1,0:T(1,128)}), s32[8,1,16]{2,1,0:T(1,128)S(1)}, u32[]{:S(2)}, u32[]{:S(2)}) async-start(s32[8,1,16]{2,1,0:T(1,128)} %iota_add_fusion.1), calls=%async_computation | async-start | bytes 8192 | tf_op jit(solution)/shard_map/all_to_all | solution.py:93
  46.0 9.9 %collective-permute-start = (bf16[4,6,8,1024]{3,2,1,0:T(8,128)(2,1)}, bf16[4,6,8,1024]{3,2,1,0:T(8,128)(2,1)S(1)}, u32[]{:S(2)}, u32[]{:S(2)}) collective-permute-start(bf16[4,6,8,1024]{3,2,1,0:T(8,128)(2,1)} %bitcast.7), channel_id=1, source_target_pairs={{0,32},{32,64},{64,96},{96,128},{128,160},{160,192},{192,224},{224... | collective-permute-start | bytes 1179656 | tf_op jit(solution)/shard_map/ppermute | solution.py:99
  49.2 9.7 %collective-permute-start.1 = (bf16[4,6,8,1024]{3,2,1,0:T(8,128)(2,1)S(1)}, bf16[4,6,8,1024]{3,2,1,0:T(8,128)(2,1)S(1)}, u32[]{:S(2)}, u32[]{:S(2)}) collective-permute-start(bf16[4,6,8,1024]{3,2,1,0:T(8,128)(2,1)S(1)} %bitcast.31), channel_id=1, source_target_pairs={{0,480},{32,0},{64,32},{96,64},{128,96},{160,128},{192,160},{224,1... | collective-permute-start | bytes 1179656 | tf_op jit(solution)/shard_map/ppermute | solution.py:100
  64.1 5.6 %collective-permute-start.2 = (bf16[4,4,9,16,256]{4,3,2,1,0:T(8,128)(2,1)S(1)}, bf16[4,4,9,16,256]{4,3,2,1,0:T(8,128)(2,1)S(1)}, u32[]{:S(2)}, u32[]{:S(2)}) collective-permute-start(bf16[4,4,9,16,256]{4,3,2,1,0:T(8,128)(2,1)S(1)} %get-tuple-element.13), channel_id=1, source_target_pairs={{0,4},{4,0},{8,12},{12,8},{16,20},{20,16},{24,28},{28,24},{1,5},{5... | collective-permute-start | bytes 3538952 | tf_op jit(solution)/shard_map/ppermute | solution.py:133

commit v4 on v3

v4 whole, which is shorter than its diff:
```python
import functools
import math

import jax
import jax.numpy as jnp
from jax import lax
from jax.experimental import pallas as pl
from jax.experimental.pallas import tpu as pltpu
from jax.sharding import PartitionSpec as P

LAGS = 1024
NZ, NG, NY, NC, NX = 16, 8, 4, 2, 4
SD, PD, NB = 8, 16, 8192
W = NB // NG
FINE = 32
HALF = NY * PD
CH = 128
TW = LAGS // NX
TWO_PI = 2.0 * math.pi
VMEM_LIMIT = 24 * 1024 * 1024


def phases(bins):
    lag = jnp.arange(LAGS, dtype=jnp.int32) - LAGS // 2
    ang = jnp.mod(bins[:, None] * lag[None, :], 2 * NB).astype(jnp.float32) * (TWO_PI / (2 * NB))
    return jnp.cos(ang), jnp.sin(ang)


def stage(hc_ref, hs_ref, lc_ref, ls_ref, near_ref, first_ref, second_ref, table, stations):
    lc, ls = lc_ref[...], ls_ref[...]

    def fill(i, carry):
        hc, hs = hc_ref[pl.ds(i, 1), :], hs_ref[pl.ds(i, 1), :]
        row = pl.multiple_of(i * FINE, FINE)
        table[pl.ds(row, FINE), :] = (hc * lc - hs * ls).astype(jnp.bfloat16)
        table[pl.ds(W + row, FINE), :] = (-(hs * lc + hc * ls)).astype(jnp.bfloat16)
        return carry

    lax.fori_loop(0, W // FINE, fill, 0)
    for comp in range(6):
        row = 0
        for ref in (near_ref, first_ref, second_ref):
            x = ref[:, comp].astype(jnp.float32).reshape(-1, W).astype(jnp.bfloat16)
            stations[comp, row : row + x.shape[0]] = x
            row += x.shape[0]


def correlate(other, code_ref, core_ref, mine_ref, stations, table, out_ref, pick_r, pick_s, cross):
    core = core_ref[0] ^ other
    lane = lax.broadcasted_iota(jnp.int32, (1, NZ * SD), 1)

    def mark(p, carry):
        code = code_ref[p // PD * NC + core, p % PD]
        pick_r[pl.ds(p, 1), :] = (lane == code // SD).astype(jnp.float32)
        pick_s[pl.ds(p, 1), :] = (lane == code % SD).astype(jnp.float32)
        return carry

    lax.fori_loop(0, HALF, mark, 0, unroll=8)
    of_r = pick_r[...].astype(jnp.bfloat16)
    of_s = pick_s[:, :SD].astype(jnp.bfloat16)
    for k in range(W // CH):
        at = k * CH
        r, s = [], []
        for comp in range(6):
            r.append(jnp.dot(of_r, stations[comp, :, at : at + CH], preferred_element_type=jnp.float32))
            s.append(jnp.dot(of_s, mine_ref[comp, :, at : at + CH], preferred_element_type=jnp.float32))
        for a in range(3):
            for b in range(3):
                r0 = (3 * a + b) * HALF
                re = s[a] * r[b] + s[3 + a] * r[3 + b]
                im = s[a] * r[3 + b] - s[3 + a] * r[b]
                cross[r0 : r0 + HALF, at : at + CH] = re.astype(jnp.bfloat16)
                cross[r0 : r0 + HALF, W + at : W + at + CH] = im.astype(jnp.bfloat16)

    for n in range(NX):
        out = jnp.dot(cross[...], table[:, n * TW : (n + 1) * TW], preferred_element_type=jnp.float32)
        for c in range(9):
            for k in range(NY):
                r0 = c * HALF + k * PD
                out_ref[k, n, c] = out[r0 : r0 + PD].astype(out_ref.dtype)


def vmem(n):
    return [pl.BlockSpec(memory_space=pltpu.VMEM)] * n


def body(spectra, pair_source, pair_owner, pair_row):
    s, g = lax.axis_index("sta"), lax.axis_index("grp")
    core, parity = g % NC, s % 2

    mine = lax.dynamic_slice_in_dim(spectra[0], g * W, W, 2).transpose(1, 0, 2)
    planes = [list(range(p, NZ, 2)) for p in range(2)]
    near = lax.all_gather(mine, "sta", axis=0, axis_index_groups=planes)

    def neighbour(x, step):
        turn = [step if i % NC == 0 else -step for i in range(NG)]
        perm = [(z * NG + i, (z + turn[i]) % NZ * NG + i) for z in range(NZ) for i in range(NG)]
        return lax.ppermute(x, ("sta", "grp"), perm)

    first = neighbour(near[: NZ // 4], 1)
    second = neighbour(near[NZ // 4 :], -1)

    slot = jnp.where(pair_owner[:, 0] % 2 == parity, 0, NZ // 2) + pair_owner[:, 0] // 2
    code = (slot * SD + pair_row) * SD + pair_source
    pos = lax.axis_index("hr") * TW + jnp.arange(TW, dtype=jnp.int32)
    taper = 0.75 - 0.25 * jnp.cos(TWO_PI * (pos.astype(jnp.float32) + 0.5) / LAGS)
    scale = taper / (NX * math.sqrt(NB))
    hc, hs = phases(g * W + FINE * jnp.arange(W // FINE, dtype=jnp.int32))
    lc, ls = phases(jnp.arange(FINE, dtype=jnp.int32))
    near, code, hc, scale = lax.optimization_barrier((near, code, hc, scale))
    code = lax.all_to_all(jnp.broadcast_to(code[None], (NG, PD)), "grp", 0, 0, tiled=True)
    code, first, second = lax.optimization_barrier((code, first, second))

    params = pltpu.CompilerParams(vmem_limit_bytes=VMEM_LIMIT)
    table, stations = pl.pallas_call(
        stage,
        out_shape=(
            jax.ShapeDtypeStruct((2 * W, LAGS), jnp.bfloat16),
            jax.ShapeDtypeStruct((6, NZ * SD, W), jnp.bfloat16),
        ),
        in_specs=vmem(7),
        out_specs=tuple(vmem(2)),
        compiler_params=params,
        name="stage",
    )(hc, hs, lc, ls, near, first, second)

    def lags(other, dtype):
        return pl.pallas_call(
            functools.partial(correlate, other),
            out_shape=jax.ShapeDtypeStruct((NY, NX, 9, PD, TW), dtype),
            in_specs=[pl.BlockSpec(memory_space=pltpu.SMEM)] * 2 + vmem(3),
            out_specs=vmem(1)[0],
            scratch_shapes=[
                pltpu.VMEM((HALF, NZ * SD), jnp.float32),
                pltpu.VMEM((HALF, NZ * SD), jnp.float32),
                pltpu.VMEM((9 * HALF, 2 * W), jnp.bfloat16),
            ],
            compiler_params=params,
            name="correlate",
        )(code, core[None], mine, stations, table)

    send = lags(1, jnp.bfloat16)
    keep = lags(0, jnp.float32)
    part = keep + lax.ppermute(send, "grp", [(i, i ^ 1) for i in range(NG)]).astype(jnp.float32)
    part = part.astype(jnp.bfloat16).reshape(NY * NX, 9, PD, TW)
    chips = [[(NC * y + c) * NX + x for y in range(NY) for x in range(NX)] for c in range(NC)]
    part = lax.all_to_all(part, ("grp", "hr"), 0, 0, axis_index_groups=chips, tiled=True)
    total = jnp.sum(part.astype(jnp.float32), axis=0)
    return lax.all_gather(total * scale, "hr", axis=2, tiled=True).transpose(1, 0, 2)


def solution(mesh):
    placed = (
        P("hr", "sta", None, None),
        P(("sta", "grp")),
        P(("sta", "grp"), None),
        P(("sta", "grp")),
    )
    return jax.shard_map(
        body, mesh=mesh, in_specs=placed, out_specs=P(("sta", "grp"), None, None), check_vma=False
    )
```

time: 110 us -> 111 us (level)
  the two profiles are of different devices: /device:TPU:32 before, /device:TPU:8 now
where the time goes in v4:
time: 111 us
  blocking collectives  76 us (68%)
  starting transfers between devices  13.9 us (13%)
  Pallas kernels  11.9 us (11%)
  waiting for transfers between devices  3.81 us (3%)
  local copies, waits for them, and re-layouts  3.33 us (3%)
  other arithmetic  1.73 us (2%)
    all_gather x1, blocking collectives, body(): near = lax.all_gather(mine, 'sta', axis=0, axis_index_groups=planes)  38.6 us
    all_to_all x1, blocking collectives, body(): lax.all_to_all(part, ('grp', 'hr'), 0, 0, axis_index_groups=chips, tiled=...  23.7 us
    all_gather x1, blocking collectives, body(): lax.all_gather(total * scale, 'hr', axis=2, tiled=True).transpose(1, 0, 2)  13.6 us
    pallas_call x2, Pallas kernels, lags(): pl.pallas_call(functools.partial(correlate, other), out_shape=jax.ShapeDt...  10.2 us
    ppermute x2, starting transfers between devices, neighbour(): return lax.ppermute(x, ('sta', 'grp'), perm)  7.04 us
    all_to_all x1, starting transfers between devices, body(): lax.all_to_all(jnp.broadcast_to(code[None], (NG, PD)), 'grp', 0, 0, tiled...  4.92 us
    all_to_all x1, waiting for transfers between devices, body(): lax.all_to_all(jnp.broadcast_to(code[None], (NG, PD)), 'grp', 0, 0, tiled...  3.8 us
  transfers between devices with their start and end apart: 4, of which 1 were waited for; matrix products, arithmetic and copies ran while one was open for 2% of the time, Pallas kernels for 5%

profile of v4, /device:TPU:8, one launch (start us, length us, event | category | flops | bytes accessed | tf_op | source)
XLA Modules:
  0.0 110.7 jit_solution(14836519078052216537)
XLA Ops:
  0.0 0.0 copy-start
  0.0 0.0 copy-start.1
  0.0 1.1 %copy-done = bf16[1,8,6,8192]{3,1,2,0:T(8,128)(2,1)S(1)} copy-done((bf16[1,8,6,8192]{3,1,2,0:T(8,128)(2,1)S(1)}, bf16[1,8,6,8192]{3,1,2,0:T(8,128)(2,1)}, u32[]{:S(2)}) %copy-start) | copy-done | bytes 786456
  1.1 38.6 %all-gather = bf16[48,8,1024]{2,1,0:T(8,128)(2,1)S(1)} all-gather(bf16[6,8,1024]{2,1,0:T(8,128)(2,1)S(1)} %dynamic-slice_bitcast_fusion.mine_ref), channel_id=2, replica_groups={{0,64,128,192,256,320,384,448},{32,96,160,224,288,352,416,480},{1,65,12..., dimensions={0}, use_global_device_ids=true | all-gather | bytes 884736 | tf_op jit(solution)/shard_map/all_gather | solution.py:93
  39.7 0.8 fusion.14
  40.5 3.4 %collective-permute-start = (bf16[4,6,8,1024]{3,2,1,0:T(8,128)(2,1)}, bf16[4,6,8,1024]{3,2,1,0:T(8,128)(2,1)S(1)}, u32[]{:S(2)}, u32[]{:S(2)}) collective-permute-start(bf16[4,6,8,1024]{3,2,1,0:T(8,128)(2,1)} %bitcast.5), channel_id=1, source_target_pairs={{0,32},{4,484},{8,40},{12,492},{16,48},{20,500},{24,56},{28,508},{... | collective-permute-start | bytes 1179656 | tf_op jit(solution)/shard_map/ppermute | solution.py:98
  44.0 3.6 %collective-permute-start.1 = (bf16[4,6,8,1024]{3,2,1,0:T(8,128)(2,1)S(1)}, bf16[4,6,8,1024]{3,2,1,0:T(8,128)(2,1)S(1)}, u32[]{:S(2)}, u32[]{:S(2)}) collective-permute-start(bf16[4,6,8,1024]{3,2,1,0:T(8,128)(2,1)S(1)} %bitcast.31), channel_id=1, source_target_pairs={{0,480},{4,36},{8,488},{12,44},{16,496},{20,52},{24,504},{28,60},{... | collective-permute-start | bytes 1179656 | tf_op jit(solution)/shard_map/ppermute | solution.py:98
  47.6 0.0 copy-done.2
  47.7 1.1 fusion.11
  48.8 0.6 broadcast_in_dim.11
  49.4 4.9 %all-to-all-start = ((s32[8,1,16]{2,1,0:T(1,128)}), s32[8,1,16]{2,1,0:T(1,128)S(1)}, u32[]{:S(2)}, u32[]{:S(2)}) async-start(s32[8,1,16]{2,1,0:T(1,128)} %broadcast_in_dim.11), calls=%async_computation | async-start | bytes 8192 | tf_op jit(solution)/shard_map/all_to_all | solution.py:111
  54.3 3.8 %all-to-all-done = s32[8,1,16]{2,1,0:T(1,128)S(1)} async-done(((s32[8,1,16]{2,1,0:T(1,128)}), s32[8,1,16]{2,1,0:T(1,128)S(1)}, u32[]{:S(2)}, u32[]{:S(2)}) %all-to-all-start) | async-done | bytes 544 | tf_op jit(solution)/shard_map/all_to_all | solution.py:111
  58.1 0.0 collective-permute-done.first_ref
  58.1 0.0 collective-permute-done.1.second_ref
  58.1 1.7 %stage.1 = (bf16[2048,1024]{1,0:T(8,128)(2,1)S(1)}, bf16[6,128,1024]{2,1,0:T(8,128)(2,1)S(1)}) custom-call(f32[32,1024]{1,0:T(8,128)S(1)} %get-tuple-element.16.hc_ref, f32[32,1024]{1,0:T(8,128)S(1)} %get-tuple-element.25.hs_ref, f32[32,1024]{1,0:T(8,128)S(1)} %get-tuple-element.28.lc_ref, f32[32,1024]{1,0:T(8,128)S(1)} %get-tuple-element.27.ls_ref, ...), custom_call_target="tpu_custom_call" | custom-call | tf_op jit(solution)/shard_map/stage/pallas_call | solution.py:115
  59.8 5.1 %correlate.3 = bf16[4,4,9,16,256]{4,3,2,1,0:T(8,128)(2,1)S(1)} custom-call(s32[8,16]{1,0:T(8,128)S(1)} %bitcast.27, s32[1]{0:T(128)} %bitcast.7.core_ref, bf16[6,8,1024]{2,1,0:T(8,128)(2,1)S(1)} %dynamic-slice_bitcast_fusion.mine_ref, bf16[6,128,1024]{2,1,0:T(8,128)(2,1)S(1)} %get-tuple-element.20.stations, bf16[2048,1024]{1,0:T(8,128)(2,1)S(1)} %get-tuple-element.21.table), custom_call_target="tpu_custom_call" | custom-call | tf_op jit(solution)/shard_map/correlate/pallas_call | solution.py:128
  64.9 1.9 %collective-permute-start.2 = (bf16[4,4,9,16,256]{4,3,2,1,0:T(8,128)(2,1)S(1)}, bf16[4,4,9,16,256]{4,3,2,1,0:T(8,128)(2,1)S(1)}, u32[]{:S(2)}, u32[]{:S(2)}) collective-permute-start(bf16[4,4,9,16,256]{4,3,2,1,0:T(8,128)(2,1)S(1)} %correlate.3), channel_id=1, source_target_pairs={{0,4},{4,0},{8,12},{12,8},{16,20},{20,16},{24,28},{28,24},{1,5},{5... | collective-permute-start | bytes 3538952 | tf_op jit(solution)/shard_map/ppermute | solution.py:144
  66.8 5.1 %correlate.2 = f32[4,4,9,16,256]{4,3,2,1,0:T(8,128)S(1)} custom-call(s32[8,16]{1,0:T(8,128)S(1)} %bitcast.28, s32[1]{0:T(128)} %bitcast.7.core_ref, bf16[6,8,1024]{2,1,0:T(8,128)(2,1)S(1)} %dynamic-slice_bitcast_fusion.mine_ref, bf16[6,128,1024]{2,1,0:T(8,128)(2,1)S(1)} %get-tuple-element.20.stations, bf16[2048,1024]{1,0:T(8,128)(2,1)S(1)} %get-tuple-element.21.table), custom_call_target="tpu_custom_call" | custom-call | tf_op jit(solution)/shard_map/correlate/pallas_call | solution.py:128
  71.9 0.0 collective-permute-done.2
  71.9 0.4 add_convert_fusion
  72.3 23.7 %all_to_all.14 = bf16[16,9,16,256]{3,2,1,0:T(8,128)(2,1)S(1)} all-to-all(bf16[16,9,16,256]{3,2,1,0:T(8,128)(2,1)S(1)} %bitcast.29), channel_id=1, replica_groups={{0,1,2,3,8,9,10,11,16,17,18,19,24,25,26,27},{4,5,6,7,12,13,14,15,20,21,..., dimensions={0} | all-to-all | bytes 2359296 | tf_op jit(solution)/shard_map/all_to_all | solution.py:147
  96.1 0.2 convert_reduce_fusion
  96.3 13.6 %all_gather.11 = f32[9,16,1024]{2,1,0:T(8,128)S(1)} all-gather(f32[9,16,256]{2,1,0:T(8,128)S(1)} %broadcast_multiply_fusion), channel_id=1, replica_groups=mesh['sta'=16,'grp'=8,'hr'=4] {'hr'}, dimensions={2}, use_global_device_ids=true | all-gather | bytes 737280 | tf_op jit(solution)/shard_map/all_gather | solution.py:149
  109.9 0.8 copy.6
  (10 shorter events, 0.1 us)
Async XLA Ops:
  0.0 1.1 %copy-start = (bf16[1,8,6,8192]{3,1,2,0:T(8,128)(2,1)S(1)}, bf16[1,8,6,8192]{3,1,2,0:T(8,128)(2,1)}, u32[]{:S(2)}) copy-start(bf16[1,8,6,8192]{3,1,2,0:T(8,128)(2,1)} %param.4) | copy-start | bytes 2359300
  0.0 47.6 %copy-start.2 = (s32[16]{0:T(128)S(1)}, s32[16]{0:T(128)}, u32[]{:S(2)}) copy-start(s32[16]{0:T(128)} %param.7) | copy-start | bytes 196
  0.0 47.6 %copy-start.3 = (s32[16,1]{0,1:T(1,128)S(1)}, s32[16,1]{0,1:T(1,128)}, u32[]{:S(2)}) copy-start(s32[16,1]{0,1:T(1,128)} %param.6) | copy-start | bytes 196
  0.0 47.6 %copy-start.1 = (s32[16]{0:T(128)S(1)}, s32[16]{0:T(128)}, u32[]{:S(2)}) copy-start(s32[16]{0:T(128)} %param.5) | copy-start | bytes 196
  40.5 17.6 %collective-permute-start = (bf16[4,6,8,1024]{3,2,1,0:T(8,128)(2,1)}, bf16[4,6,8,1024]{3,2,1,0:T(8,128)(2,1)S(1)}, u32[]{:S(2)}, u32[]{:S(2)}) collective-permute-start(bf16[4,6,8,1024]{3,2,1,0:T(8,128)(2,1)} %bitcast.5), channel_id=1, source_target_pairs={{0,32},{4,484},{8,40},{12,492},{16,48},{20,500},{24,56},{28,508},{... | collective-permute-start | bytes 1179656 | tf_op jit(solution)/shard_map/ppermute | solution.py:98
  44.0 14.1 %collective-permute-start.1 = (bf16[4,6,8,1024]{3,2,1,0:T(8,128)(2,1)S(1)}, bf16[4,6,8,1024]{3,2,1,0:T(8,128)(2,1)S(1)}, u32[]{:S(2)}, u32[]{:S(2)}) collective-permute-start(bf16[4,6,8,1024]{3,2,1,0:T(8,128)(2,1)S(1)} %bitcast.31), channel_id=1, source_target_pairs={{0,480},{4,36},{8,488},{12,44},{16,496},{20,52},{24,504},{28,60},{... | collective-permute-start | bytes 1179656 | tf_op jit(solution)/shard_map/ppermute | solution.py:98
  49.4 8.7 %all-to-all-start = ((s32[8,1,16]{2,1,0:T(1,128)}), s32[8,1,16]{2,1,0:T(1,128)S(1)}, u32[]{:S(2)}, u32[]{:S(2)}) async-start(s32[8,1,16]{2,1,0:T(1,128)} %broadcast_in_dim.11), calls=%async_computation | async-start | bytes 8192 | tf_op jit(solution)/shard_map/all_to_all | solution.py:111
  64.9 7.0 %collective-permute-start.2 = (bf16[4,4,9,16,256]{4,3,2,1,0:T(8,128)(2,1)S(1)}, bf16[4,4,9,16,256]{4,3,2,1,0:T(8,128)(2,1)S(1)}, u32[]{:S(2)}, u32[]{:S(2)}) collective-permute-start(bf16[4,4,9,16,256]{4,3,2,1,0:T(8,128)(2,1)S(1)} %correlate.3), channel_id=1, source_target_pairs={{0,4},{4,0},{8,12},{12,8},{16,20},{20,16},{24,28},{28,24},{1,5},{5... | collective-permute-start | bytes 3538952 | tf_op jit(solution)/shard_map/ppermute | solution.py:144

commit v5 on v4

v5 whole, which is shorter than its diff:
```python
import functools
import math

import jax
import jax.numpy as jnp
from jax import lax
from jax.experimental import pallas as pl
from jax.experimental.pallas import tpu as pltpu
from jax.sharding import PartitionSpec as P

LAGS = 1024
NZ, NG, NY, NC, NX = 16, 8, 4, 2, 4
SD, PD, NB = 8, 16, 8192
W = NB // NG
BITS = 10
FINE = 32
HALF = NY * PD
CH = 128
TW = LAGS // NX
TWO_PI = 2.0 * math.pi
VMEM_LIMIT = 24 * 1024 * 1024


def codes(plane_ref, source_ref, owner_ref, row_ref, out_ref):
    plane, owner = plane_ref[0], owner_ref[...]
    slot = jnp.where(owner % 2 == plane % 2, 0, NZ // 2) + owner // 2
    code = (slot * SD + row_ref[...]) * (NZ * SD) + plane // 2 * SD + source_ref[...]
    out_ref[...] = jnp.broadcast_to(code, (NG, PD))


def stage(grp_ref, code_ref, near_ref, first_ref, second_ref, table, stations, pick, row, hi_c, hi_s):
    core, g = grp_ref[0] % NC, grp_ref[0]
    bit = lax.broadcasted_iota(jnp.int32, (16, LAGS), 0)
    lag = lax.broadcasted_iota(jnp.int32, (16, LAGS), 1) - LAGS // 2
    bins = jnp.where(bit < BITS, jnp.left_shift(1, bit), g * W)
    ang = ((bins * lag) & (2 * NB - 1)).astype(jnp.float32) * (TWO_PI / (2 * NB))
    cos, sin = jnp.cos(ang), jnp.sin(ang)

    def turned(c, s, bits):
        at = lax.broadcasted_iota(jnp.int32, (FINE, LAGS), 0)
        for k, b in enumerate(bits):
            on = (jnp.right_shift(at, k) & 1) == 1
            kc, ks = jnp.where(on, cos[b : b + 1], 1.0), jnp.where(on, sin[b : b + 1], 0.0)
            c, s = c * kc - s * ks, s * kc + c * ks
        return c, s

    half_bits = BITS // 2
    lc, ls = turned(jnp.ones((FINE, LAGS), jnp.float32), jnp.zeros((FINE, LAGS), jnp.float32), range(half_bits))
    base = jnp.broadcast_to(cos[BITS : BITS + 1], (FINE, LAGS)), jnp.broadcast_to(sin[BITS : BITS + 1], (FINE, LAGS))
    hi_c[...], hi_s[...] = turned(*base, range(half_bits, BITS))

    def fill(i, carry):
        hc, hs = hi_c[pl.ds(i, 1), :], hi_s[pl.ds(i, 1), :]
        at = pl.multiple_of(i * FINE, FINE)
        table[pl.ds(at, FINE), :] = (hc * lc - hs * ls).astype(jnp.bfloat16)
        table[pl.ds(W + at, FINE), :] = (-(hs * lc + hc * ls)).astype(jnp.bfloat16)
        return carry

    lax.fori_loop(0, W // FINE, fill, 0)

    even = core == 0
    for k in range(NY):
        c0, c1 = code_ref[NC * k : NC * k + 1], code_ref[NC * k + 1 : NC * k + 2]
        for half, code in enumerate((jnp.where(even, c1, c0), jnp.where(even, c0, c1))):
            at = half * 2 * HALF + k * PD
            row[0:1, at : at + PD] = code // (NZ * SD)
            row[0:1, at + HALF : at + HALF + PD] = code % (NZ * SD)
    station = lax.broadcasted_iota(jnp.int32, (NZ * SD, 2 * HALF), 0)
    for half in range(NC):
        hot = (station == row[0:1, half * 2 * HALF : (half + 1) * 2 * HALF]).astype(jnp.float32)
        pick[half] = hot.T.astype(jnp.bfloat16)
    for comp in range(6):
        at = 0
        for ref in (near_ref, first_ref, second_ref):
            x = ref[:, comp].astype(jnp.float32).reshape(-1, W).astype(jnp.bfloat16)
            stations[comp, at : at + x.shape[0]] = x
            at += x.shape[0]


def correlate(half, pick, stations, table, out_ref, cross):
    for k in range(W // CH):
        at = k * CH
        r, s = [], []
        for comp in range(6):
            x = jnp.dot(pick[half], stations[comp, :, at : at + CH], preferred_element_type=jnp.float32)
            r.append(x[:HALF])
            s.append(x[HALF:])
        for a in range(3):
            for b in range(3):
                r0 = (3 * a + b) * HALF
                re = s[a] * r[b] + s[3 + a] * r[3 + b]
                im = s[a] * r[3 + b] - s[3 + a] * r[b]
                cross[r0 : r0 + HALF, at : at + CH] = re.astype(jnp.bfloat16)
                cross[r0 : r0 + HALF, W + at : W + at + CH] = im.astype(jnp.bfloat16)

    for n in range(NX):
        out = jnp.dot(cross[...], table[:, n * TW : (n + 1) * TW], preferred_element_type=jnp.float32)
        for c in range(9):
            for k in range(NY):
                r0 = c * HALF + k * PD
                out_ref[k, n, c] = out[r0 : r0 + PD].astype(out_ref.dtype)


def vmem(n):
    return [pl.BlockSpec(memory_space=pltpu.VMEM)] * n


def body(spectra, pair_source, pair_owner, pair_row):
    s, g = lax.axis_index("sta"), lax.axis_index("grp")
    mine = lax.dynamic_slice_in_dim(spectra[0], g * W, W, 2).transpose(1, 0, 2)
    planes = [list(range(p, NZ, 2)) for p in range(2)]
    near = lax.all_gather(mine, "sta", axis=0, axis_index_groups=planes)

    def neighbour(x, step):
        turn = [step if i % NC == 0 else -step for i in range(NG)]
        perm = [(z * NG + i, (z + turn[i]) % NZ * NG + i) for z in range(NZ) for i in range(NG)]
        return lax.ppermute(x, ("sta", "grp"), perm)

    pos = lax.axis_index("hr") * TW + jnp.arange(TW, dtype=jnp.int32)
    taper = 0.75 - 0.25 * jnp.cos(TWO_PI * (pos.astype(jnp.float32) + 0.5) / LAGS)
    scale = taper / (NX * math.sqrt(NB))
    low, high = near[: NZ // 4], near[NZ // 4 :]
    low, high, pair_row = lax.optimization_barrier((low, high, pair_row))
    first, second = neighbour(low, 1), neighbour(high, -1)

    smem = pl.BlockSpec(memory_space=pltpu.SMEM)
    code = pl.pallas_call(
        codes,
        out_shape=jax.ShapeDtypeStruct((NG, PD), jnp.int32),
        in_specs=[smem] + vmem(3),
        out_specs=vmem(1)[0],
        cost_estimate=pl.CostEstimate(flops=10**10, bytes_accessed=10**6, transcendentals=0),
        name="codes",
    )(s[None], pair_source[None], pair_owner.T, pair_row[None])
    code = lax.all_to_all(code, "grp", 0, 0, tiled=True)
    code, first, second, scale = lax.optimization_barrier((code, first, second, scale))

    params = pltpu.CompilerParams(vmem_limit_bytes=VMEM_LIMIT)
    table, stations, pick = pl.pallas_call(
        stage,
        out_shape=(
            jax.ShapeDtypeStruct((2 * W, LAGS), jnp.bfloat16),
            jax.ShapeDtypeStruct((6, NZ * SD, W), jnp.bfloat16),
            jax.ShapeDtypeStruct((NC, 2 * HALF, NZ * SD), jnp.bfloat16),
        ),
        in_specs=[smem] + vmem(4),
        out_specs=tuple(vmem(3)),
        scratch_shapes=[
            pltpu.VMEM((8, NC * 2 * HALF), jnp.int32),
            pltpu.VMEM((FINE, LAGS), jnp.float32),
            pltpu.VMEM((FINE, LAGS), jnp.float32),
        ],
        compiler_params=params,
        name="stage",
    )(g[None], code, near, first, second)

    def lags(half, dtype):
        return pl.pallas_call(
            functools.partial(correlate, half),
            out_shape=jax.ShapeDtypeStruct((NY, NX, 9, PD, TW), dtype),
            in_specs=vmem(3),
            out_specs=vmem(1)[0],
            scratch_shapes=[pltpu.VMEM((9 * HALF, 2 * W), jnp.bfloat16)],
            compiler_params=params,
            name="correlate",
        )(pick, stations, table)

    send = lags(0, jnp.bfloat16)
    keep = lags(1, jnp.float32)
    part = keep + lax.ppermute(send, "grp", [(i, i ^ 1) for i in range(NG)]).astype(jnp.float32)
    part = part.astype(jnp.bfloat16).reshape(NY * NX, 9, PD, TW)
    chips = [[(NC * y + c) * NX + x for y in range(NY) for x in range(NX)] for c in range(NC)]
    part = lax.all_to_all(part, ("grp", "hr"), 0, 0, axis_index_groups=chips, tiled=True)
    total = jnp.sum(part.astype(jnp.float32), axis=0)
    return lax.all_gather(total * scale, "hr", axis=2, tiled=True).transpose(1, 0, 2)


def solution(mesh):
    placed = (
        P("hr", "sta", None, None),
        P(("sta", "grp")),
        P(("sta", "grp"), None),
        P(("sta", "grp")),
    )
    return jax.shard_map(
        body, mesh=mesh, in_specs=placed, out_specs=P(("sta", "grp"), None, None), check_vma=False
    )
```

time: 111 us -> 107 us (0.964)
  local copies, waits for them, and re-layouts: 3.33 us -> 2.01 us
  Pallas kernels: 11.9 us -> 10.7 us
    pallas_call x2 -> x3, Pallas kernels: 10.2 us -> 8.41 us  [the longest x2 7.12 us: lags(): pl.pallas_call(functools.partial(correlate, half), out_shape=jax.ShapeDty...]
  transfers between devices with their start and end apart: 4 -> 4, of which waited for: 1 -> 1; matrix products, arithmetic and copies ran while one was open for 2% -> 0% of each run, Pallas kernels for 5% -> 5%
where the time goes in v5:
time: 107 us
  blocking collectives  76 us (71%)
  starting transfers between devices  13.9 us (13%)
  Pallas kernels  10.7 us (10%)
  waiting for transfers between devices  3.69 us (3%)
  local copies, waits for them, and re-layouts  2.01 us (2%)
    all_gather x1, blocking collectives, body(): near = lax.all_gather(mine, 'sta', axis=0, axis_index_groups=planes)  38.6 us
    all_to_all x1, blocking collectives, body(): lax.all_to_all(part, ('grp', 'hr'), 0, 0, axis_index_groups=chips, tiled=...  23.8 us
    all_gather x1, blocking collectives, body(): lax.all_gather(total * scale, 'hr', axis=2, tiled=True).transpose(1, 0, 2)  13.6 us
    pallas_call x2, Pallas kernels, lags(): pl.pallas_call(functools.partial(correlate, half), out_shape=jax.ShapeDty...  7.12 us
    ppermute x2, starting transfers between devices, neighbour(): return lax.ppermute(x, ('sta', 'grp'), perm)  7.05 us
    all_to_all x1, starting transfers between devices, body(): code = lax.all_to_all(code, 'grp', 0, 0, tiled=True)  4.92 us
    all_to_all x1, waiting for transfers between devices, body(): code = lax.all_to_all(code, 'grp', 0, 0, tiled=True)  3.68 us
    pallas_call x1, Pallas kernels, body(): pl.pallas_call(stage, out_shape=(jax.ShapeDtypeStruct((2 * W, LAGS), jnp....  2.33 us
  transfers between devices with their start and end apart: 4, of which 1 were waited for; matrix products, arithmetic and copies ran while one was open for 0% of the time, Pallas kernels for 5%

profile of v5, /device:TPU:8, one launch (start us, length us, event | category | flops | bytes accessed | tf_op | source)
XLA Modules:
  0.0 107.0 jit_solution(3069556386343679723)
XLA Ops:
  0.0 0.0 copy-start
  0.0 1.1 %copy-done = bf16[1,8,6,8192]{3,1,2,0:T(8,128)(2,1)S(1)} copy-done((bf16[1,8,6,8192]{3,1,2,0:T(8,128)(2,1)S(1)}, bf16[1,8,6,8192]{3,1,2,0:T(8,128)(2,1)}, u32[]{:S(2)}) %copy-start) | copy-done | bytes 786456
  1.1 38.6 %all-gather = bf16[48,8,1024]{2,1,0:T(8,128)(2,1)S(1)} all-gather(bf16[6,8,1024]{2,1,0:T(8,128)(2,1)S(1)} %dynamic-slice_bitcast_fusion), channel_id=2, replica_groups={{0,64,128,192,256,320,384,448},{32,96,160,224,288,352,416,480},{1,65,12..., dimensions={0}, use_global_device_ids=true | all-gather | bytes 884736 | tf_op jit(solution)/shard_map/all_gather | solution.py:112
  39.7 0.1 fusion
  39.8 3.7 %collective-permute-start = (bf16[4,6,8,1024]{3,2,1,0:T(8,128)(2,1)S(1)}, bf16[4,6,8,1024]{3,2,1,0:T(8,128)(2,1)S(1)}, u32[]{:S(2)}, u32[]{:S(2)}) collective-permute-start(bf16[4,6,8,1024]{3,2,1,0:T(8,128)(2,1)S(1)} %bitcast.23), channel_id=1, source_target_pairs={{0,32},{4,484},{8,40},{12,492},{16,48},{20,500},{24,56},{28,508},{... | collective-permute-start | bytes 1179656 | tf_op jit(solution)/shard_map/ppermute | solution.py:117
  43.5 3.4 %collective-permute-start.1 = (bf16[4,6,8,1024]{3,2,1,0:T(8,128)(2,1)S(1)}, bf16[4,6,8,1024]{3,2,1,0:T(8,128)(2,1)S(1)}, u32[]{:S(2)}, u32[]{:S(2)}) collective-permute-start(bf16[4,6,8,1024]{3,2,1,0:T(8,128)(2,1)S(1)} %bitcast.22), channel_id=1, source_target_pairs={{0,480},{4,36},{8,488},{12,44},{16,496},{20,52},{24,504},{28,60},{... | collective-permute-start | bytes 1179656 | tf_op jit(solution)/shard_map/ppermute | solution.py:117
  46.8 1.3 %codes.1 = s32[8,16]{1,0:T(8,128)} custom-call(s32[1]{0:T(128)} %bitcast.1.plane_ref, s32[1,16]{1,0:T(1,128)} %bitcast.25, s32[1,16]{1,0:T(1,128)} %bitcast.26, s32[1,16]{1,0:T(1,128)} %bitcast.27), custom_call_target="tpu_custom_call" | custom-call | flops 10000000000 | bytes 1000000 | tf_op jit(solution)/shard_map/codes/pallas_call | solution.py:127
  48.1 4.9 %all-to-all-start = ((s32[8,1,16]{2,1,0:T(1,128)}), s32[8,1,16]{2,1,0:T(1,128)S(1)}, u32[]{:S(2)}, u32[]{:S(2)}) async-start(s32[8,1,16]{2,1,0:T(1,128)} %bitcast.24), calls=%async_computation | async-start | bytes 8192 | tf_op jit(solution)/shard_map/all_to_all | solution.py:135
  53.1 3.7 %all-to-all-done = s32[8,1,16]{2,1,0:T(1,128)S(1)} async-done(((s32[8,1,16]{2,1,0:T(1,128)}), s32[8,1,16]{2,1,0:T(1,128)S(1)}, u32[]{:S(2)}, u32[]{:S(2)}) %all-to-all-start) | async-done | bytes 544 | tf_op jit(solution)/shard_map/all_to_all | solution.py:135
  56.8 0.0 collective-permute-done.first_ref
  56.8 0.0 collective-permute-done.1.second_ref
  56.8 2.3 %stage.1 = (bf16[2048,1024]{1,0:T(8,128)(2,1)S(1)}, bf16[6,128,1024]{2,1,0:T(8,128)(2,1)S(1)}, bf16[2,128,128]{2,1,0:T(8,128)(2,1)S(1)}) custom-call(s32[1]{0:T(128)} %bitcast.grp_ref, s32[8,16]{1,0:T(8,128)S(1)} %bitcast.19, bf16[8,6,8,1024]{3,2,1,0:T(8,128)(2,1)S(1)} %bitcast.18, bf16[4,6,8,1024]{3,2,1,0:T(8,128)(2,1)S(1)} %collective-permute-done.first_ref, ...), custom_call_target="tpu_custom_call" | custom-call | tf_op jit(solution)/shard_map/stage/pallas_call | solution.py:139
  59.1 3.6 %correlate.3 = bf16[4,4,9,16,256]{4,3,2,1,0:T(8,128)(2,1)S(1)} custom-call(bf16[2,128,128]{2,1,0:T(8,128)(2,1)S(1)} %get-tuple-element.21.pick, bf16[6,128,1024]{2,1,0:T(8,128)(2,1)S(1)} %get-tuple-element.22.stations, bf16[2048,1024]{1,0:T(8,128)(2,1)S(1)} %get-tuple-element.23.table), custom_call_target="tpu_custom_call" | custom-call | tf_op jit(solution)/shard_map/correlate/pallas_call | solution.py:158
  62.7 1.9 %collective-permute-start.2 = (bf16[4,4,9,16,256]{4,3,2,1,0:T(8,128)(2,1)S(1)}, bf16[4,4,9,16,256]{4,3,2,1,0:T(8,128)(2,1)S(1)}, u32[]{:S(2)}, u32[]{:S(2)}) collective-permute-start(bf16[4,4,9,16,256]{4,3,2,1,0:T(8,128)(2,1)S(1)} %correlate.3), channel_id=1, source_target_pairs={{0,4},{4,0},{8,12},{12,8},{16,20},{20,16},{24,28},{28,24},{1,5},{5... | collective-permute-start | bytes 3538952 | tf_op jit(solution)/shard_map/ppermute | solution.py:170
  64.6 3.6 %correlate.2 = f32[4,4,9,16,256]{4,3,2,1,0:T(8,128)S(1)} custom-call(bf16[2,128,128]{2,1,0:T(8,128)(2,1)S(1)} %get-tuple-element.21.pick, bf16[6,128,1024]{2,1,0:T(8,128)(2,1)S(1)} %get-tuple-element.22.stations, bf16[2048,1024]{1,0:T(8,128)(2,1)S(1)} %get-tuple-element.23.table), custom_call_target="tpu_custom_call" | custom-call | tf_op jit(solution)/shard_map/correlate/pallas_call | solution.py:158
  68.2 0.0 collective-permute-done.2
  68.2 0.4 add_convert_fusion
  68.6 23.8 %all_to_all.17 = bf16[16,9,16,256]{3,2,1,0:T(8,128)(2,1)S(1)} all-to-all(bf16[16,9,16,256]{3,2,1,0:T(8,128)(2,1)S(1)} %bitcast.20), channel_id=1, replica_groups={{0,1,2,3,8,9,10,11,16,17,18,19,24,25,26,27},{4,5,6,7,12,13,14,15,20,21,..., dimensions={0} | all-to-all | bytes 2359296 | tf_op jit(solution)/shard_map/all_to_all | solution.py:173
  92.4 0.2 convert_reduce_fusion
  92.6 13.6 %all_gather.11 = f32[9,16,1024]{2,1,0:T(8,128)S(1)} all-gather(f32[9,16,256]{2,1,0:T(8,128)S(1)} %broadcast_multiply_fusion), channel_id=1, replica_groups=mesh['sta'=16,'grp'=8,'hr'=4] {'hr'}, dimensions={2}, use_global_device_ids=true | all-gather | bytes 737280 | tf_op jit(solution)/shard_map/all_gather | solution.py:175
  106.2 0.8 copy.7
  (3 shorter events, 0.1 us)
Async XLA Ops:
  0.0 1.1 %copy-start = (bf16[1,8,6,8192]{3,1,2,0:T(8,128)(2,1)S(1)}, bf16[1,8,6,8192]{3,1,2,0:T(8,128)(2,1)}, u32[]{:S(2)}) copy-start(bf16[1,8,6,8192]{3,1,2,0:T(8,128)(2,1)} %param.4) | copy-start | bytes 2359300
  39.8 17.0 %collective-permute-start = (bf16[4,6,8,1024]{3,2,1,0:T(8,128)(2,1)S(1)}, bf16[4,6,8,1024]{3,2,1,0:T(8,128)(2,1)S(1)}, u32[]{:S(2)}, u32[]{:S(2)}) collective-permute-start(bf16[4,6,8,1024]{3,2,1,0:T(8,128)(2,1)S(1)} %bitcast.23), channel_id=1, source_target_pairs={{0,32},{4,484},{8,40},{12,492},{16,48},{20,500},{24,56},{28,508},{... | collective-permute-start | bytes 1179656 | tf_op jit(solution)/shard_map/ppermute | solution.py:117
  43.5 13.3 %collective-permute-start.1 = (bf16[4,6,8,1024]{3,2,1,0:T(8,128)(2,1)S(1)}, bf16[4,6,8,1024]{3,2,1,0:T(8,128)(2,1)S(1)}, u32[]{:S(2)}, u32[]{:S(2)}) collective-permute-start(bf16[4,6,8,1024]{3,2,1,0:T(8,128)(2,1)S(1)} %bitcast.22), channel_id=1, source_target_pairs={{0,480},{4,36},{8,488},{12,44},{16,496},{20,52},{24,504},{28,60},{... | collective-permute-start | bytes 1179656 | tf_op jit(solution)/shard_map/ppermute | solution.py:117
  48.1 8.6 %all-to-all-start = ((s32[8,1,16]{2,1,0:T(1,128)}), s32[8,1,16]{2,1,0:T(1,128)S(1)}, u32[]{:S(2)}, u32[]{:S(2)}) async-start(s32[8,1,16]{2,1,0:T(1,128)} %bitcast.24), calls=%async_computation | async-start | bytes 8192 | tf_op jit(solution)/shard_map/all_to_all | solution.py:135
  62.7 5.5 %collective-permute-start.2 = (bf16[4,4,9,16,256]{4,3,2,1,0:T(8,128)(2,1)S(1)}, bf16[4,4,9,16,256]{4,3,2,1,0:T(8,128)(2,1)S(1)}, u32[]{:S(2)}, u32[]{:S(2)}) collective-permute-start(bf16[4,4,9,16,256]{4,3,2,1,0:T(8,128)(2,1)S(1)} %correlate.3), channel_id=1, source_target_pairs={{0,4},{4,0},{8,12},{12,8},{16,20},{20,16},{24,28},{28,24},{1,5},{5... | collective-permute-start | bytes 3538952 | tf_op jit(solution)/shard_map/ppermute | solution.py:170

commit v6 on v5

--- a/solution.py
+++ b/solution.py
@@ -12,6 +12,7 @@
 NZ, NG, NY, NC, NX = 16, 8, 4, 2, 4
 SD, PD, NB = 8, 16, 8192
 W = NB // NG
+NR = 4
 BITS = 10
 FINE = 32
 HALF = NY * PD
@@ -23,12 +24,14 @@
 
 def codes(plane_ref, source_ref, owner_ref, row_ref, out_ref):
     plane, owner = plane_ref[0], owner_ref[...]
-    slot = jnp.where(owner % 2 == plane % 2, 0, NZ // 2) + owner // 2
-    code = (slot * SD + row_ref[...]) * (NZ * SD) + plane // 2 * SD + source_ref[...]
+    away = (owner - plane) & (NR - 1)
+    first = jnp.where(away == 0, 0, jnp.where(away == 3, 1, jnp.where(away == 1, 2, 3)))
+    slot = first * (NZ // NR) + owner // NR
+    code = (slot * SD + row_ref[...]) * (NZ * SD) + plane // NR * SD + source_ref[...]
     out_ref[...] = jnp.broadcast_to(code, (NG, PD))
 
 
-def stage(grp_ref, code_ref, near_ref, first_ref, second_ref, table, stations, pick, row, hi_c, hi_s):
+def stage(grp_ref, code_ref, near_ref, first_ref, second_ref, third_ref, fourth_ref, table, stations, pick, row, hi_c, hi_s):
     core, g = grp_ref[0] % NC, grp_ref[0]
     bit = lax.broadcasted_iota(jnp.int32, (16, LAGS), 0)
     lag = lax.broadcasted_iota(jnp.int32, (16, LAGS), 1) - LAGS // 2
@@ -69,12 +72,12 @@
     for half in range(NC):
         hot = (station == row[0:1, half * 2 * HALF : (half + 1) * 2 * HALF]).astype(jnp.float32)
         pick[half] = hot.T.astype(jnp.bfloat16)
-    for comp in range(6):
-        at = 0
-        for ref in (near_ref, first_ref, second_ref):
+    part = NZ * SD // NR
+    rows = (0, pl.multiple_of(part + core * part, part), pl.multiple_of(2 * part - core * part, part), 3 * part, 7 * part // 2)
+    for at, ref in zip(rows, (near_ref, first_ref, second_ref, third_ref, fourth_ref)):
+        for comp in range(6):
             x = ref[:, comp].astype(jnp.float32).reshape(-1, W).astype(jnp.bfloat16)
-            stations[comp, at : at + x.shape[0]] = x
-            at += x.shape[0]
+            stations[comp, pl.ds(at, x.shape[0]), :] = x
 
 
 def correlate(half, pick, stations, table, out_ref, cross):
@@ -108,7 +111,7 @@
 def body(spectra, pair_source, pair_owner, pair_row):
     s, g = lax.axis_index("sta"), lax.axis_index("grp")
     mine = lax.dynamic_slice_in_dim(spectra[0], g * W, W, 2).transpose(1, 0, 2)
-    planes = [list(range(p, NZ, 2)) for p in range(2)]
+    planes = [list(range(p, NZ, NR)) for p in range(NR)]
     near = lax.all_gather(mine, "sta", axis=0, axis_index_groups=planes)
 
     def neighbour(x, step):
@@ -119,9 +122,9 @@
     pos = lax.axis_index("hr") * TW + jnp.arange(TW, dtype=jnp.int32)
     taper = 0.75 - 0.25 * jnp.cos(TWO_PI * (pos.astype(jnp.float32) + 0.5) / LAGS)
     scale = taper / (NX * math.sqrt(NB))
-    low, high = near[: NZ // 4], near[NZ // 4 :]
-    low, high, pair_row = lax.optimization_barrier((low, high, pair_row))
-    first, second = neighbour(low, 1), neighbour(high, -1)
+    half = NZ // NR // 2
+    low, high, pair_row = lax.optimization_barrier((near[:half], near[half:], pair_row))
+    moved = (neighbour(near, 1), neighbour(near, -1), neighbour(low, 2), neighbour(high, -2))
 
     smem = pl.BlockSpec(memory_space=pltpu.SMEM)
     code = pl.pallas_call(
@@ -133,7 +136,7 @@
         name="codes",
     )(s[None], pair_source[None], pair_owner.T, pair_row[None])
     code = lax.all_to_all(code, "grp", 0, 0, tiled=True)
-    code, first, second, scale = lax.optimization_barrier((code, first, second, scale))
+    code, moved, scale = lax.optimization_barrier((code, moved, scale))
 
     params = pltpu.CompilerParams(vmem_limit_bytes=VMEM_LIMIT)
     table, stations, pick = pl.pallas_call(
@@ -143,7 +146,7 @@
             jax.ShapeDtypeStruct((6, NZ * SD, W), jnp.bfloat16),
             jax.ShapeDtypeStruct((NC, 2 * HALF, NZ * SD), jnp.bfloat16),
         ),
-        in_specs=[smem] + vmem(4),
+        in_specs=[smem] + vmem(6),
         out_specs=tuple(vmem(3)),
         scratch_shapes=[
             pltpu.VMEM((8, NC * 2 * HALF), jnp.int32),
@@ -152,7 +155,7 @@
         ],
         compiler_params=params,
         name="stage",
-    )(g[None], code, near, first, second)
+    )(g[None], code, near, *moved)
 
     def lags(half, dtype):
         return pl.pallas_call(
@@ -172,7 +175,8 @@
     chips = [[(NC * y + c) * NX + x for y in range(NY) for x in range(NX)] for c in range(NC)]
     part = lax.all_to_all(part, ("grp", "hr"), 0, 0, axis_index_groups=chips, tiled=True)
     total = jnp.sum(part.astype(jnp.float32), axis=0)
-    return lax.all_gather(total * scale, "hr", axis=2, tiled=True).transpose(1, 0, 2)
+    total = lax.all_gather((total * scale).astype(jnp.bfloat16), "hr", axis=2, tiled=True)
+    return total.astype(jnp.float32).transpose(1, 0, 2)
 
 
 def solution(mesh):

time: 107 us -> 106 us (level)
  blocking collectives: 76 us -> 67 us
  starting transfers between devices: 13.9 us -> 21.8 us
    all_gather x1, blocking collectives: 38.6 us -> 30.5 us  [body(): near = lax.all_gather(mine, 'sta', axis=0, axis_index_groups=planes)]
    ppermute x2 -> x4, starting transfers between devices: 7.05 us -> 15 us  [neighbour(): return lax.ppermute(x, ('sta', 'grp'), perm)]
  transfers between devices with their start and end apart: 4 -> 6, of which waited for: 1 -> 1; matrix products, arithmetic and copies ran while one was open for 0% -> 0% of each run, Pallas kernels for 5% -> 5%
where the time goes in v6:
time: 106 us
  blocking collectives  67 us (63%)
  starting transfers between devices  21.8 us (21%)
  Pallas kernels  10.7 us (10%)
  waiting for transfers between devices  3.7 us (3%)
  other arithmetic  1.5 us (1%)
  local copies, waits for them, and re-layouts  1.17 us (1%)
    all_gather x1, blocking collectives, body(): near = lax.all_gather(mine, 'sta', axis=0, axis_index_groups=planes)  30.5 us
    all_to_all x1, blocking collectives, body(): lax.all_to_all(part, ('grp', 'hr'), 0, 0, axis_index_groups=chips, tiled=...  23.8 us
    ppermute x4, starting transfers between devices, neighbour(): return lax.ppermute(x, ('sta', 'grp'), perm)  15 us
    all_gather x1, blocking collectives, body(): lax.all_gather((total * scale).astype(jnp.bfloat16), 'hr', axis=2, tiled=...  12.7 us
    pallas_call x2, Pallas kernels, lags(): pl.pallas_call(functools.partial(correlate, half), out_shape=jax.ShapeDty...  7.1 us
    all_to_all x1, starting transfers between devices, body(): code = lax.all_to_all(code, 'grp', 0, 0, tiled=True)  4.92 us
    all_to_all x1, waiting for transfers between devices, body(): code = lax.all_to_all(code, 'grp', 0, 0, tiled=True)  3.68 us
    pallas_call x1, Pallas kernels, body(): pl.pallas_call(stage, out_shape=(jax.ShapeDtypeStruct((2 * W, LAGS), jnp....  2.35 us
  transfers between devices with their start and end apart: 6, of which 1 were waited for; matrix products, arithmetic and copies ran while one was open for 0% of the time, Pallas kernels for 5%

profile of v6, /device:TPU:8, one launch (start us, length us, event | category | flops | bytes accessed | tf_op | source)
XLA Modules:
  0.0 106.0 jit_solution(14709924860164608575)
XLA Ops:
  0.0 0.0 copy-start
  0.0 1.1 %copy-done = bf16[1,8,6,8192]{3,1,2,0:T(8,128)(2,1)S(1)} copy-done((bf16[1,8,6,8192]{3,1,2,0:T(8,128)(2,1)S(1)}, bf16[1,8,6,8192]{3,1,2,0:T(8,128)(2,1)}, u32[]{:S(2)}) %copy-start) | copy-done | bytes 786456
  1.1 30.5 %all-gather = bf16[24,8,1024]{2,1,0:T(8,128)(2,1)S(1)} all-gather(bf16[6,8,1024]{2,1,0:T(8,128)(2,1)S(1)} %dynamic-slice_bitcast_fusion), channel_id=2, replica_groups={{0,128,256,384},{32,160,288,416},{64,192,320,448},{96,224,352,480},{1,1..., dimensions={0}, use_global_device_ids=true | all-gather | bytes 491520 | tf_op jit(solution)/shard_map/all_gather | solution.py:115
  31.6 2.5 %collective-permute-start = (bf16[4,6,8,1024]{3,2,1,0:T(8,128)(2,1)S(1)}, bf16[4,6,8,1024]{3,2,1,0:T(8,128)(2,1)S(1)}, u32[]{:S(2)}, u32[]{:S(2)}) collective-permute-start(bf16[4,6,8,1024]{3,2,1,0:T(8,128)(2,1)S(1)} %bitcast.19), channel_id=1, source_target_pairs={{0,32},{4,484},{8,40},{12,492},{16,48},{20,500},{24,56},{28,508},{... | collective-permute-start | bytes 1179656 | tf_op jit(solution)/shard_map/ppermute | solution.py:120
  34.2 4.5 %collective-permute-start.1 = (bf16[4,6,8,1024]{3,2,1,0:T(8,128)(2,1)S(1)}, bf16[4,6,8,1024]{3,2,1,0:T(8,128)(2,1)S(1)}, u32[]{:S(2)}, u32[]{:S(2)}) collective-permute-start(bf16[4,6,8,1024]{3,2,1,0:T(8,128)(2,1)S(1)} %bitcast.20), channel_id=1, source_target_pairs={{0,480},{4,36},{8,488},{12,44},{16,496},{20,52},{24,504},{28,60},{... | collective-permute-start | bytes 1179656 | tf_op jit(solution)/shard_map/ppermute | solution.py:120
  38.7 1.9 %collective-permute-start.2 = (bf16[2,6,8,1024]{3,2,1,0:T(8,128)(2,1)S(1)}, bf16[2,6,8,1024]{3,2,1,0:T(8,128)(2,1)S(1)}, u32[]{:S(2)}, u32[]{:S(2)}) collective-permute-start(bf16[2,6,8,1024]{3,2,1,0:T(8,128)(2,1)S(1)} %bitcast.25), channel_id=1, source_target_pairs={{0,64},{4,452},{8,72},{12,460},{16,80},{20,468},{24,88},{28,476},{... | collective-permute-start | bytes 589832 | tf_op jit(solution)/shard_map/ppermute | solution.py:120
  40.7 6.0 %collective-permute-start.3 = (bf16[2,6,8,1024]{3,2,1,0:T(8,128)(2,1)S(1)}, bf16[2,6,8,1024]{3,2,1,0:T(8,128)(2,1)S(1)}, u32[]{:S(2)}, u32[]{:S(2)}) collective-permute-start(bf16[2,6,8,1024]{3,2,1,0:T(8,128)(2,1)S(1)} %bitcast.24), channel_id=1, source_target_pairs={{0,448},{4,68},{8,456},{12,76},{16,464},{20,84},{24,472},{28,92},{... | collective-permute-start | bytes 589832 | tf_op jit(solution)/shard_map/ppermute | solution.py:120
  46.7 1.3 %codes.1 = s32[8,16]{1,0:T(8,128)} custom-call(s32[1]{0:T(128)} %bitcast.1.plane_ref, s32[1,16]{1,0:T(1,128)} %bitcast.27, s32[1,16]{1,0:T(1,128)} %bitcast.28, s32[1,16]{1,0:T(1,128)} %bitcast.29), custom_call_target="tpu_custom_call" | custom-call | flops 10000000000 | bytes 1000000 | tf_op jit(solution)/shard_map/codes/pallas_call | solution.py:130
  48.0 4.9 %all-to-all-start = ((s32[8,1,16]{2,1,0:T(1,128)}), s32[8,1,16]{2,1,0:T(1,128)S(1)}, u32[]{:S(2)}, u32[]{:S(2)}) async-start(s32[8,1,16]{2,1,0:T(1,128)} %bitcast.26), calls=%async_computation | async-start | bytes 8192 | tf_op jit(solution)/shard_map/all_to_all | solution.py:138
  53.0 3.7 %all-to-all-done = s32[8,1,16]{2,1,0:T(1,128)S(1)} async-done(((s32[8,1,16]{2,1,0:T(1,128)}), s32[8,1,16]{2,1,0:T(1,128)S(1)}, u32[]{:S(2)}, u32[]{:S(2)}) %all-to-all-start) | async-done | bytes 544 | tf_op jit(solution)/shard_map/all_to_all | solution.py:138
  56.7 0.0 collective-permute-done.2.third_ref
  56.7 0.0 collective-permute-done.3.fourth_ref
  56.7 0.0 collective-permute-done.first_ref
  56.7 0.0 collective-permute-done.1.second_ref
  56.7 2.3 %stage.1 = (bf16[2048,1024]{1,0:T(8,128)(2,1)S(1)}, bf16[6,128,1024]{2,1,0:T(8,128)(2,1)S(1)}, bf16[2,128,128]{2,1,0:T(8,128)(2,1)S(1)}) custom-call(s32[1]{0:T(128)} %bitcast.grp_ref, s32[8,16]{1,0:T(8,128)S(1)} %bitcast.22, bf16[4,6,8,1024]{3,2,1,0:T(8,128)(2,1)S(1)} %bitcast.21, bf16[4,6,8,1024]{3,2,1,0:T(8,128)(2,1)S(1)} %collective-permute-done.first_ref, ...), custom_call_target="tpu_custom_call" | custom-call | tf_op jit(solution)/shard_map/stage/pallas_call | solution.py:142
  59.0 3.5 %correlate.3 = bf16[4,4,9,16,256]{4,3,2,1,0:T(8,128)(2,1)S(1)} custom-call(bf16[2,128,128]{2,1,0:T(8,128)(2,1)S(1)} %get-tuple-element.25.pick, bf16[6,128,1024]{2,1,0:T(8,128)(2,1)S(1)} %get-tuple-element.26.stations, bf16[2048,1024]{1,0:T(8,128)(2,1)S(1)} %get-tuple-element.27.table), custom_call_target="tpu_custom_call" | custom-call | tf_op jit(solution)/shard_map/correlate/pallas_call | solution.py:161
  62.6 1.9 %collective-permute-start.4 = (bf16[4,4,9,16,256]{4,3,2,1,0:T(8,128)(2,1)S(1)}, bf16[4,4,9,16,256]{4,3,2,1,0:T(8,128)(2,1)S(1)}, u32[]{:S(2)}, u32[]{:S(2)}) collective-permute-start(bf16[4,4,9,16,256]{4,3,2,1,0:T(8,128)(2,1)S(1)} %correlate.3), channel_id=1, source_target_pairs={{0,4},{4,0},{8,12},{12,8},{16,20},{20,16},{24,28},{28,24},{1,5},{5... | collective-permute-start | bytes 3538952 | tf_op jit(solution)/shard_map/ppermute | solution.py:173
  64.5 3.6 %correlate.2 = f32[4,4,9,16,256]{4,3,2,1,0:T(8,128)S(1)} custom-call(bf16[2,128,128]{2,1,0:T(8,128)(2,1)S(1)} %get-tuple-element.25.pick, bf16[6,128,1024]{2,1,0:T(8,128)(2,1)S(1)} %get-tuple-element.26.stations, bf16[2048,1024]{1,0:T(8,128)(2,1)S(1)} %get-tuple-element.27.table), custom_call_target="tpu_custom_call" | custom-call | tf_op jit(solution)/shard_map/correlate/pallas_call | solution.py:161
  68.1 0.0 collective-permute-done.4
  68.1 0.4 add_convert_fusion
  68.5 23.8 %all_to_all.17 = bf16[16,9,16,256]{3,2,1,0:T(8,128)(2,1)S(1)} all-to-all(bf16[16,9,16,256]{3,2,1,0:T(8,128)(2,1)S(1)} %bitcast.23), channel_id=1, replica_groups={{0,1,2,3,8,9,10,11,16,17,18,19,24,25,26,27},{4,5,6,7,12,13,14,15,20,21,..., dimensions={0} | all-to-all | bytes 2359296 | tf_op jit(solution)/shard_map/all_to_all | solution.py:176
  92.3 0.2 convert_reduce_fusion
  92.5 12.7 %all_gather.11 = bf16[9,16,1024]{2,1,0:T(8,128)(2,1)S(1)} all-gather(bf16[9,16,256]{2,1,0:T(8,128)(2,1)S(1)} %multiply_convert_fusion), channel_id=1, replica_groups=mesh['sta'=16,'grp'=8,'hr'=4] {'hr'}, dimensions={2}, use_global_device_ids=true | all-gather | bytes 368640 | tf_op jit(solution)/shard_map/all_gather | solution.py:178
  105.1 0.9 convert_bitcast_fusion
  (4 shorter events, 0.1 us)
Async XLA Ops:
  0.0 1.1 %copy-start = (bf16[1,8,6,8192]{3,1,2,0:T(8,128)(2,1)S(1)}, bf16[1,8,6,8192]{3,1,2,0:T(8,128)(2,1)}, u32[]{:S(2)}) copy-start(bf16[1,8,6,8192]{3,1,2,0:T(8,128)(2,1)} %param.4) | copy-start | bytes 2359300
  31.6 25.0 %collective-permute-start = (bf16[4,6,8,1024]{3,2,1,0:T(8,128)(2,1)S(1)}, bf16[4,6,8,1024]{3,2,1,0:T(8,128)(2,1)S(1)}, u32[]{:S(2)}, u32[]{:S(2)}) collective-permute-start(bf16[4,6,8,1024]{3,2,1,0:T(8,128)(2,1)S(1)} %bitcast.19), channel_id=1, source_target_pairs={{0,32},{4,484},{8,40},{12,492},{16,48},{20,500},{24,56},{28,508},{... | collective-permute-start | bytes 1179656 | tf_op jit(solution)/shard_map/ppermute | solution.py:120
  34.2 22.5 %collective-permute-start.1 = (bf16[4,6,8,1024]{3,2,1,0:T(8,128)(2,1)S(1)}, bf16[4,6,8,1024]{3,2,1,0:T(8,128)(2,1)S(1)}, u32[]{:S(2)}, u32[]{:S(2)}) collective-permute-start(bf16[4,6,8,1024]{3,2,1,0:T(8,128)(2,1)S(1)} %bitcast.20), channel_id=1, source_target_pairs={{0,480},{4,36},{8,488},{12,44},{16,496},{20,52},{24,504},{28,60},{... | collective-permute-start | bytes 1179656 | tf_op jit(solution)/shard_map/ppermute | solution.py:120
  38.7 17.9 %collective-permute-start.2 = (bf16[2,6,8,1024]{3,2,1,0:T(8,128)(2,1)S(1)}, bf16[2,6,8,1024]{3,2,1,0:T(8,128)(2,1)S(1)}, u32[]{:S(2)}, u32[]{:S(2)}) collective-permute-start(bf16[2,6,8,1024]{3,2,1,0:T(8,128)(2,1)S(1)} %bitcast.25), channel_id=1, source_target_pairs={{0,64},{4,452},{8,72},{12,460},{16,80},{20,468},{24,88},{28,476},{... | collective-permute-start | bytes 589832 | tf_op jit(solution)/shard_map/ppermute | solution.py:120
  40.7 16.0 %collective-permute-start.3 = (bf16[2,6,8,1024]{3,2,1,0:T(8,128)(2,1)S(1)}, bf16[2,6,8,1024]{3,2,1,0:T(8,128)(2,1)S(1)}, u32[]{:S(2)}, u32[]{:S(2)}) collective-permute-start(bf16[2,6,8,1024]{3,2,1,0:T(8,128)(2,1)S(1)} %bitcast.24), channel_id=1, source_target_pairs={{0,448},{4,68},{8,456},{12,76},{16,464},{20,84},{24,472},{28,92},{... | collective-permute-start | bytes 589832 | tf_op jit(solution)/shard_map/ppermute | solution.py:120
  48.0 8.6 %all-to-all-start = ((s32[8,1,16]{2,1,0:T(1,128)}), s32[8,1,16]{2,1,0:T(1,128)S(1)}, u32[]{:S(2)}, u32[]{:S(2)}) async-start(s32[8,1,16]{2,1,0:T(1,128)} %bitcast.26), calls=%async_computation | async-start | bytes 8192 | tf_op jit(solution)/shard_map/all_to_all | solution.py:138
  62.6 5.5 %collective-permute-start.4 = (bf16[4,4,9,16,256]{4,3,2,1,0:T(8,128)(2,1)S(1)}, bf16[4,4,9,16,256]{4,3,2,1,0:T(8,128)(2,1)S(1)}, u32[]{:S(2)}, u32[]{:S(2)}) collective-permute-start(bf16[4,4,9,16,256]{4,3,2,1,0:T(8,128)(2,1)S(1)} %correlate.3), channel_id=1, source_target_pairs={{0,4},{4,0},{8,12},{12,8},{16,20},{20,16},{24,28},{28,24},{1,5},{5... | collective-permute-start | bytes 3538952 | tf_op jit(solution)/shard_map/ppermute | solution.py:173

commit v7 on v6

--- a/solution.py
+++ b/solution.py
@@ -12,7 +12,8 @@
 NZ, NG, NY, NC, NX = 16, 8, 4, 2, 4
 SD, PD, NB = 8, 16, 8192
 W = NB // NG
-NR = 4
+STEP = 4
+ORDER = (0, 12, 4, 8, 15, 11, 3, 7, 1, 13, 5, 9, 14, 10, 2, 6)
 BITS = 10
 FINE = 32
 HALF = NY * PD
@@ -23,11 +24,8 @@
 
 
 def codes(plane_ref, source_ref, owner_ref, row_ref, out_ref):
-    plane, owner = plane_ref[0], owner_ref[...]
-    away = (owner - plane) & (NR - 1)
-    first = jnp.where(away == 0, 0, jnp.where(away == 3, 1, jnp.where(away == 1, 2, 3)))
-    slot = first * (NZ // NR) + owner // NR
-    code = (slot * SD + row_ref[...]) * (NZ * SD) + plane // NR * SD + source_ref[...]
+    away = (owner_ref[...] - plane_ref[0]) & (NZ - 1)
+    code = (away * SD + row_ref[...]) * SD + source_ref[...]
     out_ref[...] = jnp.broadcast_to(code, (NG, PD))
 
 
@@ -66,18 +64,22 @@
         c0, c1 = code_ref[NC * k : NC * k + 1], code_ref[NC * k + 1 : NC * k + 2]
         for half, code in enumerate((jnp.where(even, c1, c0), jnp.where(even, c0, c1))):
             at = half * 2 * HALF + k * PD
-            row[0:1, at : at + PD] = code // (NZ * SD)
-            row[0:1, at + HALF : at + HALF + PD] = code % (NZ * SD)
+            away, place = code // (SD * SD), jnp.zeros_like(code)
+            away = jnp.where(even, away, -away & (NZ - 1))
+            for p, d in enumerate(ORDER):
+                place = jnp.where(away == d, p, place)
+            row[0:1, at : at + PD] = place * SD + code // SD % SD
+            row[0:1, at + HALF : at + HALF + PD] = code % SD
     station = lax.broadcasted_iota(jnp.int32, (NZ * SD, 2 * HALF), 0)
     for half in range(NC):
         hot = (station == row[0:1, half * 2 * HALF : (half + 1) * 2 * HALF]).astype(jnp.float32)
         pick[half] = hot.T.astype(jnp.bfloat16)
-    part = NZ * SD // NR
-    rows = (0, pl.multiple_of(part + core * part, part), pl.multiple_of(2 * part - core * part, part), 3 * part, 7 * part // 2)
-    for at, ref in zip(rows, (near_ref, first_ref, second_ref, third_ref, fourth_ref)):
+    at = 0
+    for ref in (near_ref, first_ref, second_ref, third_ref, fourth_ref):
         for comp in range(6):
             x = ref[:, comp].astype(jnp.float32).reshape(-1, W).astype(jnp.bfloat16)
-            stations[comp, pl.ds(at, x.shape[0]), :] = x
+            stations[comp, at : at + x.shape[0]] = x
+        at += x.shape[0]
 
 
 def correlate(half, pick, stations, table, out_ref, cross):
@@ -111,8 +113,6 @@
 def body(spectra, pair_source, pair_owner, pair_row):
     s, g = lax.axis_index("sta"), lax.axis_index("grp")
     mine = lax.dynamic_slice_in_dim(spectra[0], g * W, W, 2).transpose(1, 0, 2)
-    planes = [list(range(p, NZ, NR)) for p in range(NR)]
-    near = lax.all_gather(mine, "sta", axis=0, axis_index_groups=planes)
 
     def neighbour(x, step):
         turn = [step if i % NC == 0 else -step for i in range(NG)]
@@ -122,9 +122,15 @@
     pos = lax.axis_index("hr") * TW + jnp.arange(TW, dtype=jnp.int32)
     taper = 0.75 - 0.25 * jnp.cos(TWO_PI * (pos.astype(jnp.float32) + 0.5) / LAGS)
     scale = taper / (NX * math.sqrt(NB))
-    half = NZ // NR // 2
-    low, high, pair_row = lax.optimization_barrier((near[:half], near[half:], pair_row))
-    moved = (neighbour(near, 1), neighbour(near, -1), neighbour(low, 2), neighbour(high, -2))
+    back, ahead = neighbour(mine, STEP), neighbour(mine, -STEP)
+    far = jnp.concatenate([neighbour(back[:3], STEP), neighbour(ahead[3:], -STEP)])
+    near = jnp.stack([mine, back, ahead, far])
+    moved = (
+        neighbour(near, 1),
+        neighbour(near, -1),
+        neighbour(jnp.stack([mine, back]), 2),
+        neighbour(jnp.stack([mine, ahead]), -2),
+    )
 
     smem = pl.BlockSpec(memory_space=pltpu.SMEM)
     code = pl.pallas_call(

time: 106 us -> 107 us (level)
  blocking collectives: 67 us -> 37.5 us
  starting transfers between devices: 21.8 us -> 50.5 us
  waiting for transfers between devices: 3.7 us -> 5.03 us
    all_gather x1 -> x0, blocking collectives: 30.5 us -> none  [body(): near = lax.all_gather(mine, 'sta', axis=0, axis_index_groups=planes)]
    ppermute x4 -> x8, starting transfers between devices: 15 us -> 43.6 us  [neighbour(): return lax.ppermute(x, ('sta', 'grp'), perm)]
    ppermute x4 -> x8, waiting for transfers between devices: 0.01 us -> 1.35 us  [neighbour(): return lax.ppermute(x, ('sta', 'grp'), perm)]
    unnamed x2 -> x0, local copies, waits for them, and re-layouts: 1.13 us -> none
  transfers between devices with their start and end apart: 6 -> 10, of which waited for: 1 -> 4; matrix products, arithmetic and copies ran while one was open for 0% -> 0% of each run, Pallas kernels for 5% -> 5%
where the time goes in v7:
time: 107 us; the launch traced here: 106 us
  starting transfers between devices  50.5 us (47%)
  blocking collectives  37.5 us (35%)
  Pallas kernels  10.8 us (10%)
  waiting for transfers between devices  5.03 us (5%)
  other arithmetic  1.6 us (1%)
    ppermute x8, starting transfers between devices, neighbour(): return lax.ppermute(x, ('sta', 'grp'), perm)  43.6 us
    all_to_all x1, blocking collectives, body(): lax.all_to_all(part, ('grp', 'hr'), 0, 0, axis_index_groups=chips, tiled=...  24.8 us
    all_gather x1, blocking collectives, body(): lax.all_gather((total * scale).astype(jnp.bfloat16), 'hr', axis=2, tiled=...  12.7 us
    pallas_call x2, Pallas kernels, lags(): pl.pallas_call(functools.partial(correlate, half), out_shape=jax.ShapeDty...  7.14 us
    all_to_all x1, starting transfers between devices, body(): code = lax.all_to_all(code, 'grp', 0, 0, tiled=True)  4.92 us
    all_to_all x1, waiting for transfers between devices, body(): code = lax.all_to_all(code, 'grp', 0, 0, tiled=True)  3.68 us
    pallas_call x1, Pallas kernels, body(): pl.pallas_call(stage, out_shape=(jax.ShapeDtypeStruct((2 * W, LAGS), jnp....  2.38 us
  transfers between devices with their start and end apart: 10, of which 4 were waited for; matrix products, arithmetic and copies ran while one was open for 0% of the time, Pallas kernels for 5%

profile of v7, /device:TPU:8, one launch (start us, length us, event | category | flops | bytes accessed | tf_op | source)
XLA Modules:
  0.0 106.4 jit_solution(11781747708720446919)
XLA Ops:
  0.0 0.9 dynamic-slice_bitcast_fusion
  0.9 9.1 %collective-permute-start = (bf16[6,8,1024]{2,1,0:T(8,128)(2,1)S(1)}, bf16[6,8,1024]{2,1,0:T(8,128)(2,1)S(1)}, u32[]{:S(2)}, u32[]{:S(2)}) collective-permute-start(bf16[6,8,1024]{2,1,0:T(8,128)(2,1)S(1)} %get-tuple-element.24), channel_id=1, source_target_pairs={{0,128},{4,388},{8,136},{12,396},{16,144},{20,404},{24,152},{28,41... | collective-permute-start | bytes 294920 | tf_op jit(solution)/shard_map/ppermute | solution.py:120
  10.0 5.6 %collective-permute-start.1 = (bf16[6,8,1024]{2,1,0:T(8,128)(2,1)S(1)}, bf16[6,8,1024]{2,1,0:T(8,128)(2,1)S(1)}, u32[]{:S(2)}, u32[]{:S(2)}) collective-permute-start(bf16[6,8,1024]{2,1,0:T(8,128)(2,1)S(1)} %get-tuple-element.24), channel_id=1, source_target_pairs={{0,384},{4,132},{8,392},{12,140},{16,400},{20,148},{24,408},{28,15... | collective-permute-start | bytes 294920 | tf_op jit(solution)/shard_map/ppermute | solution.py:120
  15.6 0.9 collective-permute-done
  16.5 11.3 %collective-permute-start.2 = (bf16[3,8,1024]{2,1,0:T(8,128)(2,1)S(1)}, bf16[3,8,1024]{2,1,0:T(8,128)(2,1)S(1)}, u32[]{:S(2)}, u32[]{:S(2)}) collective-permute-start(bf16[3,8,1024]{2,1,0:T(8,128)(2,1)S(1)} %slice.8), channel_id=1, source_target_pairs={{0,128},{4,388},{8,136},{12,396},{16,144},{20,404},{24,152},{28,41... | collective-permute-start | bytes 147464 | tf_op jit(solution)/shard_map/ppermute | solution.py:120
  27.8 2.6 %collective-permute-start.3 = (bf16[3,8,1024]{2,1,0:T(8,128)(2,1)S(1)}, bf16[3,8,1024]{2,1,0:T(8,128)(2,1)S(1)}, u32[]{:S(2)}, u32[]{:S(2)}) collective-permute-start(bf16[3,8,1024]{2,1,0:T(8,128)(2,1)S(1)} %slice.9), channel_id=1, source_target_pairs={{0,384},{4,132},{8,392},{12,140},{16,400},{20,148},{24,408},{28,15... | collective-permute-start | bytes 147464 | tf_op jit(solution)/shard_map/ppermute | solution.py:120
  30.4 5.9 %collective-permute-start.7 = (bf16[2,6,8,1024]{3,2,1,0:T(8,128)(2,1)S(1)}, bf16[2,6,8,1024]{3,2,1,0:T(8,128)(2,1)S(1)}, u32[]{:S(2)}, u32[]{:S(2)}) collective-permute-start(bf16[2,6,8,1024]{3,2,1,0:T(8,128)(2,1)S(1)} %get-tuple-element.25), channel_id=1, source_target_pairs={{0,448},{4,68},{8,456},{12,76},{16,464},{20,84},{24,472},{28,92},{... | collective-permute-start | bytes 589832 | tf_op jit(solution)/shard_map/ppermute | solution.py:120
  36.3 1.9 %collective-permute-start.6 = (bf16[2,6,8,1024]{3,2,1,0:T(8,128)(2,1)S(1)}, bf16[2,6,8,1024]{3,2,1,0:T(8,128)(2,1)S(1)}, u32[]{:S(2)}, u32[]{:S(2)}) collective-permute-start(bf16[2,6,8,1024]{3,2,1,0:T(8,128)(2,1)S(1)} %get-tuple-element.26), channel_id=1, source_target_pairs={{0,64},{4,452},{8,72},{12,460},{16,80},{20,468},{24,88},{28,476},{... | collective-permute-start | bytes 589832 | tf_op jit(solution)/shard_map/ppermute | solution.py:120
  38.3 0.1 collective-permute-done.3
  38.5 5.4 %collective-permute-start.5 = (bf16[4,6,8,1024]{3,2,1,0:T(8,128)(2,1)S(1)}, bf16[4,6,8,1024]{3,2,1,0:T(8,128)(2,1)S(1)}, u32[]{:S(2)}, u32[]{:S(2)}) collective-permute-start(bf16[4,6,8,1024]{3,2,1,0:T(8,128)(2,1)S(1)} %pad_maximum_fusion.near_ref), channel_id=1, source_target_pairs={{0,480},{4,36},{8,488},{12,44},{16,496},{20,52},{24,504},{28,60},{... | collective-permute-start | bytes 1179656 | tf_op jit(solution)/shard_map/ppermute | solution.py:120
  43.9 1.9 %collective-permute-start.4 = (bf16[4,6,8,1024]{3,2,1,0:T(8,128)(2,1)S(1)}, bf16[4,6,8,1024]{3,2,1,0:T(8,128)(2,1)S(1)}, u32[]{:S(2)}, u32[]{:S(2)}) collective-permute-start(bf16[4,6,8,1024]{3,2,1,0:T(8,128)(2,1)S(1)} %pad_maximum_fusion.near_ref), channel_id=1, source_target_pairs={{0,32},{4,484},{8,40},{12,492},{16,48},{20,500},{24,56},{28,508},{... | collective-permute-start | bytes 1179656 | tf_op jit(solution)/shard_map/ppermute | solution.py:120
  45.8 1.3 %codes.1 = s32[8,16]{1,0:T(8,128)} custom-call(s32[1]{0:T(128)} %bitcast.1.plane_ref, s32[1,16]{1,0:T(1,128)} %bitcast.30, s32[1,16]{1,0:T(1,128)} %bitcast.31, s32[1,16]{1,0:T(1,128)} %bitcast.32), custom_call_target="tpu_custom_call" | custom-call | flops 10000000000 | bytes 1000000 | tf_op jit(solution)/shard_map/codes/pallas_call | solution.py:136
  47.1 4.9 %all-to-all-start = ((s32[8,1,16]{2,1,0:T(1,128)}), s32[8,1,16]{2,1,0:T(1,128)S(1)}, u32[]{:S(2)}, u32[]{:S(2)}) async-start(s32[8,1,16]{2,1,0:T(1,128)} %bitcast.29), calls=%async_computation | async-start | bytes 8192 | tf_op jit(solution)/shard_map/all_to_all | solution.py:144
  52.1 3.7 %all-to-all-done = s32[8,1,16]{2,1,0:T(1,128)S(1)} async-done(((s32[8,1,16]{2,1,0:T(1,128)}), s32[8,1,16]{2,1,0:T(1,128)S(1)}, u32[]{:S(2)}, u32[]{:S(2)}) %all-to-all-start) | async-done | bytes 544 | tf_op jit(solution)/shard_map/all_to_all | solution.py:144
  55.8 0.3 collective-permute-done.4.first_ref
  56.0 2.4 %stage.1 = (bf16[2048,1024]{1,0:T(8,128)(2,1)S(1)}, bf16[6,128,1024]{2,1,0:T(8,128)(2,1)S(1)}, bf16[2,128,128]{2,1,0:T(8,128)(2,1)S(1)}) custom-call(s32[1]{0:T(128)} %bitcast.grp_ref, s32[8,16]{1,0:T(8,128)S(1)} %bitcast.23, bf16[4,6,8,1024]{3,2,1,0:T(8,128)(2,1)S(1)} %pad_maximum_fusion.near_ref, ...), custom_call_target="tpu_custom_call" | custom-call | tf_op jit(solution)/shard_map/stage/pallas_call | solution.py:148
  58.4 3.6 %correlate.3 = bf16[4,4,9,16,256]{4,3,2,1,0:T(8,128)(2,1)S(1)} custom-call(bf16[2,128,128]{2,1,0:T(8,128)(2,1)S(1)} %get-tuple-element.19.pick, bf16[6,128,1024]{2,1,0:T(8,128)(2,1)S(1)} %get-tuple-element.20.stations, bf16[2048,1024]{1,0:T(8,128)(2,1)S(1)} %get-tuple-element.21.table), custom_call_target="tpu_custom_call" | custom-call | tf_op jit(solution)/shard_map/correlate/pallas_call | solution.py:167
  62.0 1.9 %collective-permute-start.8 = (bf16[4,4,9,16,256]{4,3,2,1,0:T(8,128)(2,1)S(1)}, bf16[4,4,9,16,256]{4,3,2,1,0:T(8,128)(2,1)S(1)}, u32[]{:S(2)}, u32[]{:S(2)}) collective-permute-start(bf16[4,4,9,16,256]{4,3,2,1,0:T(8,128)(2,1)S(1)} %correlate.3), channel_id=1, source_target_pairs={{0,4},{4,0},{8,12},{12,8},{16,20},{20,16},{24,28},{28,24},{1,5},{5... | collective-permute-start | bytes 3538952 | tf_op jit(solution)/shard_map/ppermute | solution.py:179
  63.9 3.6 %correlate.2 = f32[4,4,9,16,256]{4,3,2,1,0:T(8,128)S(1)} custom-call(bf16[2,128,128]{2,1,0:T(8,128)(2,1)S(1)} %get-tuple-element.19.pick, bf16[6,128,1024]{2,1,0:T(8,128)(2,1)S(1)} %get-tuple-element.20.stations, bf16[2048,1024]{1,0:T(8,128)(2,1)S(1)} %get-tuple-element.21.table), custom_call_target="tpu_custom_call" | custom-call | tf_op jit(solution)/shard_map/correlate/pallas_call | solution.py:167
  67.5 0.4 add_convert_fusion
  67.9 24.8 %all_to_all.17 = bf16[16,9,16,256]{3,2,1,0:T(8,128)(2,1)S(1)} all-to-all(bf16[16,9,16,256]{3,2,1,0:T(8,128)(2,1)S(1)} %bitcast.24), channel_id=1, replica_groups={{0,1,2,3,8,9,10,11,16,17,18,19,24,25,26,27},{4,5,6,7,12,13,14,15,20,21,..., dimensions={0} | all-to-all | bytes 2359296 | tf_op jit(solution)/shard_map/all_to_all | solution.py:182
  92.7 0.2 convert_reduce_fusion
  92.9 12.7 %all_gather.3 = bf16[9,16,1024]{2,1,0:T(8,128)(2,1)S(1)} all-gather(bf16[9,16,256]{2,1,0:T(8,128)(2,1)S(1)} %multiply_convert_fusion), channel_id=1, replica_groups=mesh['sta'=16,'grp'=8,'hr'=4] {'hr'}, dimensions={2}, use_global_device_ids=true | all-gather | bytes 368640 | tf_op jit(solution)/shard_map/all_gather | solution.py:184
  105.6 0.9 convert_bitcast_fusion
  (13 shorter events, 0.2 us)
Async XLA Ops:
  0.9 15.6 %collective-permute-start = (bf16[6,8,1024]{2,1,0:T(8,128)(2,1)S(1)}, bf16[6,8,1024]{2,1,0:T(8,128)(2,1)S(1)}, u32[]{:S(2)}, u32[]{:S(2)}) collective-permute-start(bf16[6,8,1024]{2,1,0:T(8,128)(2,1)S(1)} %get-tuple-element.24), channel_id=1, source_target_pairs={{0,128},{4,388},{8,136},{12,396},{16,144},{20,404},{24,152},{28,41... | collective-permute-start | bytes 294920 | tf_op jit(solution)/shard_map/ppermute | solution.py:120
  10.0 17.8 %collective-permute-start.1 = (bf16[6,8,1024]{2,1,0:T(8,128)(2,1)S(1)}, bf16[6,8,1024]{2,1,0:T(8,128)(2,1)S(1)}, u32[]{:S(2)}, u32[]{:S(2)}) collective-permute-start(bf16[6,8,1024]{2,1,0:T(8,128)(2,1)S(1)} %get-tuple-element.24), channel_id=1, source_target_pairs={{0,384},{4,132},{8,392},{12,140},{16,400},{20,148},{24,408},{28,15... | collective-permute-start | bytes 294920 | tf_op jit(solution)/shard_map/ppermute | solution.py:120
  16.5 21.7 %collective-permute-start.2 = (bf16[3,8,1024]{2,1,0:T(8,128)(2,1)S(1)}, bf16[3,8,1024]{2,1,0:T(8,128)(2,1)S(1)}, u32[]{:S(2)}, u32[]{:S(2)}) collective-permute-start(bf16[3,8,1024]{2,1,0:T(8,128)(2,1)S(1)} %slice.8), channel_id=1, source_target_pairs={{0,128},{4,388},{8,136},{12,396},{16,144},{20,404},{24,152},{28,41... | collective-permute-start | bytes 147464 | tf_op jit(solution)/shard_map/ppermute | solution.py:120
  27.8 10.6 %collective-permute-start.3 = (bf16[3,8,1024]{2,1,0:T(8,128)(2,1)S(1)}, bf16[3,8,1024]{2,1,0:T(8,128)(2,1)S(1)}, u32[]{:S(2)}, u32[]{:S(2)}) collective-permute-start(bf16[3,8,1024]{2,1,0:T(8,128)(2,1)S(1)} %slice.9), channel_id=1, source_target_pairs={{0,384},{4,132},{8,392},{12,140},{16,400},{20,148},{24,408},{28,15... | collective-permute-start | bytes 147464 | tf_op jit(solution)/shard_map/ppermute | solution.py:120
  30.4 25.3 %collective-permute-start.7 = (bf16[2,6,8,1024]{3,2,1,0:T(8,128)(2,1)S(1)}, bf16[2,6,8,1024]{3,2,1,0:T(8,128)(2,1)S(1)}, u32[]{:S(2)}, u32[]{:S(2)}) collective-permute-start(bf16[2,6,8,1024]{3,2,1,0:T(8,128)(2,1)S(1)} %get-tuple-element.25), channel_id=1, source_target_pairs={{0,448},{4,68},{8,456},{12,76},{16,464},{20,84},{24,472},{28,92},{... | collective-permute-start | bytes 589832 | tf_op jit(solution)/shard_map/ppermute | solution.py:120
  36.3 19.5 %collective-permute-start.6 = (bf16[2,6,8,1024]{3,2,1,0:T(8,128)(2,1)S(1)}, bf16[2,6,8,1024]{3,2,1,0:T(8,128)(2,1)S(1)}, u32[]{:S(2)}, u32[]{:S(2)}) collective-permute-start(bf16[2,6,8,1024]{3,2,1,0:T(8,128)(2,1)S(1)} %get-tuple-element.26), channel_id=1, source_target_pairs={{0,64},{4,452},{8,72},{12,460},{16,80},{20,468},{24,88},{28,476},{... | collective-permute-start | bytes 589832 | tf_op jit(solution)/shard_map/ppermute | solution.py:120
  38.5 17.3 %collective-permute-start.5 = (bf16[4,6,8,1024]{3,2,1,0:T(8,128)(2,1)S(1)}, bf16[4,6,8,1024]{3,2,1,0:T(8,128)(2,1)S(1)}, u32[]{:S(2)}, u32[]{:S(2)}) collective-permute-start(bf16[4,6,8,1024]{3,2,1,0:T(8,128)(2,1)S(1)} %pad_maximum_fusion.near_ref), channel_id=1, source_target_pairs={{0,480},{4,36},{8,488},{12,44},{16,496},{20,52},{24,504},{28,60},{... | collective-permute-start | bytes 1179656 | tf_op jit(solution)/shard_map/ppermute | solution.py:120
  43.9 12.1 %collective-permute-start.4 = (bf16[4,6,8,1024]{3,2,1,0:T(8,128)(2,1)S(1)}, bf16[4,6,8,1024]{3,2,1,0:T(8,128)(2,1)S(1)}, u32[]{:S(2)}, u32[]{:S(2)}) collective-permute-start(bf16[4,6,8,1024]{3,2,1,0:T(8,128)(2,1)S(1)} %pad_maximum_fusion.near_ref), channel_id=1, source_target_pairs={{0,32},{4,484},{8,40},{12,492},{16,48},{20,500},{24,56},{28,508},{... | collective-permute-start | bytes 1179656 | tf_op jit(solution)/shard_map/ppermute | solution.py:120
  47.1 8.6 %all-to-all-start = ((s32[8,1,16]{2,1,0:T(1,128)}), s32[8,1,16]{2,1,0:T(1,128)S(1)}, u32[]{:S(2)}, u32[]{:S(2)}) async-start(s32[8,1,16]{2,1,0:T(1,128)} %bitcast.29), calls=%async_computation | async-start | bytes 8192 | tf_op jit(solution)/shard_map/all_to_all | solution.py:144
  62.0 5.5 %collective-permute-start.8 = (bf16[4,4,9,16,256]{4,3,2,1,0:T(8,128)(2,1)S(1)}, bf16[4,4,9,16,256]{4,3,2,1,0:T(8,128)(2,1)S(1)}, u32[]{:S(2)}, u32[]{:S(2)}) collective-permute-start(bf16[4,4,9,16,256]{4,3,2,1,0:T(8,128)(2,1)S(1)} %correlate.3), channel_id=1, source_target_pairs={{0,4},{4,0},{8,12},{12,8},{16,20},{20,16},{24,28},{28,24},{1,5},{5... | collective-permute-start | bytes 3538952 | tf_op jit(solution)/shard_map/ppermute | solution.py:179

commit v8 on v7

--- a/solution.py
+++ b/solution.py
@@ -29,37 +29,16 @@
     out_ref[...] = jnp.broadcast_to(code, (NG, PD))
 
 
-def stage(grp_ref, code_ref, near_ref, first_ref, second_ref, third_ref, fourth_ref, table, stations, pick, row, hi_c, hi_s):
-    core, g = grp_ref[0] % NC, grp_ref[0]
-    bit = lax.broadcasted_iota(jnp.int32, (16, LAGS), 0)
-    lag = lax.broadcasted_iota(jnp.int32, (16, LAGS), 1) - LAGS // 2
-    bins = jnp.where(bit < BITS, jnp.left_shift(1, bit), g * W)
-    ang = ((bins * lag) & (2 * NB - 1)).astype(jnp.float32) * (TWO_PI / (2 * NB))
-    cos, sin = jnp.cos(ang), jnp.sin(ang)
-
-    def turned(c, s, bits):
-        at = lax.broadcasted_iota(jnp.int32, (FINE, LAGS), 0)
-        for k, b in enumerate(bits):
-            on = (jnp.right_shift(at, k) & 1) == 1
-            kc, ks = jnp.where(on, cos[b : b + 1], 1.0), jnp.where(on, sin[b : b + 1], 0.0)
-            c, s = c * kc - s * ks, s * kc + c * ks
-        return c, s
-
-    half_bits = BITS // 2
-    lc, ls = turned(jnp.ones((FINE, LAGS), jnp.float32), jnp.zeros((FINE, LAGS), jnp.float32), range(half_bits))
-    base = jnp.broadcast_to(cos[BITS : BITS + 1], (FINE, LAGS)), jnp.broadcast_to(sin[BITS : BITS + 1], (FINE, LAGS))
-    hi_c[...], hi_s[...] = turned(*base, range(half_bits, BITS))
-
-    def fill(i, carry):
-        hc, hs = hi_c[pl.ds(i, 1), :], hi_s[pl.ds(i, 1), :]
-        at = pl.multiple_of(i * FINE, FINE)
-        table[pl.ds(at, FINE), :] = (hc * lc - hs * ls).astype(jnp.bfloat16)
-        table[pl.ds(W + at, FINE), :] = (-(hs * lc + hc * ls)).astype(jnp.bfloat16)
-        return carry
-
-    lax.fori_loop(0, W // FINE, fill, 0)
-
-    even = core == 0
+def stack(refs, stations, at):
+    for ref in refs:
+        for comp in range(6):
+            x = ref[:, comp].astype(jnp.float32).reshape(-1, W).astype(jnp.bfloat16)
+            stations[comp, at : at + x.shape[0]] = x
+        at += x.shape[0]
+
+
+def stage_far(grp_ref, code_ref, third_ref, fourth_ref, stations, pick, row):
+    even = grp_ref[0] % NC == 0
     for k in range(NY):
         c0, c1 = code_ref[NC * k : NC * k + 1], code_ref[NC * k + 1 : NC * k + 2]
         for half, code in enumerate((jnp.where(even, c1, c0), jnp.where(even, c0, c1))):
@@ -74,12 +53,41 @@
     for half in range(NC):
         hot = (station == row[0:1, half * 2 * HALF : (half + 1) * 2 * HALF]).astype(jnp.float32)
         pick[half] = hot.T.astype(jnp.bfloat16)
-    at = 0
-    for ref in (near_ref, first_ref, second_ref, third_ref, fourth_ref):
-        for comp in range(6):
-            x = ref[:, comp].astype(jnp.float32).reshape(-1, W).astype(jnp.bfloat16)
-            stations[comp, at : at + x.shape[0]] = x
-        at += x.shape[0]
+    stack((third_ref, fourth_ref), stations, 0)
+
+
+def stage(grp_ref, near_ref, first_ref, second_ref, far_ref, table, stations, hi_c, hi_s):
+    g = grp_ref[0]
+    bit = lax.broadcasted_iota(jnp.int32, (16, LAGS), 0)
+    lag = lax.broadcasted_iota(jnp.int32, (16, LAGS), 1) - LAGS // 2
+    bins = jnp.where(bit < BITS, jnp.left_shift(1, bit), g * W)
+    ang = ((bins * lag) & (2 * NB - 1)).astype(jnp.float32) * (TWO_PI / (2 * NB))
+    cos, sin = jnp.cos(ang), jnp.sin(ang)
+
+    def turned(c, s, bits):
+        at = lax.broadcasted_iota(jnp.int32, (FINE, LAGS), 0)
+        for k, b in enumerate(bits):
+            on = (jnp.right_shift(at, k) & 1) == 1
+            kc, ks = jnp.where(on, cos[b : b + 1], 1.0), jnp.where(on, sin[b : b + 1], 0.0)
+            c, s = c * kc - s * ks, s * kc + c * ks
+        return c, s
+
+    half_bits = BITS // 2
+    lc, ls = turned(jnp.ones((FINE, LAGS), jnp.float32), jnp.zeros((FINE, LAGS), jnp.float32), range(half_bits))
+    base = jnp.broadcast_to(cos[BITS : BITS + 1], (FINE, LAGS)), jnp.broadcast_to(sin[BITS : BITS + 1], (FINE, LAGS))
+    hi_c[...], hi_s[...] = turned(*base, range(half_bits, BITS))
+
+    def fill(i, carry):
+        hc, hs = hi_c[pl.ds(i, 1), :], hi_s[pl.ds(i, 1), :]
+        at = pl.multiple_of(i * FINE, FINE)
+        table[pl.ds(at, FINE), :] = (hc * lc - hs * ls).astype(jnp.bfloat16)
+        table[pl.ds(W + at, FINE), :] = (-(hs * lc + hc * ls)).astype(jnp.bfloat16)
+        return carry
+
+    lax.fori_loop(0, W // FINE, fill, 0)
+
+    stack((near_ref, first_ref, second_ref), stations, 0)
+    stations[:, 12 * SD :] = far_ref[...]
 
 
 def correlate(half, pick, stations, table, out_ref, cross):
@@ -122,7 +130,22 @@
     pos = lax.axis_index("hr") * TW + jnp.arange(TW, dtype=jnp.int32)
     taper = 0.75 - 0.25 * jnp.cos(TWO_PI * (pos.astype(jnp.float32) + 0.5) / LAGS)
     scale = taper / (NX * math.sqrt(NB))
+    mine, pair_row = lax.optimization_barrier((mine, pair_row))
     back, ahead = neighbour(mine, STEP), neighbour(mine, -STEP)
+
+    long = pl.CostEstimate(flops=10**10, bytes_accessed=10**6, transcendentals=0)
+    smem = pl.BlockSpec(memory_space=pltpu.SMEM)
+    code = pl.pallas_call(
+        codes,
+        out_shape=jax.ShapeDtypeStruct((NG, PD), jnp.int32),
+        in_specs=[smem] + vmem(3),
+        out_specs=vmem(1)[0],
+        cost_estimate=long,
+        name="codes",
+    )(s[None], pair_source[None], pair_owner.T, pair_row[None])
+    code = lax.all_to_all(code, "grp", 0, 0, tiled=True)
+
+    code, back, ahead, scale = lax.optimization_barrier((code, back, ahead, scale))
     far = jnp.concatenate([neighbour(back[:3], STEP), neighbour(ahead[3:], -STEP)])
     near = jnp.stack([mine, back, ahead, far])
     moved = (
@@ -132,36 +155,34 @@
         neighbour(jnp.stack([mine, ahead]), -2),
     )
 
-    smem = pl.BlockSpec(memory_space=pltpu.SMEM)
-    code = pl.pallas_call(
-        codes,
-        out_shape=jax.ShapeDtypeStruct((NG, PD), jnp.int32),
+    params = pltpu.CompilerParams(vmem_limit_bytes=VMEM_LIMIT)
+    first, second, third, fourth = moved
+    far, pick = pl.pallas_call(
+        stage_far,
+        out_shape=(
+            jax.ShapeDtypeStruct((6, 4 * SD, W), jnp.bfloat16),
+            jax.ShapeDtypeStruct((NC, 2 * HALF, NZ * SD), jnp.bfloat16),
+        ),
         in_specs=[smem] + vmem(3),
-        out_specs=vmem(1)[0],
-        cost_estimate=pl.CostEstimate(flops=10**10, bytes_accessed=10**6, transcendentals=0),
-        name="codes",
-    )(s[None], pair_source[None], pair_owner.T, pair_row[None])
-    code = lax.all_to_all(code, "grp", 0, 0, tiled=True)
-    code, moved, scale = lax.optimization_barrier((code, moved, scale))
-
-    params = pltpu.CompilerParams(vmem_limit_bytes=VMEM_LIMIT)
-    table, stations, pick = pl.pallas_call(
+        out_specs=tuple(vmem(2)),
+        scratch_shapes=[pltpu.VMEM((8, NC * 2 * HALF), jnp.int32)],
+        cost_estimate=long,
+        compiler_params=params,
+        name="stage_far",
+    )(g[None], code, third, fourth)
+    far, pick, first, second = lax.optimization_barrier((far, pick, first, second))
+    table, stations = pl.pallas_call(
         stage,
         out_shape=(
             jax.ShapeDtypeStruct((2 * W, LAGS), jnp.bfloat16),
             jax.ShapeDtypeStruct((6, NZ * SD, W), jnp.bfloat16),
-            jax.ShapeDtypeStruct((NC, 2 * HALF, NZ * SD), jnp.bfloat16),
         ),
-        in_specs=[smem] + vmem(6),
-        out_specs=tuple(vmem(3)),
-        scratch_shapes=[
-            pltpu.VMEM((8, NC * 2 * HALF), jnp.int32),
-            pltpu.VMEM((FINE, LAGS), jnp.float32),
-            pltpu.VMEM((FINE, LAGS), jnp.float32),
-        ],
+        in_specs=[smem] + vmem(4),
+        out_specs=tuple(vmem(2)),
+        scratch_shapes=[pltpu.VMEM((FINE, LAGS), jnp.float32)] * 2,
         compiler_params=params,
         name="stage",
-    )(g[None], code, near, *moved)
+    )(g[None], near, first, second, far)
 
     def lags(half, dtype):
         return pl.pallas_call(

time: 107 us -> 112 us (1.047)
  waiting for transfers between devices: 5.03 us -> 13.2 us
  starting transfers between devices: 50.5 us -> 47.6 us
    ppermute x8, waiting for transfers between devices: 1.35 us -> 9.53 us  [neighbour(): return lax.ppermute(x, ('sta', 'grp'), perm)]
    ppermute x8, starting transfers between devices: 43.6 us -> 40.8 us  [neighbour(): return lax.ppermute(x, ('sta', 'grp'), perm)]
    unnamed x0 -> x2, local copies, waits for them, and re-layouts: none -> 1.13 us
where the time goes in v8:
time: 112 us; the launch traced here: 111 us
  starting transfers between devices  47.6 us (42%)
  blocking collectives  36.7 us (33%)
  waiting for transfers between devices  13.2 us (12%)
  Pallas kernels  10.9 us (10%)
  other arithmetic  1.6 us (1%)
  local copies, waits for them, and re-layouts  1.15 us (1%)
    ppermute x8, starting transfers between devices, neighbour(): return lax.ppermute(x, ('sta', 'grp'), perm)  40.8 us
    all_to_all x1, blocking collectives, body(): lax.all_to_all(part, ('grp', 'hr'), 0, 0, axis_index_groups=chips, tiled=...  24 us
    all_gather x1, blocking collectives, body(): lax.all_gather((total * scale).astype(jnp.bfloat16), 'hr', axis=2, tiled=...  12.7 us
    ppermute x8, waiting for transfers between devices, neighbour(): return lax.ppermute(x, ('sta', 'grp'), perm)  9.53 us
    pallas_call x2, Pallas kernels, lags(): pl.pallas_call(functools.partial(correlate, half), out_shape=jax.ShapeDty...  7.12 us
    all_to_all x1, starting transfers between devices, body(): code = lax.all_to_all(code, 'grp', 0, 0, tiled=True)  4.92 us
    all_to_all x1, waiting for transfers between devices, body(): code = lax.all_to_all(code, 'grp', 0, 0, tiled=True)  3.68 us
  transfers between devices with their start and end apart: 10, of which 4 were waited for; matrix products, arithmetic and copies ran while one was open for 0% of the time, Pallas kernels for 5%

profile of v8, /device:TPU:8, one launch (start us, length us, event | category | flops | bytes accessed | tf_op | source)
XLA Modules:
  0.0 111.4 jit_solution(3337314529770437321)
XLA Ops:
  0.0 1.1 %copy-done = bf16[1,8,6,8192]{3,1,2,0:T(8,128)(2,1)S(1)} copy-done((bf16[1,8,6,8192]{3,1,2,0:T(8,128)(2,1)S(1)}, bf16[1,8,6,8192]{3,1,2,0:T(8,128)(2,1)}, u32[]{:S(2)}) %copy-start) | copy-done | bytes 786456
  1.1 12.7 %collective-permute-start.1 = (bf16[6,8,1024]{2,1,0:T(8,128)(2,1)S(1)}, bf16[6,8,1024]{2,1,0:T(8,128)(2,1)S(1)}, u32[]{:S(2)}, u32[]{:S(2)}) collective-permute-start(bf16[6,8,1024]{2,1,0:T(8,128)(2,1)S(1)} %dynamic-slice_bitcast_fusion), channel_id=1, source_target_pairs={{0,384},{4,132},{8,392},{12,140},{16,400},{20,148},{24,408},{28,15... | collective-permute-start | bytes 294920 | tf_op jit(solution)/shard_map/ppermute | solution.py:128
  13.9 1.9 %collective-permute-start = (bf16[6,8,1024]{2,1,0:T(8,128)(2,1)S(1)}, bf16[6,8,1024]{2,1,0:T(8,128)(2,1)S(1)}, u32[]{:S(2)}, u32[]{:S(2)}) collective-permute-start(bf16[6,8,1024]{2,1,0:T(8,128)(2,1)S(1)} %dynamic-slice_bitcast_fusion), channel_id=1, source_target_pairs={{0,128},{4,388},{8,136},{12,396},{16,144},{20,404},{24,152},{28,41... | collective-permute-start | bytes 294920 | tf_op jit(solution)/shard_map/ppermute | solution.py:128
  15.8 1.3 %codes.1 = s32[8,16]{1,0:T(8,128)} custom-call(s32[1]{0:T(128)} %bitcast.1.plane_ref, s32[1,16]{1,0:T(1,128)} %bitcast.30, s32[1,16]{1,0:T(1,128)} %bitcast.31, s32[1,16]{1,0:T(1,128)} %bitcast.32), custom_call_target="tpu_custom_call" | custom-call | flops 10000000000 | bytes 1000000 | tf_op jit(solution)/shard_map/codes/pallas_call | solution.py:138
  17.1 4.9 %all-to-all-start = ((s32[8,1,16]{2,1,0:T(1,128)}), s32[8,1,16]{2,1,0:T(1,128)S(1)}, u32[]{:S(2)}, u32[]{:S(2)}) async-start(s32[8,1,16]{2,1,0:T(1,128)} %bitcast.29), calls=%async_computation | async-start | bytes 8192 | tf_op jit(solution)/shard_map/all_to_all | solution.py:146
  22.1 3.7 %all-to-all-done = s32[8,1,16]{2,1,0:T(1,128)S(1)} async-done(((s32[8,1,16]{2,1,0:T(1,128)}), s32[8,1,16]{2,1,0:T(1,128)S(1)}, u32[]{:S(2)}, u32[]{:S(2)}) %all-to-all-start) | async-done | bytes 544 | tf_op jit(solution)/shard_map/all_to_all | solution.py:146
  25.8 7.8 %collective-permute-start.5 = (bf16[3,8,1024]{2,1,0:T(8,128)(2,1)S(1)}, bf16[3,8,1024]{2,1,0:T(8,128)(2,1)S(1)}, u32[]{:S(2)}, u32[]{:S(2)}) collective-permute-start(bf16[3,8,1024]{2,1,0:T(8,128)(2,1)S(1)} %slice.7), channel_id=1, source_target_pairs={{0,384},{4,132},{8,392},{12,140},{16,400},{20,148},{24,408},{28,15... | collective-permute-start | bytes 147464 | tf_op jit(solution)/shard_map/ppermute | solution.py:128
  33.6 1.9 %collective-permute-start.4 = (bf16[3,8,1024]{2,1,0:T(8,128)(2,1)S(1)}, bf16[3,8,1024]{2,1,0:T(8,128)(2,1)S(1)}, u32[]{:S(2)}, u32[]{:S(2)}) collective-permute-start(bf16[3,8,1024]{2,1,0:T(8,128)(2,1)S(1)} %slice.6), channel_id=1, source_target_pairs={{0,128},{4,388},{8,136},{12,396},{16,144},{20,404},{24,152},{28,41... | collective-permute-start | bytes 147464 | tf_op jit(solution)/shard_map/ppermute | solution.py:128
  35.6 6.9 %collective-permute-start.3 = (bf16[2,6,8,1024]{3,2,1,0:T(8,128)(2,1)S(1)}, bf16[2,6,8,1024]{3,2,1,0:T(8,128)(2,1)S(1)}, u32[]{:S(2)}, u32[]{:S(2)}) collective-permute-start(bf16[2,6,8,1024]{3,2,1,0:T(8,128)(2,1)S(1)} %get-tuple-element.33), channel_id=1, source_target_pairs={{0,448},{4,68},{8,456},{12,76},{16,464},{20,84},{24,472},{28,92},{... | collective-permute-start | bytes 589832 | tf_op jit(solution)/shard_map/ppermute | solution.py:128
  42.5 1.9 %collective-permute-start.2 = (bf16[2,6,8,1024]{3,2,1,0:T(8,128)(2,1)S(1)}, bf16[2,6,8,1024]{3,2,1,0:T(8,128)(2,1)S(1)}, u32[]{:S(2)}, u32[]{:S(2)}) collective-permute-start(bf16[2,6,8,1024]{3,2,1,0:T(8,128)(2,1)S(1)} %get-tuple-element.34), channel_id=1, source_target_pairs={{0,64},{4,452},{8,72},{12,460},{16,80},{20,468},{24,88},{28,476},{... | collective-permute-start | bytes 589832 | tf_op jit(solution)/shard_map/ppermute | solution.py:128
  44.6 5.6 %collective-permute-start.7 = (bf16[4,6,8,1024]{3,2,1,0:T(8,128)(2,1)S(1)}, bf16[4,6,8,1024]{3,2,1,0:T(8,128)(2,1)S(1)}, u32[]{:S(2)}, u32[]{:S(2)}) collective-permute-start(bf16[4,6,8,1024]{3,2,1,0:T(8,128)(2,1)S(1)} %pad_maximum_fusion.near_ref), channel_id=1, source_target_pairs={{0,480},{4,36},{8,488},{12,44},{16,496},{20,52},{24,504},{28,60},{... | collective-permute-start | bytes 1179656 | tf_op jit(solution)/shard_map/ppermute | solution.py:128
  50.2 1.9 %collective-permute-start.6 = (bf16[4,6,8,1024]{3,2,1,0:T(8,128)(2,1)S(1)}, bf16[4,6,8,1024]{3,2,1,0:T(8,128)(2,1)S(1)}, u32[]{:S(2)}, u32[]{:S(2)}) collective-permute-start(bf16[4,6,8,1024]{3,2,1,0:T(8,128)(2,1)S(1)} %pad_maximum_fusion.near_ref), channel_id=1, source_target_pairs={{0,32},{4,484},{8,40},{12,492},{16,48},{20,500},{24,56},{28,508},{... | collective-permute-start | bytes 1179656 | tf_op jit(solution)/shard_map/ppermute | solution.py:128
  52.1 3.8 %collective-permute-done.2.third_ref = bf16[2,6,8,1024]{3,2,1,0:T(8,128)(2,1)S(1)} collective-permute-done((bf16[2,6,8,1024]{3,2,1,0:T(8,128)(2,1)S(1)}, bf16[2,6,8,1024]{3,2,1,0:T(8,128)(2,1)S(1)}, u32[]{:S(2)}, u32[]{:S(2)}) %collective-permute-start.2) | collective-permute-done | bytes 196640 | tf_op jit(solution)/shard_map/ppermute | solution.py:128
  55.9 0.3 stage_far.1
  56.1 4.8 %collective-permute-done.7.second_ref = bf16[4,6,8,1024]{3,2,1,0:T(8,128)(2,1)S(1)} collective-permute-done((bf16[4,6,8,1024]{3,2,1,0:T(8,128)(2,1)S(1)}, bf16[4,6,8,1024]{3,2,1,0:T(8,128)(2,1)S(1)}, u32[]{:S(2)}, u32[]{:S(2)}) %collective-permute-start.7) | collective-permute-done | bytes 393248 | tf_op jit(solution)/shard_map/ppermute | solution.py:128
  60.9 0.9 collective-permute-done.6.first_ref
  61.9 2.2 %stage.1 = (bf16[2048,1024]{1,0:T(8,128)(2,1)S(1)}, bf16[6,128,1024]{2,1,0:T(8,128)(2,1)S(1)}) custom-call(s32[1]{0:T(128)} %bitcast.grp_ref, bf16[4,6,8,1024]{3,2,1,0:T(8,128)(2,1)S(1)} %pad_maximum_fusion.near_ref, bf16[4,6,8,1024]{3,2,1,0:T(8,128)(2,1)S(1)} %collective-permute-done.6.first_ref, ...), custom_call_target="tpu_custom_call" | custom-call | tf_op jit(solution)/shard_map/stage/pallas_call | solution.py:174
  64.1 3.6 %correlate.3 = bf16[4,4,9,16,256]{4,3,2,1,0:T(8,128)(2,1)S(1)} custom-call(bf16[2,128,128]{2,1,0:T(8,128)(2,1)S(1)} %get-tuple-element.26.pick, bf16[6,128,1024]{2,1,0:T(8,128)(2,1)S(1)} %get-tuple-element.30.stations, bf16[2048,1024]{1,0:T(8,128)(2,1)S(1)} %get-tuple-element.31.table), custom_call_target="tpu_custom_call" | custom-call | tf_op jit(solution)/shard_map/correlate/pallas_call | solution.py:188
  67.7 1.9 %collective-permute-start.8 = (bf16[4,4,9,16,256]{4,3,2,1,0:T(8,128)(2,1)S(1)}, bf16[4,4,9,16,256]{4,3,2,1,0:T(8,128)(2,1)S(1)}, u32[]{:S(2)}, u32[]{:S(2)}) collective-permute-start(bf16[4,4,9,16,256]{4,3,2,1,0:T(8,128)(2,1)S(1)} %correlate.3), channel_id=1, source_target_pairs={{0,4},{4,0},{8,12},{12,8},{16,20},{20,16},{24,28},{28,24},{1,5},{5... | collective-permute-start | bytes 3538952 | tf_op jit(solution)/shard_map/ppermute | solution.py:200
  69.6 3.6 %correlate.2 = f32[4,4,9,16,256]{4,3,2,1,0:T(8,128)S(1)} custom-call(bf16[2,128,128]{2,1,0:T(8,128)(2,1)S(1)} %get-tuple-element.26.pick, bf16[6,128,1024]{2,1,0:T(8,128)(2,1)S(1)} %get-tuple-element.30.stations, bf16[2048,1024]{1,0:T(8,128)(2,1)S(1)} %get-tuple-element.31.table), custom_call_target="tpu_custom_call" | custom-call | tf_op jit(solution)/shard_map/correlate/pallas_call | solution.py:188
  73.2 0.4 add_convert_fusion
  73.6 24.0 %all_to_all.17 = bf16[16,9,16,256]{3,2,1,0:T(8,128)(2,1)S(1)} all-to-all(bf16[16,9,16,256]{3,2,1,0:T(8,128)(2,1)S(1)} %bitcast.22), channel_id=1, replica_groups={{0,1,2,3,8,9,10,11,16,17,18,19,24,25,26,27},{4,5,6,7,12,13,14,15,20,21,..., dimensions={0} | all-to-all | bytes 2359296 | tf_op jit(solution)/shard_map/all_to_all | solution.py:203
  97.8 12.7 %all_gather.3 = bf16[9,16,1024]{2,1,0:T(8,128)(2,1)S(1)} all-gather(bf16[9,16,256]{2,1,0:T(8,128)(2,1)S(1)} %multiply_convert_fusion), channel_id=1, replica_groups=mesh['sta'=16,'grp'=8,'hr'=4] {'hr'}, dimensions={2}, use_global_device_ids=true | all-gather | bytes 368640 | tf_op jit(solution)/shard_map/all_gather | solution.py:205
  110.5 0.9 convert_bitcast_fusion
  (16 shorter events, 0.4 us)
Async XLA Ops:
  0.0 1.1 %copy-start = (bf16[1,8,6,8192]{3,1,2,0:T(8,128)(2,1)S(1)}, bf16[1,8,6,8192]{3,1,2,0:T(8,128)(2,1)}, u32[]{:S(2)}) copy-start(bf16[1,8,6,8192]{3,1,2,0:T(8,128)(2,1)} %param.4) | copy-start | bytes 2359300
  1.1 24.6 %collective-permute-start.1 = (bf16[6,8,1024]{2,1,0:T(8,128)(2,1)S(1)}, bf16[6,8,1024]{2,1,0:T(8,128)(2,1)S(1)}, u32[]{:S(2)}, u32[]{:S(2)}) collective-permute-start(bf16[6,8,1024]{2,1,0:T(8,128)(2,1)S(1)} %dynamic-slice_bitcast_fusion), channel_id=1, source_target_pairs={{0,384},{4,132},{8,392},{12,140},{16,400},{20,148},{24,408},{28,15... | collective-permute-start | bytes 294920 | tf_op jit(solution)/shard_map/ppermute | solution.py:128
  13.9 11.9 %collective-permute-start = (bf16[6,8,1024]{2,1,0:T(8,128)(2,1)S(1)}, bf16[6,8,1024]{2,1,0:T(8,128)(2,1)S(1)}, u32[]{:S(2)}, u32[]{:S(2)}) collective-permute-start(bf16[6,8,1024]{2,1,0:T(8,128)(2,1)S(1)} %dynamic-slice_bitcast_fusion), channel_id=1, source_target_pairs={{0,128},{4,388},{8,136},{12,396},{16,144},{20,404},{24,152},{28,41... | collective-permute-start | bytes 294920 | tf_op jit(solution)/shard_map/ppermute | solution.py:128
  17.1 8.6 %all-to-all-start = ((s32[8,1,16]{2,1,0:T(1,128)}), s32[8,1,16]{2,1,0:T(1,128)S(1)}, u32[]{:S(2)}, u32[]{:S(2)}) async-start(s32[8,1,16]{2,1,0:T(1,128)} %bitcast.29), calls=%async_computation | async-start | bytes 8192 | tf_op jit(solution)/shard_map/all_to_all | solution.py:146
  25.8 18.7 %collective-permute-start.5 = (bf16[3,8,1024]{2,1,0:T(8,128)(2,1)S(1)}, bf16[3,8,1024]{2,1,0:T(8,128)(2,1)S(1)}, u32[]{:S(2)}, u32[]{:S(2)}) collective-permute-start(bf16[3,8,1024]{2,1,0:T(8,128)(2,1)S(1)} %slice.7), channel_id=1, source_target_pairs={{0,384},{4,132},{8,392},{12,140},{16,400},{20,148},{24,408},{28,15... | collective-permute-start | bytes 147464 | tf_op jit(solution)/shard_map/ppermute | solution.py:128
  33.6 10.9 %collective-permute-start.4 = (bf16[3,8,1024]{2,1,0:T(8,128)(2,1)S(1)}, bf16[3,8,1024]{2,1,0:T(8,128)(2,1)S(1)}, u32[]{:S(2)}, u32[]{:S(2)}) collective-permute-start(bf16[3,8,1024]{2,1,0:T(8,128)(2,1)S(1)} %slice.6), channel_id=1, source_target_pairs={{0,128},{4,388},{8,136},{12,396},{16,144},{20,404},{24,152},{28,41... | collective-permute-start | bytes 147464 | tf_op jit(solution)/shard_map/ppermute | solution.py:128
  35.6 16.5 %collective-permute-start.3 = (bf16[2,6,8,1024]{3,2,1,0:T(8,128)(2,1)S(1)}, bf16[2,6,8,1024]{3,2,1,0:T(8,128)(2,1)S(1)}, u32[]{:S(2)}, u32[]{:S(2)}) collective-permute-start(bf16[2,6,8,1024]{3,2,1,0:T(8,128)(2,1)S(1)} %get-tuple-element.33), channel_id=1, source_target_pairs={{0,448},{4,68},{8,456},{12,76},{16,464},{20,84},{24,472},{28,92},{... | collective-permute-start | bytes 589832 | tf_op jit(solution)/shard_map/ppermute | solution.py:128
  42.5 13.3 %collective-permute-start.2 = (bf16[2,6,8,1024]{3,2,1,0:T(8,128)(2,1)S(1)}, bf16[2,6,8,1024]{3,2,1,0:T(8,128)(2,1)S(1)}, u32[]{:S(2)}, u32[]{:S(2)}) collective-permute-start(bf16[2,6,8,1024]{3,2,1,0:T(8,128)(2,1)S(1)} %get-tuple-element.34), channel_id=1, source_target_pairs={{0,64},{4,452},{8,72},{12,460},{16,80},{20,468},{24,88},{28,476},{... | collective-permute-start | bytes 589832 | tf_op jit(solution)/shard_map/ppermute | solution.py:128
  44.6 16.4 %collective-permute-start.7 = (bf16[4,6,8,1024]{3,2,1,0:T(8,128)(2,1)S(1)}, bf16[4,6,8,1024]{3,2,1,0:T(8,128)(2,1)S(1)}, u32[]{:S(2)}, u32[]{:S(2)}) collective-permute-start(bf16[4,6,8,1024]{3,2,1,0:T(8,128)(2,1)S(1)} %pad_maximum_fusion.near_ref), channel_id=1, source_target_pairs={{0,480},{4,36},{8,488},{12,44},{16,496},{20,52},{24,504},{28,60},{... | collective-permute-start | bytes 1179656 | tf_op jit(solution)/shard_map/ppermute | solution.py:128
  50.2 11.7 %collective-permute-start.6 = (bf16[4,6,8,1024]{3,2,1,0:T(8,128)(2,1)S(1)}, bf16[4,6,8,1024]{3,2,1,0:T(8,128)(2,1)S(1)}, u32[]{:S(2)}, u32[]{:S(2)}) collective-permute-start(bf16[4,6,8,1024]{3,2,1,0:T(8,128)(2,1)S(1)} %pad_maximum_fusion.near_ref), channel_id=1, source_target_pairs={{0,32},{4,484},{8,40},{12,492},{16,48},{20,500},{24,56},{28,508},{... | collective-permute-start | bytes 1179656 | tf_op jit(solution)/shard_map/ppermute | solution.py:128
  67.7 5.5 %collective-permute-start.8 = (bf16[4,4,9,16,256]{4,3,2,1,0:T(8,128)(2,1)S(1)}, bf16[4,4,9,16,256]{4,3,2,1,0:T(8,128)(2,1)S(1)}, u32[]{:S(2)}, u32[]{:S(2)}) collective-permute-start(bf16[4,4,9,16,256]{4,3,2,1,0:T(8,128)(2,1)S(1)} %correlate.3), channel_id=1, source_target_pairs={{0,4},{4,0},{8,12},{12,8},{16,20},{20,16},{24,28},{28,24},{1,5},{5... | collective-permute-start | bytes 3538952 | tf_op jit(solution)/shard_map/ppermute | solution.py:200

commit v9 on v6

--- a/solution.py
+++ b/solution.py
@@ -17,6 +17,8 @@
 FINE = 32
 HALF = NY * PD
 CH = 128
+TN = LAGS // 2
+TA = TN + CH
 TW = LAGS // NX
 TWO_PI = 2.0 * math.pi
 VMEM_LIMIT = 24 * 1024 * 1024
@@ -31,16 +33,16 @@
     out_ref[...] = jnp.broadcast_to(code, (NG, PD))
 
 
-def stage(grp_ref, code_ref, near_ref, first_ref, second_ref, third_ref, fourth_ref, table, stations, pick, row, hi_c, hi_s):
+def stage(grp_ref, code_ref, near_ref, first_ref, second_ref, third_ref, fourth_ref, table, edge, stations, pick, row, hi_c, hi_s):
     core, g = grp_ref[0] % NC, grp_ref[0]
-    bit = lax.broadcasted_iota(jnp.int32, (16, LAGS), 0)
-    lag = lax.broadcasted_iota(jnp.int32, (16, LAGS), 1) - LAGS // 2
+    bit = lax.broadcasted_iota(jnp.int32, (16, TA), 0)
+    lag = jnp.minimum(lax.broadcasted_iota(jnp.int32, (16, TA), 1), TN)
     bins = jnp.where(bit < BITS, jnp.left_shift(1, bit), g * W)
     ang = ((bins * lag) & (2 * NB - 1)).astype(jnp.float32) * (TWO_PI / (2 * NB))
     cos, sin = jnp.cos(ang), jnp.sin(ang)
 
     def turned(c, s, bits):
-        at = lax.broadcasted_iota(jnp.int32, (FINE, LAGS), 0)
+        at = lax.broadcasted_iota(jnp.int32, (FINE, TA), 0)
         for k, b in enumerate(bits):
             on = (jnp.right_shift(at, k) & 1) == 1
             kc, ks = jnp.where(on, cos[b : b + 1], 1.0), jnp.where(on, sin[b : b + 1], 0.0)
@@ -48,15 +50,20 @@
         return c, s
 
     half_bits = BITS // 2
-    lc, ls = turned(jnp.ones((FINE, LAGS), jnp.float32), jnp.zeros((FINE, LAGS), jnp.float32), range(half_bits))
-    base = jnp.broadcast_to(cos[BITS : BITS + 1], (FINE, LAGS)), jnp.broadcast_to(sin[BITS : BITS + 1], (FINE, LAGS))
+    lc, ls = turned(jnp.ones((FINE, TA), jnp.float32), jnp.zeros((FINE, TA), jnp.float32), range(half_bits))
+    base = jnp.broadcast_to(cos[BITS : BITS + 1], (FINE, TA)), jnp.broadcast_to(sin[BITS : BITS + 1], (FINE, TA))
     hi_c[...], hi_s[...] = turned(*base, range(half_bits, BITS))
+
+    zero = lax.broadcasted_iota(jnp.int32, (FINE, CH), 1) == 0
 
     def fill(i, carry):
         hc, hs = hi_c[pl.ds(i, 1), :], hi_s[pl.ds(i, 1), :]
         at = pl.multiple_of(i * FINE, FINE)
-        table[pl.ds(at, FINE), :] = (hc * lc - hs * ls).astype(jnp.bfloat16)
-        table[pl.ds(W + at, FINE), :] = (-(hs * lc + hc * ls)).astype(jnp.bfloat16)
+        c, s = hc * lc - hs * ls, hs * lc + hc * ls
+        table[pl.ds(at, FINE), :] = c[:, :TN].astype(jnp.bfloat16)
+        table[pl.ds(W + at, FINE), :] = (-s[:, :TN]).astype(jnp.bfloat16)
+        table[pl.ds(W + at, FINE), 0:CH] = jnp.where(zero, s[:, TN:], -s[:, :CH]).astype(jnp.bfloat16)
+        edge[pl.ds(at, FINE), :] = jnp.where(zero, c[:, TN:], 0.0).astype(jnp.bfloat16)
         return carry
 
     lax.fori_loop(0, W // FINE, fill, 0)
@@ -80,7 +87,7 @@
             stations[comp, pl.ds(at, x.shape[0]), :] = x
 
 
-def correlate(half, pick, stations, table, out_ref, cross):
+def correlate(half, pick, stations, table, edge, out_ref, cross):
     for k in range(W // CH):
         at = k * CH
         r, s = [], []
@@ -97,11 +104,30 @@
                 cross[r0 : r0 + HALF, W + at : W + at + CH] = im.astype(jnp.bfloat16)
 
     for n in range(NX):
-        out = jnp.dot(cross[...], table[:, n * TW : (n + 1) * TW], preferred_element_type=jnp.float32)
+        odd, at = n // 2 * W, n % 2 * TW
+        part = cross[:, odd : odd + W]
+        out = jnp.dot(part, table[odd : odd + W, at : at + TW], preferred_element_type=jnp.float32)
+        if n == 2:
+            low = out[:, :CH] + jnp.dot(cross[:, :W], edge[...], preferred_element_type=jnp.float32)
+            out = jnp.concatenate([low, out[:, CH:]], axis=1)
         for c in range(9):
             for k in range(NY):
                 r0 = c * HALF + k * PD
                 out_ref[k, n, c] = out[r0 : r0 + PD].astype(out_ref.dtype)
+
+
+def unfold(scale_ref, x_ref, out_ref):
+    x = x_ref[...].reshape(9 * PD, LAGS)
+    even, odd = x[:, :TN], x[:, TN:]
+    turn = lax.broadcasted_iota(jnp.int32, (TN, TN), 0) + lax.broadcasted_iota(jnp.int32, (TN, TN), 1) == TN
+    turn = turn.astype(jnp.float32).astype(jnp.bfloat16)
+    back = jnp.dot(even, turn, preferred_element_type=jnp.float32) - jnp.dot(odd, turn, preferred_element_type=jnp.float32)
+    even, odd = even.astype(jnp.float32), odd.astype(jnp.float32)
+    zero = lax.broadcasted_iota(jnp.int32, (9 * PD, TN), 1) == 0
+    back = jnp.where(zero, odd, back) * scale_ref[:, :TN]
+    ahead = jnp.where(zero, even, even + odd) * scale_ref[:, TN:]
+    out_ref[:, :, :TN] = back.reshape(9, PD, TN)
+    out_ref[:, :, TN:] = ahead.reshape(9, PD, TN)
 
 
 def vmem(n):
@@ -119,8 +145,8 @@
         perm = [(z * NG + i, (z + turn[i]) % NZ * NG + i) for z in range(NZ) for i in range(NG)]
         return lax.ppermute(x, ("sta", "grp"), perm)
 
-    pos = lax.axis_index("hr") * TW + jnp.arange(TW, dtype=jnp.int32)
-    taper = 0.75 - 0.25 * jnp.cos(TWO_PI * (pos.astype(jnp.float32) + 0.5) / LAGS)
+    pos = jnp.arange(LAGS, dtype=jnp.float32)[None]
+    taper = 0.75 - 0.25 * jnp.cos(TWO_PI * (pos + 0.5) / LAGS)
     scale = taper / (NX * math.sqrt(NB))
     half = NZ // NR // 2
     low, high, pair_row = lax.optimization_barrier((near[:half], near[half:], pair_row))
@@ -139,19 +165,20 @@
     code, moved, scale = lax.optimization_barrier((code, moved, scale))
 
     params = pltpu.CompilerParams(vmem_limit_bytes=VMEM_LIMIT)
-    table, stations, pick = pl.pallas_call(
+    table, edge, stations, pick = pl.pallas_call(
         stage,
         out_shape=(
-            jax.ShapeDtypeStruct((2 * W, LAGS), jnp.bfloat16),
+            jax.ShapeDtypeStruct((2 * W, TN), jnp.bfloat16),
+            jax.ShapeDtypeStruct((W, CH), jnp.bfloat16),
             jax.ShapeDtypeStruct((6, NZ * SD, W), jnp.bfloat16),
             jax.ShapeDtypeStruct((NC, 2 * HALF, NZ * SD), jnp.bfloat16),
         ),
         in_specs=[smem] + vmem(6),
-        out_specs=tuple(vmem(3)),
+        out_specs=tuple(vmem(4)),
         scratch_shapes=[
             pltpu.VMEM((8, NC * 2 * HALF), jnp.int32),
-            pltpu.VMEM((FINE, LAGS), jnp.float32),
-            pltpu.VMEM((FINE, LAGS), jnp.float32),
+            pltpu.VMEM((FINE, TA), jnp.float32),
+            pltpu.VMEM((FINE, TA), jnp.float32),
         ],
         compiler_params=params,
         name="stage",
@@ -161,12 +188,12 @@
         return pl.pallas_call(
             functools.partial(correlate, half),
             out_shape=jax.ShapeDtypeStruct((NY, NX, 9, PD, TW), dtype),
-            in_specs=vmem(3),
+            in_specs=vmem(4),
             out_specs=vmem(1)[0],
             scratch_shapes=[pltpu.VMEM((9 * HALF, 2 * W), jnp.bfloat16)],
             compiler_params=params,
             name="correlate",
-        )(pick, stations, table)
+        )(pick, stations, table, edge)
 
     send = lags(0, jnp.bfloat16)
     keep = lags(1, jnp.float32)
@@ -174,9 +201,16 @@
     part = part.astype(jnp.bfloat16).reshape(NY * NX, 9, PD, TW)
     chips = [[(NC * y + c) * NX + x for y in range(NY) for x in range(NX)] for c in range(NC)]
     part = lax.all_to_all(part, ("grp", "hr"), 0, 0, axis_index_groups=chips, tiled=True)
-    total = jnp.sum(part.astype(jnp.float32), axis=0)
-    total = lax.all_gather((total * scale).astype(jnp.bfloat16), "hr", axis=2, tiled=True)
-    return total.astype(jnp.float32).transpose(1, 0, 2)
+    total = jnp.sum(part.astype(jnp.float32), axis=0).astype(jnp.bfloat16)
+    total = lax.all_gather(total, "hr", axis=2, tiled=True)
+    return pl.pallas_call(
+        unfold,
+        out_shape=jax.ShapeDtypeStruct((9, PD, LAGS), jnp.float32),
+        in_specs=vmem(2),
+        out_specs=vmem(1)[0],
+        compiler_params=params,
+        name="unfold",
+    )(scale, total).transpose(1, 0, 2)
 
 
 def solution(mesh):

time: 106 us -> 105 us (level)
    pallas_call x2, Pallas kernels: 7.1 us -> 5.79 us  [lags(): pl.pallas_call(functools.partial(correlate, half), out_shape=jax.ShapeDty...]
    pallas_call x1 -> x2, Pallas kernels: 2.35 us -> 2.76 us  [the longest x1 1.64 us: body(): pl.pallas_call(stage, out_shape=(jax.ShapeDtypeStruct((2 * W, TN), jnp.bf...]
  transfers between devices with their start and end apart: 6 -> 6, of which waited for: 1 -> 1; matrix products, arithmetic and copies ran while one was open for 0% -> 0% of each run, Pallas kernels for 5% -> 4%
where the time goes in v9:
time: 105 us; the launch traced here: 104 us
  blocking collectives  66.9 us (64%)
  starting transfers between devices  21.8 us (21%)
  Pallas kernels  9.84 us (9%)
  waiting for transfers between devices  3.61 us (3%)
  local copies, waits for them, and re-layouts  1.17 us (1%)
    all_gather x1, blocking collectives, body(): near = lax.all_gather(mine, 'sta', axis=0, axis_index_groups=planes)  30.5 us
    all_to_all x1, blocking collectives, body(): lax.all_to_all(part, ('grp', 'hr'), 0, 0, axis_index_groups=chips, tiled=...  23.7 us
    ppermute x4, starting transfers between devices, neighbour(): return lax.ppermute(x, ('sta', 'grp'), perm)  15 us
    all_gather x1, blocking collectives, body(): total = lax.all_gather(total, 'hr', axis=2, tiled=True)  12.7 us
    pallas_call x2, Pallas kernels, lags(): pl.pallas_call(functools.partial(correlate, half), out_shape=jax.ShapeDty...  5.79 us
    all_to_all x1, starting transfers between devices, body(): code = lax.all_to_all(code, 'grp', 0, 0, tiled=True)  4.92 us
    all_to_all x1, waiting for transfers between devices, body(): code = lax.all_to_all(code, 'grp', 0, 0, tiled=True)  3.59 us
  transfers between devices with their start and end apart: 6, of which 1 were waited for; matrix products, arithmetic and copies ran while one was open for 0% of the time, Pallas kernels for 4%

profile of v9, /device:TPU:8, one launch (start us, length us, event | category | flops | bytes accessed | tf_op | source)
XLA Modules:
  0.0 104.2 jit_solution(11778911421527081163)
XLA Ops:
  0.0 1.1 %copy-done = bf16[1,8,6,8192]{3,1,2,0:T(8,128)(2,1)S(1)} copy-done((bf16[1,8,6,8192]{3,1,2,0:T(8,128)(2,1)S(1)}, bf16[1,8,6,8192]{3,1,2,0:T(8,128)(2,1)}, u32[]{:S(2)}) %copy-start) | copy-done | bytes 786456
  1.1 30.5 %all-gather = bf16[24,8,1024]{2,1,0:T(8,128)(2,1)S(1)} all-gather(bf16[6,8,1024]{2,1,0:T(8,128)(2,1)S(1)} %dynamic-slice_bitcast_fusion), channel_id=2, replica_groups={{0,128,256,384},{32,160,288,416},{64,192,320,448},{96,224,352,480},{1,1..., dimensions={0}, use_global_device_ids=true | all-gather | bytes 491520 | tf_op jit(solution)/shard_map/all_gather | solution.py:141
  31.6 2.5 %collective-permute-start = (bf16[4,6,8,1024]{3,2,1,0:T(8,128)(2,1)S(1)}, bf16[4,6,8,1024]{3,2,1,0:T(8,128)(2,1)S(1)}, u32[]{:S(2)}, u32[]{:S(2)}) collective-permute-start(bf16[4,6,8,1024]{3,2,1,0:T(8,128)(2,1)S(1)} %bitcast.18), channel_id=1, source_target_pairs={{0,32},{4,484},{8,40},{12,492},{16,48},{20,500},{24,56},{28,508},{... | collective-permute-start | bytes 1179656 | tf_op jit(solution)/shard_map/ppermute | solution.py:146
  34.2 4.5 %collective-permute-start.1 = (bf16[4,6,8,1024]{3,2,1,0:T(8,128)(2,1)S(1)}, bf16[4,6,8,1024]{3,2,1,0:T(8,128)(2,1)S(1)}, u32[]{:S(2)}, u32[]{:S(2)}) collective-permute-start(bf16[4,6,8,1024]{3,2,1,0:T(8,128)(2,1)S(1)} %bitcast.19), channel_id=1, source_target_pairs={{0,480},{4,36},{8,488},{12,44},{16,496},{20,52},{24,504},{28,60},{... | collective-permute-start | bytes 1179656 | tf_op jit(solution)/shard_map/ppermute | solution.py:146
  38.7 1.9 %collective-permute-start.2 = (bf16[2,6,8,1024]{3,2,1,0:T(8,128)(2,1)S(1)}, bf16[2,6,8,1024]{3,2,1,0:T(8,128)(2,1)S(1)}, u32[]{:S(2)}, u32[]{:S(2)}) collective-permute-start(bf16[2,6,8,1024]{3,2,1,0:T(8,128)(2,1)S(1)} %bitcast.24), channel_id=1, source_target_pairs={{0,64},{4,452},{8,72},{12,460},{16,80},{20,468},{24,88},{28,476},{... | collective-permute-start | bytes 589832 | tf_op jit(solution)/shard_map/ppermute | solution.py:146
  40.7 6.0 %collective-permute-start.3 = (bf16[2,6,8,1024]{3,2,1,0:T(8,128)(2,1)S(1)}, bf16[2,6,8,1024]{3,2,1,0:T(8,128)(2,1)S(1)}, u32[]{:S(2)}, u32[]{:S(2)}) collective-permute-start(bf16[2,6,8,1024]{3,2,1,0:T(8,128)(2,1)S(1)} %bitcast.23), channel_id=1, source_target_pairs={{0,448},{4,68},{8,456},{12,76},{16,464},{20,84},{24,472},{28,92},{... | collective-permute-start | bytes 589832 | tf_op jit(solution)/shard_map/ppermute | solution.py:146
  46.7 1.3 %codes.1 = s32[8,16]{1,0:T(8,128)} custom-call(s32[1]{0:T(128)} %bitcast.plane_ref, s32[1,16]{1,0:T(1,128)} %bitcast.26, s32[1,16]{1,0:T(1,128)} %bitcast.27, s32[1,16]{1,0:T(1,128)} %bitcast.28), custom_call_target="tpu_custom_call" | custom-call | flops 10000000000 | bytes 1000000 | tf_op jit(solution)/shard_map/codes/pallas_call | solution.py:156
  48.0 4.9 %all-to-all-start = ((s32[8,1,16]{2,1,0:T(1,128)}), s32[8,1,16]{2,1,0:T(1,128)S(1)}, u32[]{:S(2)}, u32[]{:S(2)}) async-start(s32[8,1,16]{2,1,0:T(1,128)} %bitcast.25), calls=%async_computation | async-start | bytes 8192 | tf_op jit(solution)/shard_map/all_to_all | solution.py:164
  52.9 0.1 subtract_multiply_fusion.scale_ref
  53.1 3.6 %all-to-all-done = s32[8,1,16]{2,1,0:T(1,128)S(1)} async-done(((s32[8,1,16]{2,1,0:T(1,128)}), s32[8,1,16]{2,1,0:T(1,128)S(1)}, u32[]{:S(2)}, u32[]{:S(2)}) %all-to-all-start) | async-done | bytes 544 | tf_op jit(solution)/shard_map/all_to_all | solution.py:164
  56.7 0.0 collective-permute-done.2.third_ref
  56.7 0.0 collective-permute-done.3.fourth_ref
  56.7 0.0 collective-permute-done.first_ref
  56.7 0.0 collective-permute-done.1.second_ref
  56.7 1.6 %stage.1 = (bf16[2048,512]{1,0:T(8,128)(2,1)S(1)}, bf16[1024,128]{1,0:T(8,128)(2,1)S(1)}, bf16[6,128,1024]{2,1,0:T(8,128)(2,1)S(1)}, bf16[2,128,128]{2,1,0:T(8,128)(2,1)S(1)}) custom-call(s32[1]{0:T(128)} %bitcast.12.grp_ref, s32[8,16]{1,0:T(8,128)S(1)} %bitcast.21, bf16[4,6,8,1024]{3,2,1,0:T(8,128)(2,1)S(1)} %bitcast.20, ...), custom_call_target="tpu_custom_call" | custom-call | tf_op jit(solution)/shard_map/stage/pallas_call | solution.py:168
  58.3 2.9 %correlate.3 = bf16[4,4,9,16,256]{4,3,2,1,0:T(8,128)(2,1)S(1)} custom-call(bf16[2,128,128]{2,1,0:T(8,128)(2,1)S(1)} %get-tuple-element.27.pick, bf16[6,128,1024]{2,1,0:T(8,128)(2,1)S(1)} %get-tuple-element.28.stations, bf16[2048,512]{1,0:T(8,128)(2,1)S(1)} %get-tuple-element.29.table, bf16[1024,128]{1,0:T(8,128)(2,1)S(1)} %get-tuple-element.30.edge), custom_call_target="tpu_custom_call" | custom-call | tf_op jit(solution)/shard_map/correlate/pallas_call | solution.py:188
  61.2 1.9 %collective-permute-start.4 = (bf16[4,4,9,16,256]{4,3,2,1,0:T(8,128)(2,1)S(1)}, bf16[4,4,9,16,256]{4,3,2,1,0:T(8,128)(2,1)S(1)}, u32[]{:S(2)}, u32[]{:S(2)}) collective-permute-start(bf16[4,4,9,16,256]{4,3,2,1,0:T(8,128)(2,1)S(1)} %correlate.3), channel_id=1, source_target_pairs={{0,4},{4,0},{8,12},{12,8},{16,20},{20,16},{24,28},{28,24},{1,5},{5... | collective-permute-start | bytes 3538952 | tf_op jit(solution)/shard_map/ppermute | solution.py:200
  63.2 2.9 %correlate.2 = f32[4,4,9,16,256]{4,3,2,1,0:T(8,128)S(1)} custom-call(bf16[2,128,128]{2,1,0:T(8,128)(2,1)S(1)} %get-tuple-element.27.pick, bf16[6,128,1024]{2,1,0:T(8,128)(2,1)S(1)} %get-tuple-element.28.stations, bf16[2048,512]{1,0:T(8,128)(2,1)S(1)} %get-tuple-element.29.table, bf16[1024,128]{1,0:T(8,128)(2,1)S(1)} %get-tuple-element.30.edge), custom_call_target="tpu_custom_call" | custom-call | tf_op jit(solution)/shard_map/correlate/pallas_call | solution.py:188
  66.1 0.0 collective-permute-done.4
  66.1 0.4 add_convert_fusion
  66.5 23.7 %all_to_all.17 = bf16[16,9,16,256]{3,2,1,0:T(8,128)(2,1)S(1)} all-to-all(bf16[16,9,16,256]{3,2,1,0:T(8,128)(2,1)S(1)} %bitcast.22), channel_id=1, replica_groups={{0,1,2,3,8,9,10,11,16,17,18,19,24,25,26,27},{4,5,6,7,12,13,14,15,20,21,..., dimensions={0} | all-to-all | bytes 2359296 | tf_op jit(solution)/shard_map/all_to_all | solution.py:203
  90.2 0.2 reduce_sum.12
  90.4 12.7 %all_gather.11.x_ref = bf16[9,16,1024]{2,1,0:T(8,128)(2,1)S(1)} all-gather(bf16[9,16,256]{2,1,0:T(8,128)(2,1)S(1)} %reduce_sum.12), channel_id=1, replica_groups=mesh['sta'=16,'grp'=8,'hr'=4] {'hr'}, dimensions={2}, use_global_device_ids=true | all-gather | bytes 368640 | tf_op jit(solution)/shard_map/all_gather | solution.py:205
  103.1 1.1 %unfold.1 = f32[9,16,1024]{2,1,0:T(8,128)} custom-call(f32[1,1024]{1,0:T(1,128)S(1)} %subtract_multiply_fusion.scale_ref, bf16[9,16,1024]{2,1,0:T(8,128)(2,1)S(1)} %all_gather.11.x_ref), custom_call_target="tpu_custom_call" | custom-call | tf_op jit(solution)/shard_map/unfold/pallas_call | solution.py:206
  (3 shorter events, 0.0 us)
Async XLA Ops:
  0.0 1.1 %copy-start = (bf16[1,8,6,8192]{3,1,2,0:T(8,128)(2,1)S(1)}, bf16[1,8,6,8192]{3,1,2,0:T(8,128)(2,1)}, u32[]{:S(2)}) copy-start(bf16[1,8,6,8192]{3,1,2,0:T(8,128)(2,1)} %param.4) | copy-start | bytes 2359300
  31.6 25.0 %collective-permute-start = (bf16[4,6,8,1024]{3,2,1,0:T(8,128)(2,1)S(1)}, bf16[4,6,8,1024]{3,2,1,0:T(8,128)(2,1)S(1)}, u32[]{:S(2)}, u32[]{:S(2)}) collective-permute-start(bf16[4,6,8,1024]{3,2,1,0:T(8,128)(2,1)S(1)} %bitcast.18), channel_id=1, source_target_pairs={{0,32},{4,484},{8,40},{12,492},{16,48},{20,500},{24,56},{28,508},{... | collective-permute-start | bytes 1179656 | tf_op jit(solution)/shard_map/ppermute | solution.py:146
  34.2 22.5 %collective-permute-start.1 = (bf16[4,6,8,1024]{3,2,1,0:T(8,128)(2,1)S(1)}, bf16[4,6,8,1024]{3,2,1,0:T(8,128)(2,1)S(1)}, u32[]{:S(2)}, u32[]{:S(2)}) collective-permute-start(bf16[4,6,8,1024]{3,2,1,0:T(8,128)(2,1)S(1)} %bitcast.19), channel_id=1, source_target_pairs={{0,480},{4,36},{8,488},{12,44},{16,496},{20,52},{24,504},{28,60},{... | collective-permute-start | bytes 1179656 | tf_op jit(solution)/shard_map/ppermute | solution.py:146
  38.7 17.9 %collective-permute-start.2 = (bf16[2,6,8,1024]{3,2,1,0:T(8,128)(2,1)S(1)}, bf16[2,6,8,1024]{3,2,1,0:T(8,128)(2,1)S(1)}, u32[]{:S(2)}, u32[]{:S(2)}) collective-permute-start(bf16[2,6,8,1024]{3,2,1,0:T(8,128)(2,1)S(1)} %bitcast.24), channel_id=1, source_target_pairs={{0,64},{4,452},{8,72},{12,460},{16,80},{20,468},{24,88},{28,476},{... | collective-permute-start | bytes 589832 | tf_op jit(solution)/shard_map/ppermute | solution.py:146
  40.7 16.0 %collective-permute-start.3 = (bf16[2,6,8,1024]{3,2,1,0:T(8,128)(2,1)S(1)}, bf16[2,6,8,1024]{3,2,1,0:T(8,128)(2,1)S(1)}, u32[]{:S(2)}, u32[]{:S(2)}) collective-permute-start(bf16[2,6,8,1024]{3,2,1,0:T(8,128)(2,1)S(1)} %bitcast.23), channel_id=1, source_target_pairs={{0,448},{4,68},{8,456},{12,76},{16,464},{20,84},{24,472},{28,92},{... | collective-permute-start | bytes 589832 | tf_op jit(solution)/shard_map/ppermute | solution.py:146
  48.0 8.6 %all-to-all-start = ((s32[8,1,16]{2,1,0:T(1,128)}), s32[8,1,16]{2,1,0:T(1,128)S(1)}, u32[]{:S(2)}, u32[]{:S(2)}) async-start(s32[8,1,16]{2,1,0:T(1,128)} %bitcast.25), calls=%async_computation | async-start | bytes 8192 | tf_op jit(solution)/shard_map/all_to_all | solution.py:164
  61.2 4.8 %collective-permute-start.4 = (bf16[4,4,9,16,256]{4,3,2,1,0:T(8,128)(2,1)S(1)}, bf16[4,4,9,16,256]{4,3,2,1,0:T(8,128)(2,1)S(1)}, u32[]{:S(2)}, u32[]{:S(2)}) collective-permute-start(bf16[4,4,9,16,256]{4,3,2,1,0:T(8,128)(2,1)S(1)} %correlate.3), channel_id=1, source_target_pairs={{0,4},{4,0},{8,12},{12,8},{16,20},{20,16},{24,28},{28,24},{1,5},{5... | collective-permute-start | bytes 3538952 | tf_op jit(solution)/shard_map/ppermute | solution.py:200

commit v10 on v9

--- a/solution.py
+++ b/solution.py
@@ -33,42 +33,8 @@
     out_ref[...] = jnp.broadcast_to(code, (NG, PD))
 
 
-def stage(grp_ref, code_ref, near_ref, first_ref, second_ref, third_ref, fourth_ref, table, edge, stations, pick, row, hi_c, hi_s):
-    core, g = grp_ref[0] % NC, grp_ref[0]
-    bit = lax.broadcasted_iota(jnp.int32, (16, TA), 0)
-    lag = jnp.minimum(lax.broadcasted_iota(jnp.int32, (16, TA), 1), TN)
-    bins = jnp.where(bit < BITS, jnp.left_shift(1, bit), g * W)
-    ang = ((bins * lag) & (2 * NB - 1)).astype(jnp.float32) * (TWO_PI / (2 * NB))
-    cos, sin = jnp.cos(ang), jnp.sin(ang)
-
-    def turned(c, s, bits):
-        at = lax.broadcasted_iota(jnp.int32, (FINE, TA), 0)
-        for k, b in enumerate(bits):
-            on = (jnp.right_shift(at, k) & 1) == 1
-            kc, ks = jnp.where(on, cos[b : b + 1], 1.0), jnp.where(on, sin[b : b + 1], 0.0)
-            c, s = c * kc - s * ks, s * kc + c * ks
-        return c, s
-
-    half_bits = BITS // 2
-    lc, ls = turned(jnp.ones((FINE, TA), jnp.float32), jnp.zeros((FINE, TA), jnp.float32), range(half_bits))
-    base = jnp.broadcast_to(cos[BITS : BITS + 1], (FINE, TA)), jnp.broadcast_to(sin[BITS : BITS + 1], (FINE, TA))
-    hi_c[...], hi_s[...] = turned(*base, range(half_bits, BITS))
-
-    zero = lax.broadcasted_iota(jnp.int32, (FINE, CH), 1) == 0
-
-    def fill(i, carry):
-        hc, hs = hi_c[pl.ds(i, 1), :], hi_s[pl.ds(i, 1), :]
-        at = pl.multiple_of(i * FINE, FINE)
-        c, s = hc * lc - hs * ls, hs * lc + hc * ls
-        table[pl.ds(at, FINE), :] = c[:, :TN].astype(jnp.bfloat16)
-        table[pl.ds(W + at, FINE), :] = (-s[:, :TN]).astype(jnp.bfloat16)
-        table[pl.ds(W + at, FINE), 0:CH] = jnp.where(zero, s[:, TN:], -s[:, :CH]).astype(jnp.bfloat16)
-        edge[pl.ds(at, FINE), :] = jnp.where(zero, c[:, TN:], 0.0).astype(jnp.bfloat16)
-        return carry
-
-    lax.fori_loop(0, W // FINE, fill, 0)
-
-    even = core == 0
+def one_hots(grp_ref, code_ref, pick, row):
+    even = grp_ref[0] % NC == 0
     for k in range(NY):
         c0, c1 = code_ref[NC * k : NC * k + 1], code_ref[NC * k + 1 : NC * k + 2]
         for half, code in enumerate((jnp.where(even, c1, c0), jnp.where(even, c0, c1))):
@@ -79,6 +45,43 @@
     for half in range(NC):
         hot = (station == row[0:1, half * 2 * HALF : (half + 1) * 2 * HALF]).astype(jnp.float32)
         pick[half] = hot.T.astype(jnp.bfloat16)
+
+
+def stage(grp_ref, near_ref, first_ref, second_ref, third_ref, fourth_ref, table, edge, stations, hi_c, hi_s):
+    core, g = grp_ref[0] % NC, grp_ref[0]
+    bit = lax.broadcasted_iota(jnp.int32, (16, TA), 0)
+    lag = jnp.minimum(lax.broadcasted_iota(jnp.int32, (16, TA), 1), TN)
+    bins = jnp.where(bit < BITS, jnp.left_shift(1, bit), g * W)
+    ang = ((bins * lag) & (2 * NB - 1)).astype(jnp.float32) * (TWO_PI / (2 * NB))
+    cos, sin = jnp.cos(ang), jnp.sin(ang)
+
+    def turned(c, s, bits):
+        at = lax.broadcasted_iota(jnp.int32, (FINE, TA), 0)
+        for k, b in enumerate(bits):
+            on = (jnp.right_shift(at, k) & 1) == 1
+            kc, ks = jnp.where(on, cos[b : b + 1], 1.0), jnp.where(on, sin[b : b + 1], 0.0)
+            c, s = c * kc - s * ks, s * kc + c * ks
+        return c, s
+
+    half_bits = BITS // 2
+    lc, ls = turned(jnp.ones((FINE, TA), jnp.float32), jnp.zeros((FINE, TA), jnp.float32), range(half_bits))
+    base = jnp.broadcast_to(cos[BITS : BITS + 1], (FINE, TA)), jnp.broadcast_to(sin[BITS : BITS + 1], (FINE, TA))
+    hi_c[...], hi_s[...] = turned(*base, range(half_bits, BITS))
+
+    zero = lax.broadcasted_iota(jnp.int32, (FINE, CH), 1) == 0
+
+    def fill(i, carry):
+        hc, hs = hi_c[pl.ds(i, 1), :], hi_s[pl.ds(i, 1), :]
+        at = pl.multiple_of(i * FINE, FINE)
+        c, s = hc * lc - hs * ls, hs * lc + hc * ls
+        table[pl.ds(at, FINE), :] = c[:, :TN].astype(jnp.bfloat16)
+        table[pl.ds(W + at, FINE), :] = (-s[:, :TN]).astype(jnp.bfloat16)
+        table[pl.ds(W + at, FINE), 0:CH] = jnp.where(zero, s[:, TN:], -s[:, :CH]).astype(jnp.bfloat16)
+        edge[pl.ds(at, FINE), :] = jnp.where(zero, c[:, TN:], 0.0).astype(jnp.bfloat16)
+        return carry
+
+    lax.fori_loop(0, W // FINE, fill, 0)
+
     part = NZ * SD // NR
     rows = (0, pl.multiple_of(part + core * part, part), pl.multiple_of(2 * part - core * part, part), 3 * part, 7 * part // 2)
     for at, ref in zip(rows, (near_ref, first_ref, second_ref, third_ref, fourth_ref)):
@@ -150,39 +153,49 @@
     scale = taper / (NX * math.sqrt(NB))
     half = NZ // NR // 2
     low, high, pair_row = lax.optimization_barrier((near[:half], near[half:], pair_row))
-    moved = (neighbour(near, 1), neighbour(near, -1), neighbour(low, 2), neighbour(high, -2))
-
+    first, second, third = neighbour(near, 1), neighbour(near, -1), neighbour(low, 2)
+
+    long = pl.CostEstimate(flops=10**10, bytes_accessed=10**6, transcendentals=0)
     smem = pl.BlockSpec(memory_space=pltpu.SMEM)
     code = pl.pallas_call(
         codes,
         out_shape=jax.ShapeDtypeStruct((NG, PD), jnp.int32),
         in_specs=[smem] + vmem(3),
         out_specs=vmem(1)[0],
-        cost_estimate=pl.CostEstimate(flops=10**10, bytes_accessed=10**6, transcendentals=0),
+        cost_estimate=long,
         name="codes",
     )(s[None], pair_source[None], pair_owner.T, pair_row[None])
+    code, high = lax.optimization_barrier((code, high))
     code = lax.all_to_all(code, "grp", 0, 0, tiled=True)
-    code, moved, scale = lax.optimization_barrier((code, moved, scale))
-
+    moved = (first, second, third, neighbour(high, -2))
     params = pltpu.CompilerParams(vmem_limit_bytes=VMEM_LIMIT)
-    table, edge, stations, pick = pl.pallas_call(
+    pick = pl.pallas_call(
+        one_hots,
+        out_shape=jax.ShapeDtypeStruct((NC, 2 * HALF, NZ * SD), jnp.bfloat16),
+        in_specs=[smem] + vmem(1),
+        out_specs=vmem(1)[0],
+        scratch_shapes=[pltpu.VMEM((8, NC * 2 * HALF), jnp.int32)],
+        cost_estimate=long,
+        compiler_params=params,
+        name="one_hots",
+    )(g[None], code)
+    pick, moved, scale = lax.optimization_barrier((pick, moved, scale))
+    table, edge, stations = pl.pallas_call(
         stage,
         out_shape=(
             jax.ShapeDtypeStruct((2 * W, TN), jnp.bfloat16),
             jax.ShapeDtypeStruct((W, CH), jnp.bfloat16),
             jax.ShapeDtypeStruct((6, NZ * SD, W), jnp.bfloat16),
-            jax.ShapeDtypeStruct((NC, 2 * HALF, NZ * SD), jnp.bfloat16),
         ),
-        in_specs=[smem] + vmem(6),
-        out_specs=tuple(vmem(4)),
+        in_specs=[smem] + vmem(5),
+        out_specs=tuple(vmem(3)),
         scratch_shapes=[
-            pltpu.VMEM((8, NC * 2 * HALF), jnp.int32),
             pltpu.VMEM((FINE, TA), jnp.float32),
             pltpu.VMEM((FINE, TA), jnp.float32),
         ],
         compiler_params=params,
         name="stage",
-    )(g[None], code, near, *moved)
+    )(g[None], near, *moved)
 
     def lags(half, dtype):
         return pl.pallas_call(

time: 105 us -> 109 us (1.038)
  the two profiles are of different devices: /device:TPU:8 before, /device:TPU:32 now
where the time goes in v10:
time: 109 us; the launch traced here: 108 us
  blocking collectives  68.2 us (63%)
  starting transfers between devices  19 us (17%)
  Pallas kernels  9.92 us (9%)
  waiting for transfers between devices  9.11 us (8%)
  local copies, waits for them, and re-layouts  1.17 us (1%)
    all_gather x1, blocking collectives, body(): near = lax.all_gather(mine, 'sta', axis=0, axis_index_groups=planes)  29.2 us
    all_to_all x1, blocking collectives, body(): lax.all_to_all(part, ('grp', 'hr'), 0, 0, axis_index_groups=chips, tiled=...  26.5 us
    ppermute x4, starting transfers between devices, neighbour(): return lax.ppermute(x, ('sta', 'grp'), perm)  12.6 us
    all_gather x1, blocking collectives, body(): total = lax.all_gather(total, 'hr', axis=2, tiled=True)  12.5 us
    ppermute x4, waiting for transfers between devices, neighbour(): return lax.ppermute(x, ('sta', 'grp'), perm)  9.1 us
    pallas_call x2, Pallas kernels, lags(): pl.pallas_call(functools.partial(correlate, half), out_shape=jax.ShapeDty...  5.78 us
    all_to_all x1, starting transfers between devices, body(): code = lax.all_to_all(code, 'grp', 0, 0, tiled=True)  4.47 us
  transfers between devices with their start and end apart: 6, of which 2 were waited for; matrix products, arithmetic and copies ran while one was open for 0% of the time, Pallas kernels for 4%

profile of v10, /device:TPU:32, one launch (start us, length us, event | category | flops | bytes accessed | tf_op | source)
XLA Modules:
  0.0 108.2 jit_solution(9515624302687418498)
XLA Ops:
  0.0 1.1 %copy-done = bf16[1,8,6,8192]{3,1,2,0:T(8,128)(2,1)S(1)} copy-done((bf16[1,8,6,8192]{3,1,2,0:T(8,128)(2,1)S(1)}, bf16[1,8,6,8192]{3,1,2,0:T(8,128)(2,1)}, u32[]{:S(2)}) %copy-start) | copy-done | bytes 786456
  1.1 29.2 %all-gather = bf16[24,8,1024]{2,1,0:T(8,128)(2,1)S(1)} all-gather(bf16[6,8,1024]{2,1,0:T(8,128)(2,1)S(1)} %dynamic-slice_bitcast_fusion), channel_id=2, replica_groups={{0,128,256,384},{32,160,288,416},{64,192,320,448},{96,224,352,480},{1,1..., dimensions={0}, use_global_device_ids=true | all-gather | bytes 491520 | tf_op jit(solution)/shard_map/all_gather | solution.py:144
  30.4 2.9 %collective-permute-start = (bf16[4,6,8,1024]{3,2,1,0:T(8,128)(2,1)S(1)}, bf16[4,6,8,1024]{3,2,1,0:T(8,128)(2,1)S(1)}, u32[]{:S(2)}, u32[]{:S(2)}) collective-permute-start(bf16[4,6,8,1024]{3,2,1,0:T(8,128)(2,1)S(1)} %bitcast.18), channel_id=1, source_target_pairs={{0,32},{4,484},{8,40},{12,492},{16,48},{20,500},{24,56},{28,508},{... | collective-permute-start | bytes 1179656 | tf_op jit(solution)/shard_map/ppermute | solution.py:149
  33.3 2.9 %collective-permute-start.1 = (bf16[4,6,8,1024]{3,2,1,0:T(8,128)(2,1)S(1)}, bf16[4,6,8,1024]{3,2,1,0:T(8,128)(2,1)S(1)}, u32[]{:S(2)}, u32[]{:S(2)}) collective-permute-start(bf16[4,6,8,1024]{3,2,1,0:T(8,128)(2,1)S(1)} %bitcast.19), channel_id=1, source_target_pairs={{0,480},{4,36},{8,488},{12,44},{16,496},{20,52},{24,504},{28,60},{... | collective-permute-start | bytes 1179656 | tf_op jit(solution)/shard_map/ppermute | solution.py:149
  36.3 1.3 %codes.1 = s32[8,16]{1,0:T(8,128)} custom-call(s32[1]{0:T(128)} %bitcast.1.plane_ref, s32[1,16]{1,0:T(1,128)} %bitcast.26, s32[1,16]{1,0:T(1,128)} %bitcast.27, s32[1,16]{1,0:T(1,128)} %bitcast.28), custom_call_target="tpu_custom_call" | custom-call | flops 10000000000 | bytes 1000000 | tf_op jit(solution)/shard_map/codes/pallas_call | solution.py:160
  37.6 4.5 %all-to-all-start = ((s32[8,1,16]{2,1,0:T(1,128)}), s32[8,1,16]{2,1,0:T(1,128)S(1)}, u32[]{:S(2)}, u32[]{:S(2)}) async-start(s32[8,1,16]{2,1,0:T(1,128)} %bitcast.25), calls=%async_computation | async-start | bytes 8192 | tf_op jit(solution)/shard_map/all_to_all | solution.py:169
  42.0 3.9 %collective-permute-start.3 = (bf16[2,6,8,1024]{3,2,1,0:T(8,128)(2,1)S(1)}, bf16[2,6,8,1024]{3,2,1,0:T(8,128)(2,1)S(1)}, u32[]{:S(2)}, u32[]{:S(2)}) collective-permute-start(bf16[2,6,8,1024]{3,2,1,0:T(8,128)(2,1)S(1)} %bitcast.24), channel_id=1, source_target_pairs={{0,448},{4,68},{8,456},{12,76},{16,464},{20,84},{24,472},{28,92},{... | collective-permute-start | bytes 589832 | tf_op jit(solution)/shard_map/ppermute | solution.py:149
  46.0 2.8 %collective-permute-start.2 = (bf16[2,6,8,1024]{3,2,1,0:T(8,128)(2,1)S(1)}, bf16[2,6,8,1024]{3,2,1,0:T(8,128)(2,1)S(1)}, u32[]{:S(2)}, u32[]{:S(2)}) collective-permute-start(bf16[2,6,8,1024]{3,2,1,0:T(8,128)(2,1)S(1)} %bitcast.23), channel_id=1, source_target_pairs={{0,64},{4,452},{8,72},{12,460},{16,80},{20,468},{24,88},{28,476},{... | collective-permute-start | bytes 589832 | tf_op jit(solution)/shard_map/ppermute | solution.py:149
  48.8 0.1 subtract_multiply_fusion.scale_ref
  48.9 0.0 all-to-all-done
  48.9 0.2 one_hots.1.pick
  49.1 2.2 %collective-permute-done.3.fourth_ref = bf16[2,6,8,1024]{3,2,1,0:T(8,128)(2,1)S(1)} collective-permute-done((bf16[2,6,8,1024]{3,2,1,0:T(8,128)(2,1)S(1)}, bf16[2,6,8,1024]{3,2,1,0:T(8,128)(2,1)S(1)}, u32[]{:S(2)}, u32[]{:S(2)}) %collective-permute-start.3) | collective-permute-done | bytes 196640 | tf_op jit(solution)/shard_map/ppermute | solution.py:149
  51.3 6.9 %collective-permute-done.2.third_ref = bf16[2,6,8,1024]{3,2,1,0:T(8,128)(2,1)S(1)} collective-permute-done((bf16[2,6,8,1024]{3,2,1,0:T(8,128)(2,1)S(1)}, bf16[2,6,8,1024]{3,2,1,0:T(8,128)(2,1)S(1)}, u32[]{:S(2)}, u32[]{:S(2)}) %collective-permute-start.2) | collective-permute-done | bytes 196640 | tf_op jit(solution)/shard_map/ppermute | solution.py:149
  58.2 0.0 collective-permute-done.first_ref
  58.2 0.0 collective-permute-done.1.second_ref
  58.2 1.5 %stage.1 = (bf16[2048,512]{1,0:T(8,128)(2,1)S(1)}, bf16[1024,128]{1,0:T(8,128)(2,1)S(1)}, bf16[6,128,1024]{2,1,0:T(8,128)(2,1)S(1)}) custom-call(s32[1]{0:T(128)} %bitcast.grp_ref, bf16[4,6,8,1024]{3,2,1,0:T(8,128)(2,1)S(1)} %bitcast.20, bf16[4,6,8,1024]{3,2,1,0:T(8,128)(2,1)S(1)} %collective-permute-done.first_ref, ...), custom_call_target="tpu_custom_call" | custom-call | tf_op jit(solution)/shard_map/stage/pallas_call | solution.py:183
  59.8 2.9 %correlate.3 = bf16[4,4,9,16,256]{4,3,2,1,0:T(8,128)(2,1)S(1)} custom-call(bf16[2,128,128]{2,1,0:T(8,128)(2,1)S(1)} %one_hots.1.pick, bf16[6,128,1024]{2,1,0:T(8,128)(2,1)S(1)} %get-tuple-element.30.stations, bf16[2048,512]{1,0:T(8,128)(2,1)S(1)} %get-tuple-element.31.table, bf16[1024,128]{1,0:T(8,128)(2,1)S(1)} %get-tuple-element.32.edge), custom_call_target="tpu_custom_call" | custom-call | tf_op jit(solution)/shard_map/correlate/pallas_call | solution.py:201
  62.7 1.9 %collective-permute-start.4 = (bf16[4,4,9,16,256]{4,3,2,1,0:T(8,128)(2,1)S(1)}, bf16[4,4,9,16,256]{4,3,2,1,0:T(8,128)(2,1)S(1)}, u32[]{:S(2)}, u32[]{:S(2)}) collective-permute-start(bf16[4,4,9,16,256]{4,3,2,1,0:T(8,128)(2,1)S(1)} %correlate.3), channel_id=1, source_target_pairs={{0,4},{4,0},{8,12},{12,8},{16,20},{20,16},{24,28},{28,24},{1,5},{5... | collective-permute-start | bytes 3538952 | tf_op jit(solution)/shard_map/ppermute | solution.py:213
  64.6 2.9 %correlate.2 = f32[4,4,9,16,256]{4,3,2,1,0:T(8,128)S(1)} custom-call(bf16[2,128,128]{2,1,0:T(8,128)(2,1)S(1)} %one_hots.1.pick, bf16[6,128,1024]{2,1,0:T(8,128)(2,1)S(1)} %get-tuple-element.30.stations, bf16[2048,512]{1,0:T(8,128)(2,1)S(1)} %get-tuple-element.31.table, bf16[1024,128]{1,0:T(8,128)(2,1)S(1)} %get-tuple-element.32.edge), custom_call_target="tpu_custom_call" | custom-call | tf_op jit(solution)/shard_map/correlate/pallas_call | solution.py:201
  67.5 0.4 add_convert_fusion
  67.9 26.5 %all_to_all.16 = bf16[16,9,16,256]{3,2,1,0:T(8,128)(2,1)S(1)} all-to-all(bf16[16,9,16,256]{3,2,1,0:T(8,128)(2,1)S(1)} %bitcast.22), channel_id=1, replica_groups={{0,1,2,3,8,9,10,11,16,17,18,19,24,25,26,27},{4,5,6,7,12,13,14,15,20,21,..., dimensions={0} | all-to-all | bytes 2359296 | tf_op jit(solution)/shard_map/all_to_all | solution.py:216
  94.4 0.2 reduce_sum.12
  94.6 12.5 %all_gather.11.x_ref = bf16[9,16,1024]{2,1,0:T(8,128)(2,1)S(1)} all-gather(bf16[9,16,256]{2,1,0:T(8,128)(2,1)S(1)} %reduce_sum.12), channel_id=1, replica_groups=mesh['sta'=16,'grp'=8,'hr'=4] {'hr'}, dimensions={2}, use_global_device_ids=true | all-gather | bytes 368640 | tf_op jit(solution)/shard_map/all_gather | solution.py:218
  107.0 1.1 %unfold.1 = f32[9,16,1024]{2,1,0:T(8,128)} custom-call(f32[1,1024]{1,0:T(1,128)S(1)} %subtract_multiply_fusion.scale_ref, bf16[9,16,1024]{2,1,0:T(8,128)(2,1)S(1)} %all_gather.11.x_ref), custom_call_target="tpu_custom_call" | custom-call | tf_op jit(solution)/shard_map/unfold/pallas_call | solution.py:219
  (4 shorter events, 0.0 us)
Async XLA Ops:
  0.0 1.1 %copy-start = (bf16[1,8,6,8192]{3,1,2,0:T(8,128)(2,1)S(1)}, bf16[1,8,6,8192]{3,1,2,0:T(8,128)(2,1)}, u32[]{:S(2)}) copy-start(bf16[1,8,6,8192]{3,1,2,0:T(8,128)(2,1)} %param.4) | copy-start | bytes 2359300
  30.4 27.9 %collective-permute-start = (bf16[4,6,8,1024]{3,2,1,0:T(8,128)(2,1)S(1)}, bf16[4,6,8,1024]{3,2,1,0:T(8,128)(2,1)S(1)}, u32[]{:S(2)}, u32[]{:S(2)}) collective-permute-start(bf16[4,6,8,1024]{3,2,1,0:T(8,128)(2,1)S(1)} %bitcast.18), channel_id=1, source_target_pairs={{0,32},{4,484},{8,40},{12,492},{16,48},{20,500},{24,56},{28,508},{... | collective-permute-start | bytes 1179656 | tf_op jit(solution)/shard_map/ppermute | solution.py:149
  33.3 25.0 %collective-permute-start.1 = (bf16[4,6,8,1024]{3,2,1,0:T(8,128)(2,1)S(1)}, bf16[4,6,8,1024]{3,2,1,0:T(8,128)(2,1)S(1)}, u32[]{:S(2)}, u32[]{:S(2)}) collective-permute-start(bf16[4,6,8,1024]{3,2,1,0:T(8,128)(2,1)S(1)} %bitcast.19), channel_id=1, source_target_pairs={{0,480},{4,36},{8,488},{12,44},{16,496},{20,52},{24,504},{28,60},{... | collective-permute-start | bytes 1179656 | tf_op jit(solution)/shard_map/ppermute | solution.py:149
  37.6 11.4 %all-to-all-start = ((s32[8,1,16]{2,1,0:T(1,128)}), s32[8,1,16]{2,1,0:T(1,128)S(1)}, u32[]{:S(2)}, u32[]{:S(2)}) async-start(s32[8,1,16]{2,1,0:T(1,128)} %bitcast.25), calls=%async_computation | async-start | bytes 8192 | tf_op jit(solution)/shard_map/all_to_all | solution.py:169
  42.0 9.3 %collective-permute-start.3 = (bf16[2,6,8,1024]{3,2,1,0:T(8,128)(2,1)S(1)}, bf16[2,6,8,1024]{3,2,1,0:T(8,128)(2,1)S(1)}, u32[]{:S(2)}, u32[]{:S(2)}) collective-permute-start(bf16[2,6,8,1024]{3,2,1,0:T(8,128)(2,1)S(1)} %bitcast.24), channel_id=1, source_target_pairs={{0,448},{4,68},{8,456},{12,76},{16,464},{20,84},{24,472},{28,92},{... | collective-permute-start | bytes 589832 | tf_op jit(solution)/shard_map/ppermute | solution.py:149
  46.0 12.3 %collective-permute-start.2 = (bf16[2,6,8,1024]{3,2,1,0:T(8,128)(2,1)S(1)}, bf16[2,6,8,1024]{3,2,1,0:T(8,128)(2,1)S(1)}, u32[]{:S(2)}, u32[]{:S(2)}) collective-permute-start(bf16[2,6,8,1024]{3,2,1,0:T(8,128)(2,1)S(1)} %bitcast.23), channel_id=1, source_target_pairs={{0,64},{4,452},{8,72},{12,460},{16,80},{20,468},{24,88},{28,476},{... | collective-permute-start | bytes 589832 | tf_op jit(solution)/shard_map/ppermute | solution.py:149
  62.7 4.8 %collective-permute-start.4 = (bf16[4,4,9,16,256]{4,3,2,1,0:T(8,128)(2,1)S(1)}, bf16[4,4,9,16,256]{4,3,2,1,0:T(8,128)(2,1)S(1)}, u32[]{:S(2)}, u32[]{:S(2)}) collective-permute-start(bf16[4,4,9,16,256]{4,3,2,1,0:T(8,128)(2,1)S(1)} %correlate.3), channel_id=1, source_target_pairs={{0,4},{4,0},{8,12},{12,8},{16,20},{20,16},{24,28},{28,24},{1,5},{5... | collective-permute-start | bytes 3538952 | tf_op jit(solution)/shard_map/ppermute | solution.py:213

commit v11 on v10

--- a/solution.py
+++ b/solution.py
@@ -139,35 +139,32 @@
 
 def body(spectra, pair_source, pair_owner, pair_row):
     s, g = lax.axis_index("sta"), lax.axis_index("grp")
-    mine = lax.dynamic_slice_in_dim(spectra[0], g * W, W, 2).transpose(1, 0, 2)
-    planes = [list(range(p, NZ, NR)) for p in range(NR)]
-    near = lax.all_gather(mine, "sta", axis=0, axis_index_groups=planes)
-
-    def neighbour(x, step):
-        turn = [step if i % NC == 0 else -step for i in range(NG)]
-        perm = [(z * NG + i, (z + turn[i]) % NZ * NG + i) for z in range(NZ) for i in range(NG)]
-        return lax.ppermute(x, ("sta", "grp"), perm)
-
-    pos = jnp.arange(LAGS, dtype=jnp.float32)[None]
-    taper = 0.75 - 0.25 * jnp.cos(TWO_PI * (pos + 0.5) / LAGS)
-    scale = taper / (NX * math.sqrt(NB))
-    half = NZ // NR // 2
-    low, high, pair_row = lax.optimization_barrier((near[:half], near[half:], pair_row))
-    first, second, third = neighbour(near, 1), neighbour(near, -1), neighbour(low, 2)
-
-    long = pl.CostEstimate(flops=10**10, bytes_accessed=10**6, transcendentals=0)
     smem = pl.BlockSpec(memory_space=pltpu.SMEM)
     code = pl.pallas_call(
         codes,
         out_shape=jax.ShapeDtypeStruct((NG, PD), jnp.int32),
         in_specs=[smem] + vmem(3),
         out_specs=vmem(1)[0],
-        cost_estimate=long,
         name="codes",
     )(s[None], pair_source[None], pair_owner.T, pair_row[None])
-    code, high = lax.optimization_barrier((code, high))
     code = lax.all_to_all(code, "grp", 0, 0, tiled=True)
-    moved = (first, second, third, neighbour(high, -2))
+
+    mine = lax.dynamic_slice_in_dim(spectra[0], g * W, W, 2).transpose(1, 0, 2)
+    planes = [list(range(p, NZ, NR)) for p in range(NR)]
+    near = lax.all_gather(mine, "sta", axis=0, axis_index_groups=planes)
+    near, code = lax.optimization_barrier((near, code))
+
+    def neighbour(x, step):
+        turn = [step if i % NC == 0 else -step for i in range(NG)]
+        perm = [(z * NG + i, (z + turn[i]) % NZ * NG + i) for z in range(NZ) for i in range(NG)]
+        return lax.ppermute(x, ("sta", "grp"), perm)
+
+    pos = jnp.arange(LAGS, dtype=jnp.float32)[None]
+    taper = 0.75 - 0.25 * jnp.cos(TWO_PI * (pos + 0.5) / LAGS)
+    scale = taper / (NX * math.sqrt(NB))
+    half = NZ // NR // 2
+    moved = (neighbour(near, 1), neighbour(near, -1), neighbour(near[:half], 2), neighbour(near[half:], -2))
+
     params = pltpu.CompilerParams(vmem_limit_bytes=VMEM_LIMIT)
     pick = pl.pallas_call(
         one_hots,
@@ -175,7 +172,6 @@
         in_specs=[smem] + vmem(1),
         out_specs=vmem(1)[0],
         scratch_shapes=[pltpu.VMEM((8, NC * 2 * HALF), jnp.int32)],
-        cost_estimate=long,
         compiler_params=params,
         name="one_hots",
     )(g[None], code)

time: 109 us -> 107 us (0.982)
  the two profiles are of different devices: /device:TPU:32 before, /device:TPU:8 now
where the time goes in v11:
time: 107 us
  blocking collectives  62.1 us (58%)
  starting transfers between devices  24.3 us (23%)
  Pallas kernels  9.99 us (9%)
  waiting for transfers between devices  9.82 us (9%)
    all_gather x1, blocking collectives, body(): near = lax.all_gather(mine, 'sta', axis=0, axis_index_groups=planes)  24.7 us
    all_to_all x1, blocking collectives, body(): lax.all_to_all(part, ('grp', 'hr'), 0, 0, axis_index_groups=chips, tiled=...  24.7 us
    ppermute x4, starting transfers between devices, neighbour(): return lax.ppermute(x, ('sta', 'grp'), perm)  13.4 us
    all_gather x1, blocking collectives, body(): total = lax.all_gather(total, 'hr', axis=2, tiled=True)  12.7 us
    ppermute x4, waiting for transfers between devices, neighbour(): return lax.ppermute(x, ('sta', 'grp'), perm)  9.82 us
    all_to_all x1, starting transfers between devices, body(): code = lax.all_to_all(code, 'grp', 0, 0, tiled=True)  9.04 us
    pallas_call x2, Pallas kernels, lags(): pl.pallas_call(functools.partial(correlate, half), out_shape=jax.ShapeDty...  5.79 us
  transfers between devices with their start and end apart: 6, of which 2 were waited for; matrix products, arithmetic and copies ran while one was open for 0% of the time, Pallas kernels for 3%

profile of v11, /device:TPU:8, one launch (start us, length us, event | category | flops | bytes accessed | tf_op | source)
XLA Modules:
  0.0 107.0 jit_solution(3929505785514980082)
XLA Ops:
  0.0 1.4 %codes.1 = s32[8,16]{1,0:T(8,128)} custom-call(s32[1]{0:T(128)} %bitcast.4.plane_ref, s32[1,16]{1,0:T(1,128)} %bitcast.23, s32[1,16]{1,0:T(1,128)} %bitcast.24, s32[1,16]{1,0:T(1,128)} %bitcast.25), custom_call_target="tpu_custom_call" | custom-call | tf_op jit(solution)/shard_map/codes/pallas_call | solution.py:143
  1.4 9.0 %all-to-all-start = ((s32[8,1,16]{2,1,0:T(1,128)}), s32[8,1,16]{2,1,0:T(1,128)S(1)}, u32[]{:S(2)}, u32[]{:S(2)}) async-start(s32[8,1,16]{2,1,0:T(1,128)} %bitcast.22), calls=%async_computation | async-start | bytes 8192 | tf_op jit(solution)/shard_map/all_to_all | solution.py:150
  10.4 24.7 %all-gather = bf16[24,8,1024]{2,1,0:T(8,128)(2,1)S(1)} all-gather(bf16[6,8,1024]{2,1,0:T(8,128)(2,1)S(1)} %dynamic-slice_bitcast_fusion), channel_id=2, replica_groups={{0,128,256,384},{32,160,288,416},{64,192,320,448},{96,224,352,480},{1,1..., dimensions={0}, use_global_device_ids=true | all-gather | bytes 491520 | tf_op jit(solution)/shard_map/all_gather | solution.py:154
  35.1 0.0 all-to-all-done
  35.1 4.7 %collective-permute-start.1 = (bf16[4,6,8,1024]{3,2,1,0:T(8,128)(2,1)S(1)}, bf16[4,6,8,1024]{3,2,1,0:T(8,128)(2,1)S(1)}, u32[]{:S(2)}, u32[]{:S(2)}) collective-permute-start(bf16[4,6,8,1024]{3,2,1,0:T(8,128)(2,1)S(1)} %bitcast.16), channel_id=1, source_target_pairs={{0,480},{4,36},{8,488},{12,44},{16,496},{20,52},{24,504},{28,60},{... | collective-permute-start | bytes 1179656 | tf_op jit(solution)/shard_map/ppermute | solution.py:160
  39.9 1.9 %collective-permute-start = (bf16[4,6,8,1024]{3,2,1,0:T(8,128)(2,1)S(1)}, bf16[4,6,8,1024]{3,2,1,0:T(8,128)(2,1)S(1)}, u32[]{:S(2)}, u32[]{:S(2)}) collective-permute-start(bf16[4,6,8,1024]{3,2,1,0:T(8,128)(2,1)S(1)} %bitcast.17), channel_id=1, source_target_pairs={{0,32},{4,484},{8,40},{12,492},{16,48},{20,500},{24,56},{28,508},{... | collective-permute-start | bytes 1179656 | tf_op jit(solution)/shard_map/ppermute | solution.py:160
  41.8 4.7 %collective-permute-start.3 = (bf16[2,6,8,1024]{3,2,1,0:T(8,128)(2,1)S(1)}, bf16[2,6,8,1024]{3,2,1,0:T(8,128)(2,1)S(1)}, u32[]{:S(2)}, u32[]{:S(2)}) collective-permute-start(bf16[2,6,8,1024]{3,2,1,0:T(8,128)(2,1)S(1)} %get-tuple-element.27), channel_id=1, source_target_pairs={{0,448},{4,68},{8,456},{12,76},{16,464},{20,84},{24,472},{28,92},{... | collective-permute-start | bytes 589832 | tf_op jit(solution)/shard_map/ppermute | solution.py:160
  46.5 2.1 %collective-permute-start.2 = (bf16[2,6,8,1024]{3,2,1,0:T(8,128)(2,1)S(1)}, bf16[2,6,8,1024]{3,2,1,0:T(8,128)(2,1)S(1)}, u32[]{:S(2)}, u32[]{:S(2)}) collective-permute-start(bf16[2,6,8,1024]{3,2,1,0:T(8,128)(2,1)S(1)} %get-tuple-element.28), channel_id=1, source_target_pairs={{0,64},{4,452},{8,72},{12,460},{16,80},{20,468},{24,88},{28,476},{... | collective-permute-start | bytes 589832 | tf_op jit(solution)/shard_map/ppermute | solution.py:160
  48.6 0.1 subtract_multiply_fusion.scale_ref
  48.7 0.2 one_hots.1.pick
  48.9 9.2 %collective-permute-done.3.fourth_ref = bf16[2,6,8,1024]{3,2,1,0:T(8,128)(2,1)S(1)} collective-permute-done((bf16[2,6,8,1024]{3,2,1,0:T(8,128)(2,1)S(1)}, bf16[2,6,8,1024]{3,2,1,0:T(8,128)(2,1)S(1)}, u32[]{:S(2)}, u32[]{:S(2)}) %collective-permute-start.3) | collective-permute-done | bytes 196640 | tf_op jit(solution)/shard_map/ppermute | solution.py:160
  58.1 0.6 collective-permute-done.2.third_ref
  58.7 0.0 collective-permute-done.1.second_ref
  58.7 0.0 collective-permute-done.first_ref
  58.7 1.5 %stage.1 = (bf16[2048,512]{1,0:T(8,128)(2,1)S(1)}, bf16[1024,128]{1,0:T(8,128)(2,1)S(1)}, bf16[6,128,1024]{2,1,0:T(8,128)(2,1)S(1)}) custom-call(s32[1]{0:T(128)} %bitcast.grp_ref, bf16[4,6,8,1024]{3,2,1,0:T(8,128)(2,1)S(1)} %bitcast.19, bf16[4,6,8,1024]{3,2,1,0:T(8,128)(2,1)S(1)} %collective-permute-done.first_ref, ...), custom_call_target="tpu_custom_call" | custom-call | tf_op jit(solution)/shard_map/stage/pallas_call | solution.py:179
  60.3 2.9 %correlate.3 = bf16[4,4,9,16,256]{4,3,2,1,0:T(8,128)(2,1)S(1)} custom-call(bf16[2,128,128]{2,1,0:T(8,128)(2,1)S(1)} %one_hots.1.pick, bf16[6,128,1024]{2,1,0:T(8,128)(2,1)S(1)} %get-tuple-element.24.stations, bf16[2048,512]{1,0:T(8,128)(2,1)S(1)} %get-tuple-element.25.table, bf16[1024,128]{1,0:T(8,128)(2,1)S(1)} %get-tuple-element.26.edge), custom_call_target="tpu_custom_call" | custom-call | tf_op jit(solution)/shard_map/correlate/pallas_call | solution.py:197
  63.2 1.9 %collective-permute-start.4 = (bf16[4,4,9,16,256]{4,3,2,1,0:T(8,128)(2,1)S(1)}, bf16[4,4,9,16,256]{4,3,2,1,0:T(8,128)(2,1)S(1)}, u32[]{:S(2)}, u32[]{:S(2)}) collective-permute-start(bf16[4,4,9,16,256]{4,3,2,1,0:T(8,128)(2,1)S(1)} %correlate.3), channel_id=1, source_target_pairs={{0,4},{4,0},{8,12},{12,8},{16,20},{20,16},{24,28},{28,24},{1,5},{5... | collective-permute-start | bytes 3538952 | tf_op jit(solution)/shard_map/ppermute | solution.py:209
  65.1 2.9 %correlate.2 = f32[4,4,9,16,256]{4,3,2,1,0:T(8,128)S(1)} custom-call(bf16[2,128,128]{2,1,0:T(8,128)(2,1)S(1)} %one_hots.1.pick, bf16[6,128,1024]{2,1,0:T(8,128)(2,1)S(1)} %get-tuple-element.24.stations, bf16[2048,512]{1,0:T(8,128)(2,1)S(1)} %get-tuple-element.25.table, bf16[1024,128]{1,0:T(8,128)(2,1)S(1)} %get-tuple-element.26.edge), custom_call_target="tpu_custom_call" | custom-call | tf_op jit(solution)/shard_map/correlate/pallas_call | solution.py:197
  68.0 0.0 collective-permute-done.4
  68.0 0.4 add_convert_fusion
  68.4 24.7 %all_to_all.17 = bf16[16,9,16,256]{3,2,1,0:T(8,128)(2,1)S(1)} all-to-all(bf16[16,9,16,256]{3,2,1,0:T(8,128)(2,1)S(1)} %bitcast.21), channel_id=1, replica_groups={{0,1,2,3,8,9,10,11,16,17,18,19,24,25,26,27},{4,5,6,7,12,13,14,15,20,21,..., dimensions={0} | all-to-all | bytes 2359296 | tf_op jit(solution)/shard_map/all_to_all | solution.py:212
  93.1 0.2 reduce_sum.12
  93.2 12.7 %all_gather.11.x_ref = bf16[9,16,1024]{2,1,0:T(8,128)(2,1)S(1)} all-gather(bf16[9,16,256]{2,1,0:T(8,128)(2,1)S(1)} %reduce_sum.12), channel_id=1, replica_groups=mesh['sta'=16,'grp'=8,'hr'=4] {'hr'}, dimensions={2}, use_global_device_ids=true | all-gather | bytes 368640 | tf_op jit(solution)/shard_map/all_gather | solution.py:214
  105.9 1.1 %unfold.1 = f32[9,16,1024]{2,1,0:T(8,128)} custom-call(f32[1,1024]{1,0:T(1,128)S(1)} %subtract_multiply_fusion.scale_ref, bf16[9,16,1024]{2,1,0:T(8,128)(2,1)S(1)} %all_gather.11.x_ref), custom_call_target="tpu_custom_call" | custom-call | tf_op jit(solution)/shard_map/unfold/pallas_call | solution.py:215
  (4 shorter events, 0.0 us)
Async XLA Ops:
  0.0 10.4 %copy-start = (bf16[1,8,6,8192]{3,1,2,0:T(8,128)(2,1)S(1)}, bf16[1,8,6,8192]{3,1,2,0:T(8,128)(2,1)}, u32[]{:S(2)}) copy-start(bf16[1,8,6,8192]{3,1,2,0:T(8,128)(2,1)} %param.4) | copy-start | bytes 2359300
  1.4 33.8 %all-to-all-start = ((s32[8,1,16]{2,1,0:T(1,128)}), s32[8,1,16]{2,1,0:T(1,128)S(1)}, u32[]{:S(2)}, u32[]{:S(2)}) async-start(s32[8,1,16]{2,1,0:T(1,128)} %bitcast.22), calls=%async_computation | async-start | bytes 8192 | tf_op jit(solution)/shard_map/all_to_all | solution.py:150
  35.1 23.6 %collective-permute-start.1 = (bf16[4,6,8,1024]{3,2,1,0:T(8,128)(2,1)S(1)}, bf16[4,6,8,1024]{3,2,1,0:T(8,128)(2,1)S(1)}, u32[]{:S(2)}, u32[]{:S(2)}) collective-permute-start(bf16[4,6,8,1024]{3,2,1,0:T(8,128)(2,1)S(1)} %bitcast.16), channel_id=1, source_target_pairs={{0,480},{4,36},{8,488},{12,44},{16,496},{20,52},{24,504},{28,60},{... | collective-permute-start | bytes 1179656 | tf_op jit(solution)/shard_map/ppermute | solution.py:160
  39.9 18.9 %collective-permute-start = (bf16[4,6,8,1024]{3,2,1,0:T(8,128)(2,1)S(1)}, bf16[4,6,8,1024]{3,2,1,0:T(8,128)(2,1)S(1)}, u32[]{:S(2)}, u32[]{:S(2)}) collective-permute-start(bf16[4,6,8,1024]{3,2,1,0:T(8,128)(2,1)S(1)} %bitcast.17), channel_id=1, source_target_pairs={{0,32},{4,484},{8,40},{12,492},{16,48},{20,500},{24,56},{28,508},{... | collective-permute-start | bytes 1179656 | tf_op jit(solution)/shard_map/ppermute | solution.py:160
  41.8 16.3 %collective-permute-start.3 = (bf16[2,6,8,1024]{3,2,1,0:T(8,128)(2,1)S(1)}, bf16[2,6,8,1024]{3,2,1,0:T(8,128)(2,1)S(1)}, u32[]{:S(2)}, u32[]{:S(2)}) collective-permute-start(bf16[2,6,8,1024]{3,2,1,0:T(8,128)(2,1)S(1)} %get-tuple-element.27), channel_id=1, source_target_pairs={{0,448},{4,68},{8,456},{12,76},{16,464},{20,84},{24,472},{28,92},{... | collective-permute-start | bytes 589832 | tf_op jit(solution)/shard_map/ppermute | solution.py:160
  46.5 12.2 %collective-permute-start.2 = (bf16[2,6,8,1024]{3,2,1,0:T(8,128)(2,1)S(1)}, bf16[2,6,8,1024]{3,2,1,0:T(8,128)(2,1)S(1)}, u32[]{:S(2)}, u32[]{:S(2)}) collective-permute-start(bf16[2,6,8,1024]{3,2,1,0:T(8,128)(2,1)S(1)} %get-tuple-element.28), channel_id=1, source_target_pairs={{0,64},{4,452},{8,72},{12,460},{16,80},{20,468},{24,88},{28,476},{... | collective-permute-start | bytes 589832 | tf_op jit(solution)/shard_map/ppermute | solution.py:160
  63.2 4.8 %collective-permute-start.4 = (bf16[4,4,9,16,256]{4,3,2,1,0:T(8,128)(2,1)S(1)}, bf16[4,4,9,16,256]{4,3,2,1,0:T(8,128)(2,1)S(1)}, u32[]{:S(2)}, u32[]{:S(2)}) collective-permute-start(bf16[4,4,9,16,256]{4,3,2,1,0:T(8,128)(2,1)S(1)} %correlate.3), channel_id=1, source_target_pairs={{0,4},{4,0},{8,12},{12,8},{16,20},{20,16},{24,28},{28,24},{1,5},{5... | collective-permute-start | bytes 3538952 | tf_op jit(solution)/shard_map/ppermute | solution.py:209

commit v12 on v9

--- a/solution.py
+++ b/solution.py
@@ -17,6 +17,7 @@
 FINE = 32
 HALF = NY * PD
 CH = 128
+PC = 256
 TN = LAGS // 2
 TA = TN + CH
 TW = LAGS // NX
@@ -88,11 +89,11 @@
 
 
 def correlate(half, pick, stations, table, edge, out_ref, cross):
-    for k in range(W // CH):
-        at = k * CH
+    for k in range(W // PC):
+        at = k * PC
         r, s = [], []
         for comp in range(6):
-            x = jnp.dot(pick[half], stations[comp, :, at : at + CH], preferred_element_type=jnp.float32)
+            x = jnp.dot(pick[half], stations[comp, :, at : at + PC], preferred_element_type=jnp.float32)
             r.append(x[:HALF])
             s.append(x[HALF:])
         for a in range(3):
@@ -100,8 +101,8 @@
                 r0 = (3 * a + b) * HALF
                 re = s[a] * r[b] + s[3 + a] * r[3 + b]
                 im = s[a] * r[3 + b] - s[3 + a] * r[b]
-                cross[r0 : r0 + HALF, at : at + CH] = re.astype(jnp.bfloat16)
-                cross[r0 : r0 + HALF, W + at : W + at + CH] = im.astype(jnp.bfloat16)
+                cross[r0 : r0 + HALF, at : at + PC] = re.astype(jnp.bfloat16)
+                cross[r0 : r0 + HALF, W + at : W + at + PC] = im.astype(jnp.bfloat16)
 
     for n in range(NX):
         odd, at = n // 2 * W, n % 2 * TW

time: 105 us -> 103 us (0.981)
  transfers between devices with their start and end apart: 6 -> 6, of which waited for: 1 -> 2; matrix products, arithmetic and copies ran while one was open for 0% -> 0% of each run, Pallas kernels for 4% -> 4%
where the time goes in v12:
time: 103 us
  blocking collectives  66.4 us (64%)
  starting transfers between devices  21.8 us (21%)
  Pallas kernels  8.84 us (9%)
  waiting for transfers between devices  4.02 us (4%)
  local copies, waits for them, and re-layouts  1.17 us (1%)
    all_gather x1, blocking collectives, body(): near = lax.all_gather(mine, 'sta', axis=0, axis_index_groups=planes)  30.5 us
    all_to_all x1, blocking collectives, body(): lax.all_to_all(part, ('grp', 'hr'), 0, 0, axis_index_groups=chips, tiled=...  23.4 us
    ppermute x4, starting transfers between devices, neighbour(): return lax.ppermute(x, ('sta', 'grp'), perm)  15 us
    all_gather x1, blocking collectives, body(): total = lax.all_gather(total, 'hr', axis=2, tiled=True)  12.5 us
    all_to_all x1, starting transfers between devices, body(): code = lax.all_to_all(code, 'grp', 0, 0, tiled=True)  4.92 us
    pallas_call x2, Pallas kernels, lags(): pl.pallas_call(functools.partial(correlate, half), out_shape=jax.ShapeDty...  4.78 us
    all_to_all x1, waiting for transfers between devices, body(): code = lax.all_to_all(code, 'grp', 0, 0, tiled=True)  3.59 us
  transfers between devices with their start and end apart: 6, of which 2 were waited for; matrix products, arithmetic and copies ran while one was open for 0% of the time, Pallas kernels for 4%

profile of v12, /device:TPU:8, one launch (start us, length us, event | category | flops | bytes accessed | tf_op | source)
XLA Modules:
  0.0 103.1 jit_solution(14352962925790923042)
XLA Ops:
  0.0 1.1 %copy-done = bf16[1,8,6,8192]{3,1,2,0:T(8,128)(2,1)S(1)} copy-done((bf16[1,8,6,8192]{3,1,2,0:T(8,128)(2,1)S(1)}, bf16[1,8,6,8192]{3,1,2,0:T(8,128)(2,1)}, u32[]{:S(2)}) %copy-start) | copy-done | bytes 786456
  1.1 30.5 %all-gather = bf16[24,8,1024]{2,1,0:T(8,128)(2,1)S(1)} all-gather(bf16[6,8,1024]{2,1,0:T(8,128)(2,1)S(1)} %dynamic-slice_bitcast_fusion), channel_id=2, replica_groups={{0,128,256,384},{32,160,288,416},{64,192,320,448},{96,224,352,480},{1,1..., dimensions={0}, use_global_device_ids=true | all-gather | bytes 491520 | tf_op jit(solution)/shard_map/all_gather | solution.py:142
  31.6 2.5 %collective-permute-start = (bf16[4,6,8,1024]{3,2,1,0:T(8,128)(2,1)S(1)}, bf16[4,6,8,1024]{3,2,1,0:T(8,128)(2,1)S(1)}, u32[]{:S(2)}, u32[]{:S(2)}) collective-permute-start(bf16[4,6,8,1024]{3,2,1,0:T(8,128)(2,1)S(1)} %bitcast.18), channel_id=1, source_target_pairs={{0,32},{4,484},{8,40},{12,492},{16,48},{20,500},{24,56},{28,508},{... | collective-permute-start | bytes 1179656 | tf_op jit(solution)/shard_map/ppermute | solution.py:147
  34.2 4.5 %collective-permute-start.1 = (bf16[4,6,8,1024]{3,2,1,0:T(8,128)(2,1)S(1)}, bf16[4,6,8,1024]{3,2,1,0:T(8,128)(2,1)S(1)}, u32[]{:S(2)}, u32[]{:S(2)}) collective-permute-start(bf16[4,6,8,1024]{3,2,1,0:T(8,128)(2,1)S(1)} %bitcast.19), channel_id=1, source_target_pairs={{0,480},{4,36},{8,488},{12,44},{16,496},{20,52},{24,504},{28,60},{... | collective-permute-start | bytes 1179656 | tf_op jit(solution)/shard_map/ppermute | solution.py:147
  38.7 1.9 %collective-permute-start.2 = (bf16[2,6,8,1024]{3,2,1,0:T(8,128)(2,1)S(1)}, bf16[2,6,8,1024]{3,2,1,0:T(8,128)(2,1)S(1)}, u32[]{:S(2)}, u32[]{:S(2)}) collective-permute-start(bf16[2,6,8,1024]{3,2,1,0:T(8,128)(2,1)S(1)} %bitcast.24), channel_id=1, source_target_pairs={{0,64},{4,452},{8,72},{12,460},{16,80},{20,468},{24,88},{28,476},{... | collective-permute-start | bytes 589832 | tf_op jit(solution)/shard_map/ppermute | solution.py:147
  40.7 6.0 %collective-permute-start.3 = (bf16[2,6,8,1024]{3,2,1,0:T(8,128)(2,1)S(1)}, bf16[2,6,8,1024]{3,2,1,0:T(8,128)(2,1)S(1)}, u32[]{:S(2)}, u32[]{:S(2)}) collective-permute-start(bf16[2,6,8,1024]{3,2,1,0:T(8,128)(2,1)S(1)} %bitcast.23), channel_id=1, source_target_pairs={{0,448},{4,68},{8,456},{12,76},{16,464},{20,84},{24,472},{28,92},{... | collective-permute-start | bytes 589832 | tf_op jit(solution)/shard_map/ppermute | solution.py:147
  46.7 1.3 %codes.1 = s32[8,16]{1,0:T(8,128)} custom-call(s32[1]{0:T(128)} %bitcast.plane_ref, s32[1,16]{1,0:T(1,128)} %bitcast.26, s32[1,16]{1,0:T(1,128)} %bitcast.27, s32[1,16]{1,0:T(1,128)} %bitcast.28), custom_call_target="tpu_custom_call" | custom-call | flops 10000000000 | bytes 1000000 | tf_op jit(solution)/shard_map/codes/pallas_call | solution.py:157
  48.0 4.9 %all-to-all-start = ((s32[8,1,16]{2,1,0:T(1,128)}), s32[8,1,16]{2,1,0:T(1,128)S(1)}, u32[]{:S(2)}, u32[]{:S(2)}) async-start(s32[8,1,16]{2,1,0:T(1,128)} %bitcast.25), calls=%async_computation | async-start | bytes 8192 | tf_op jit(solution)/shard_map/all_to_all | solution.py:165
  52.9 0.1 subtract_multiply_fusion.scale_ref
  53.1 3.6 %all-to-all-done = s32[8,1,16]{2,1,0:T(1,128)S(1)} async-done(((s32[8,1,16]{2,1,0:T(1,128)}), s32[8,1,16]{2,1,0:T(1,128)S(1)}, u32[]{:S(2)}, u32[]{:S(2)}) %all-to-all-start) | async-done | bytes 544 | tf_op jit(solution)/shard_map/all_to_all | solution.py:165
  56.7 0.0 collective-permute-done.2.third_ref
  56.7 0.0 collective-permute-done.3.fourth_ref
  56.7 0.0 collective-permute-done.first_ref
  56.7 0.0 collective-permute-done.1.second_ref
  56.7 1.6 %stage.1 = (bf16[2048,512]{1,0:T(8,128)(2,1)S(1)}, bf16[1024,128]{1,0:T(8,128)(2,1)S(1)}, bf16[6,128,1024]{2,1,0:T(8,128)(2,1)S(1)}, bf16[2,128,128]{2,1,0:T(8,128)(2,1)S(1)}) custom-call(s32[1]{0:T(128)} %bitcast.12.grp_ref, s32[8,16]{1,0:T(8,128)S(1)} %bitcast.21, bf16[4,6,8,1024]{3,2,1,0:T(8,128)(2,1)S(1)} %bitcast.20, ...), custom_call_target="tpu_custom_call" | custom-call | tf_op jit(solution)/shard_map/stage/pallas_call | solution.py:169
  58.3 2.4 %correlate.3 = bf16[4,4,9,16,256]{4,3,2,1,0:T(8,128)(2,1)S(1)} custom-call(bf16[2,128,128]{2,1,0:T(8,128)(2,1)S(1)} %get-tuple-element.27.pick, bf16[6,128,1024]{2,1,0:T(8,128)(2,1)S(1)} %get-tuple-element.28.stations, bf16[2048,512]{1,0:T(8,128)(2,1)S(1)} %get-tuple-element.29.table, bf16[1024,128]{1,0:T(8,128)(2,1)S(1)} %get-tuple-element.30.edge), custom_call_target="tpu_custom_call" | custom-call | tf_op jit(solution)/shard_map/correlate/pallas_call | solution.py:189
  60.7 1.9 %collective-permute-start.4 = (bf16[4,4,9,16,256]{4,3,2,1,0:T(8,128)(2,1)S(1)}, bf16[4,4,9,16,256]{4,3,2,1,0:T(8,128)(2,1)S(1)}, u32[]{:S(2)}, u32[]{:S(2)}) collective-permute-start(bf16[4,4,9,16,256]{4,3,2,1,0:T(8,128)(2,1)S(1)} %correlate.3), channel_id=1, source_target_pairs={{0,4},{4,0},{8,12},{12,8},{16,20},{20,16},{24,28},{28,24},{1,5},{5... | collective-permute-start | bytes 3538952 | tf_op jit(solution)/shard_map/ppermute | solution.py:201
  62.6 2.4 %correlate.2 = f32[4,4,9,16,256]{4,3,2,1,0:T(8,128)S(1)} custom-call(bf16[2,128,128]{2,1,0:T(8,128)(2,1)S(1)} %get-tuple-element.27.pick, bf16[6,128,1024]{2,1,0:T(8,128)(2,1)S(1)} %get-tuple-element.28.stations, bf16[2048,512]{1,0:T(8,128)(2,1)S(1)} %get-tuple-element.29.table, bf16[1024,128]{1,0:T(8,128)(2,1)S(1)} %get-tuple-element.30.edge), custom_call_target="tpu_custom_call" | custom-call | tf_op jit(solution)/shard_map/correlate/pallas_call | solution.py:189
  65.0 0.4 collective-permute-done.4
  65.5 0.4 add_convert_fusion
  65.9 23.4 %all_to_all.17 = bf16[16,9,16,256]{3,2,1,0:T(8,128)(2,1)S(1)} all-to-all(bf16[16,9,16,256]{3,2,1,0:T(8,128)(2,1)S(1)} %bitcast.22), channel_id=1, replica_groups={{0,1,2,3,8,9,10,11,16,17,18,19,24,25,26,27},{4,5,6,7,12,13,14,15,20,21,..., dimensions={0} | all-to-all | bytes 2359296 | tf_op jit(solution)/shard_map/all_to_all | solution.py:204
  89.2 0.2 reduce_sum.12
  89.4 12.5 %all_gather.11.x_ref = bf16[9,16,1024]{2,1,0:T(8,128)(2,1)S(1)} all-gather(bf16[9,16,256]{2,1,0:T(8,128)(2,1)S(1)} %reduce_sum.12), channel_id=1, replica_groups=mesh['sta'=16,'grp'=8,'hr'=4] {'hr'}, dimensions={2}, use_global_device_ids=true | all-gather | bytes 368640 | tf_op jit(solution)/shard_map/all_gather | solution.py:206
  101.9 1.1 %unfold.1 = f32[9,16,1024]{2,1,0:T(8,128)} custom-call(f32[1,1024]{1,0:T(1,128)S(1)} %subtract_multiply_fusion.scale_ref, bf16[9,16,1024]{2,1,0:T(8,128)(2,1)S(1)} %all_gather.11.x_ref), custom_call_target="tpu_custom_call" | custom-call | tf_op jit(solution)/shard_map/unfold/pallas_call | solution.py:207
  (3 shorter events, 0.0 us)
Async XLA Ops:
  0.0 1.1 %copy-start = (bf16[1,8,6,8192]{3,1,2,0:T(8,128)(2,1)S(1)}, bf16[1,8,6,8192]{3,1,2,0:T(8,128)(2,1)}, u32[]{:S(2)}) copy-start(bf16[1,8,6,8192]{3,1,2,0:T(8,128)(2,1)} %param.4) | copy-start | bytes 2359300
  31.6 25.0 %collective-permute-start = (bf16[4,6,8,1024]{3,2,1,0:T(8,128)(2,1)S(1)}, bf16[4,6,8,1024]{3,2,1,0:T(8,128)(2,1)S(1)}, u32[]{:S(2)}, u32[]{:S(2)}) collective-permute-start(bf16[4,6,8,1024]{3,2,1,0:T(8,128)(2,1)S(1)} %bitcast.18), channel_id=1, source_target_pairs={{0,32},{4,484},{8,40},{12,492},{16,48},{20,500},{24,56},{28,508},{... | collective-permute-start | bytes 1179656 | tf_op jit(solution)/shard_map/ppermute | solution.py:147
  34.2 22.5 %collective-permute-start.1 = (bf16[4,6,8,1024]{3,2,1,0:T(8,128)(2,1)S(1)}, bf16[4,6,8,1024]{3,2,1,0:T(8,128)(2,1)S(1)}, u32[]{:S(2)}, u32[]{:S(2)}) collective-permute-start(bf16[4,6,8,1024]{3,2,1,0:T(8,128)(2,1)S(1)} %bitcast.19), channel_id=1, source_target_pairs={{0,480},{4,36},{8,488},{12,44},{16,496},{20,52},{24,504},{28,60},{... | collective-permute-start | bytes 1179656 | tf_op jit(solution)/shard_map/ppermute | solution.py:147
  38.7 17.9 %collective-permute-start.2 = (bf16[2,6,8,1024]{3,2,1,0:T(8,128)(2,1)S(1)}, bf16[2,6,8,1024]{3,2,1,0:T(8,128)(2,1)S(1)}, u32[]{:S(2)}, u32[]{:S(2)}) collective-permute-start(bf16[2,6,8,1024]{3,2,1,0:T(8,128)(2,1)S(1)} %bitcast.24), channel_id=1, source_target_pairs={{0,64},{4,452},{8,72},{12,460},{16,80},{20,468},{24,88},{28,476},{... | collective-permute-start | bytes 589832 | tf_op jit(solution)/shard_map/ppermute | solution.py:147
  40.7 16.0 %collective-permute-start.3 = (bf16[2,6,8,1024]{3,2,1,0:T(8,128)(2,1)S(1)}, bf16[2,6,8,1024]{3,2,1,0:T(8,128)(2,1)S(1)}, u32[]{:S(2)}, u32[]{:S(2)}) collective-permute-start(bf16[2,6,8,1024]{3,2,1,0:T(8,128)(2,1)S(1)} %bitcast.23), channel_id=1, source_target_pairs={{0,448},{4,68},{8,456},{12,76},{16,464},{20,84},{24,472},{28,92},{... | collective-permute-start | bytes 589832 | tf_op jit(solution)/shard_map/ppermute | solution.py:147
  48.0 8.6 %all-to-all-start = ((s32[8,1,16]{2,1,0:T(1,128)}), s32[8,1,16]{2,1,0:T(1,128)S(1)}, u32[]{:S(2)}, u32[]{:S(2)}) async-start(s32[8,1,16]{2,1,0:T(1,128)} %bitcast.25), calls=%async_computation | async-start | bytes 8192 | tf_op jit(solution)/shard_map/all_to_all | solution.py:165
  60.7 4.7 %collective-permute-start.4 = (bf16[4,4,9,16,256]{4,3,2,1,0:T(8,128)(2,1)S(1)}, bf16[4,4,9,16,256]{4,3,2,1,0:T(8,128)(2,1)S(1)}, u32[]{:S(2)}, u32[]{:S(2)}) collective-permute-start(bf16[4,4,9,16,256]{4,3,2,1,0:T(8,128)(2,1)S(1)} %correlate.3), channel_id=1, source_target_pairs={{0,4},{4,0},{8,12},{12,8},{16,20},{20,16},{24,28},{28,24},{1,5},{5... | collective-permute-start | bytes 3538952 | tf_op jit(solution)/shard_map/ppermute | solution.py:201

commit v13 on v12

--- a/solution.py
+++ b/solution.py
@@ -137,31 +137,31 @@
 
 def body(spectra, pair_source, pair_owner, pair_row):
     s, g = lax.axis_index("sta"), lax.axis_index("grp")
-    mine = lax.dynamic_slice_in_dim(spectra[0], g * W, W, 2).transpose(1, 0, 2)
-    planes = [list(range(p, NZ, NR)) for p in range(NR)]
-    near = lax.all_gather(mine, "sta", axis=0, axis_index_groups=planes)
-
-    def neighbour(x, step):
-        turn = [step if i % NC == 0 else -step for i in range(NG)]
-        perm = [(z * NG + i, (z + turn[i]) % NZ * NG + i) for z in range(NZ) for i in range(NG)]
-        return lax.ppermute(x, ("sta", "grp"), perm)
-
-    pos = jnp.arange(LAGS, dtype=jnp.float32)[None]
-    taper = 0.75 - 0.25 * jnp.cos(TWO_PI * (pos + 0.5) / LAGS)
-    scale = taper / (NX * math.sqrt(NB))
-    half = NZ // NR // 2
-    low, high, pair_row = lax.optimization_barrier((near[:half], near[half:], pair_row))
-    moved = (neighbour(near, 1), neighbour(near, -1), neighbour(low, 2), neighbour(high, -2))
-
     smem = pl.BlockSpec(memory_space=pltpu.SMEM)
     code = pl.pallas_call(
         codes,
         out_shape=jax.ShapeDtypeStruct((NG, PD), jnp.int32),
         in_specs=[smem] + vmem(3),
         out_specs=vmem(1)[0],
-        cost_estimate=pl.CostEstimate(flops=10**10, bytes_accessed=10**6, transcendentals=0),
         name="codes",
     )(s[None], pair_source[None], pair_owner.T, pair_row[None])
+
+    spectra, code = lax.optimization_barrier((spectra, code))
+    mine = lax.dynamic_slice_in_dim(spectra[0], g * W, W, 2).transpose(1, 0, 2)
+    planes = [list(range(p, NZ, NR)) for p in range(NR)]
+    near = lax.all_gather(mine, "sta", axis=0, axis_index_groups=planes)
+
+    def neighbour(x, step):
+        turn = [step if i % NC == 0 else -step for i in range(NG)]
+        perm = [(z * NG + i, (z + turn[i]) % NZ * NG + i) for z in range(NZ) for i in range(NG)]
+        return lax.ppermute(x, ("sta", "grp"), perm)
+
+    pos = jnp.arange(LAGS, dtype=jnp.float32)[None]
+    taper = 0.75 - 0.25 * jnp.cos(TWO_PI * (pos + 0.5) / LAGS)
+    scale = taper / (NX * math.sqrt(NB))
+    half = NZ // NR // 2
+    low, high, code = lax.optimization_barrier((near[:half], near[half:], code))
+    moved = (neighbour(near, 1), neighbour(near, -1), neighbour(low, 2), neighbour(high, -2))
     code = lax.all_to_all(code, "grp", 0, 0, tiled=True)
     code, moved, scale = lax.optimization_barrier((code, moved, scale))
 

time: 103 us -> 102 us (level)
  local copies, waits for them, and re-layouts: 1.17 us -> 0.04 us
    unnamed x2, local copies, waits for them, and re-layouts: 1.13 us -> 0.01 us
  transfers between devices with their start and end apart: 6 -> 6, of which waited for: 2 -> 2; matrix products, arithmetic and copies ran while one was open for 0% -> 0% of each run, Pallas kernels for 4% -> 2%
where the time goes in v13:
time: 102 us
  blocking collectives  66.4 us (65%)
  starting transfers between devices  21.8 us (21%)
  Pallas kernels  8.94 us (9%)
  waiting for transfers between devices  3.99 us (4%)
    all_gather x1, blocking collectives, body(): near = lax.all_gather(mine, 'sta', axis=0, axis_index_groups=planes)  30.5 us
    all_to_all x1, blocking collectives, body(): lax.all_to_all(part, ('grp', 'hr'), 0, 0, axis_index_groups=chips, tiled=...  23.4 us
    ppermute x4, starting transfers between devices, neighbour(): return lax.ppermute(x, ('sta', 'grp'), perm)  15 us
    all_gather x1, blocking collectives, body(): total = lax.all_gather(total, 'hr', axis=2, tiled=True)  12.5 us
    all_to_all x1, starting transfers between devices, body(): code = lax.all_to_all(code, 'grp', 0, 0, tiled=True)  4.93 us
    pallas_call x2, Pallas kernels, lags(): pl.pallas_call(functools.partial(correlate, half), out_shape=jax.ShapeDty...  4.81 us
    all_to_all x1, waiting for transfers between devices, body(): code = lax.all_to_all(code, 'grp', 0, 0, tiled=True)  3.59 us
  transfers between devices with their start and end apart: 6, of which 2 were waited for; matrix products, arithmetic and copies ran while one was open for 0% of the time, Pallas kernels for 2%

profile of v13, /device:TPU:8, one launch (start us, length us, event | category | flops | bytes accessed | tf_op | source)
XLA Modules:
  0.0 102.0 jit_solution(8873737883403478036)
XLA Ops:
  0.0 1.4 %codes.1 = s32[8,16]{1,0:T(8,128)} custom-call(s32[1]{0:T(128)} %bitcast.plane_ref, s32[1,16]{1,0:T(1,128)} %bitcast.26, s32[1,16]{1,0:T(1,128)} %bitcast.27, s32[1,16]{1,0:T(1,128)} %bitcast.28), custom_call_target="tpu_custom_call" | custom-call | tf_op jit(solution)/shard_map/codes/pallas_call | solution.py:141
  1.4 0.0 copy-done
  1.4 30.5 %all-gather = bf16[24,8,1024]{2,1,0:T(8,128)(2,1)S(1)} all-gather(bf16[6,8,1024]{2,1,0:T(8,128)(2,1)S(1)} %dynamic-slice_bitcast_fusion), channel_id=2, replica_groups={{0,128,256,384},{32,160,288,416},{64,192,320,448},{96,224,352,480},{1,1..., dimensions={0}, use_global_device_ids=true | all-gather | bytes 491520 | tf_op jit(solution)/shard_map/all_gather | solution.py:152
  31.9 2.5 %collective-permute-start = (bf16[4,6,8,1024]{3,2,1,0:T(8,128)(2,1)S(1)}, bf16[4,6,8,1024]{3,2,1,0:T(8,128)(2,1)S(1)}, u32[]{:S(2)}, u32[]{:S(2)}) collective-permute-start(bf16[4,6,8,1024]{3,2,1,0:T(8,128)(2,1)S(1)} %bitcast.18), channel_id=1, source_target_pairs={{0,32},{4,484},{8,40},{12,492},{16,48},{20,500},{24,56},{28,508},{... | collective-permute-start | bytes 1179656 | tf_op jit(solution)/shard_map/ppermute | solution.py:157
  34.4 4.5 %collective-permute-start.1 = (bf16[4,6,8,1024]{3,2,1,0:T(8,128)(2,1)S(1)}, bf16[4,6,8,1024]{3,2,1,0:T(8,128)(2,1)S(1)}, u32[]{:S(2)}, u32[]{:S(2)}) collective-permute-start(bf16[4,6,8,1024]{3,2,1,0:T(8,128)(2,1)S(1)} %bitcast.19), channel_id=1, source_target_pairs={{0,480},{4,36},{8,488},{12,44},{16,496},{20,52},{24,504},{28,60},{... | collective-permute-start | bytes 1179656 | tf_op jit(solution)/shard_map/ppermute | solution.py:157
  39.0 1.9 %collective-permute-start.2 = (bf16[2,6,8,1024]{3,2,1,0:T(8,128)(2,1)S(1)}, bf16[2,6,8,1024]{3,2,1,0:T(8,128)(2,1)S(1)}, u32[]{:S(2)}, u32[]{:S(2)}) collective-permute-start(bf16[2,6,8,1024]{3,2,1,0:T(8,128)(2,1)S(1)} %bitcast.24), channel_id=1, source_target_pairs={{0,64},{4,452},{8,72},{12,460},{16,80},{20,468},{24,88},{28,476},{... | collective-permute-start | bytes 589832 | tf_op jit(solution)/shard_map/ppermute | solution.py:157
  40.9 6.0 %collective-permute-start.3 = (bf16[2,6,8,1024]{3,2,1,0:T(8,128)(2,1)S(1)}, bf16[2,6,8,1024]{3,2,1,0:T(8,128)(2,1)S(1)}, u32[]{:S(2)}, u32[]{:S(2)}) collective-permute-start(bf16[2,6,8,1024]{3,2,1,0:T(8,128)(2,1)S(1)} %bitcast.23), channel_id=1, source_target_pairs={{0,448},{4,68},{8,456},{12,76},{16,464},{20,84},{24,472},{28,92},{... | collective-permute-start | bytes 589832 | tf_op jit(solution)/shard_map/ppermute | solution.py:157
  47.0 4.9 %all-to-all-start = ((s32[8,1,16]{2,1,0:T(1,128)}), s32[8,1,16]{2,1,0:T(1,128)S(1)}, u32[]{:S(2)}, u32[]{:S(2)}) async-start(s32[8,1,16]{2,1,0:T(1,128)} %bitcast.25), calls=%async_computation | async-start | bytes 8192 | tf_op jit(solution)/shard_map/all_to_all | solution.py:165
  51.9 0.1 subtract_multiply_fusion.scale_ref
  52.0 3.6 %all-to-all-done = s32[8,1,16]{2,1,0:T(1,128)S(1)} async-done(((s32[8,1,16]{2,1,0:T(1,128)}), s32[8,1,16]{2,1,0:T(1,128)S(1)}, u32[]{:S(2)}, u32[]{:S(2)}) %all-to-all-start) | async-done | bytes 544 | tf_op jit(solution)/shard_map/all_to_all | solution.py:165
  55.6 0.0 collective-permute-done.2.third_ref
  55.6 0.0 collective-permute-done.3.fourth_ref
  55.6 0.0 collective-permute-done.first_ref
  55.6 0.0 collective-permute-done.1.second_ref
  55.6 1.6 %stage.1 = (bf16[2048,512]{1,0:T(8,128)(2,1)S(1)}, bf16[1024,128]{1,0:T(8,128)(2,1)S(1)}, bf16[6,128,1024]{2,1,0:T(8,128)(2,1)S(1)}, bf16[2,128,128]{2,1,0:T(8,128)(2,1)S(1)}) custom-call(s32[1]{0:T(128)} %bitcast.12.grp_ref, s32[8,16]{1,0:T(8,128)S(1)} %bitcast.21, bf16[4,6,8,1024]{3,2,1,0:T(8,128)(2,1)S(1)} %bitcast.20, ...), custom_call_target="tpu_custom_call" | custom-call | tf_op jit(solution)/shard_map/stage/pallas_call | solution.py:169
  57.3 2.4 %correlate.3 = bf16[4,4,9,16,256]{4,3,2,1,0:T(8,128)(2,1)S(1)} custom-call(bf16[2,128,128]{2,1,0:T(8,128)(2,1)S(1)} %get-tuple-element.31.pick, bf16[6,128,1024]{2,1,0:T(8,128)(2,1)S(1)} %get-tuple-element.32.stations, bf16[2048,512]{1,0:T(8,128)(2,1)S(1)} %get-tuple-element.33.table, bf16[1024,128]{1,0:T(8,128)(2,1)S(1)} %get-tuple-element.34.edge), custom_call_target="tpu_custom_call" | custom-call | tf_op jit(solution)/shard_map/correlate/pallas_call | solution.py:189
  59.7 1.9 %collective-permute-start.4 = (bf16[4,4,9,16,256]{4,3,2,1,0:T(8,128)(2,1)S(1)}, bf16[4,4,9,16,256]{4,3,2,1,0:T(8,128)(2,1)S(1)}, u32[]{:S(2)}, u32[]{:S(2)}) collective-permute-start(bf16[4,4,9,16,256]{4,3,2,1,0:T(8,128)(2,1)S(1)} %correlate.3), channel_id=1, source_target_pairs={{0,4},{4,0},{8,12},{12,8},{16,20},{20,16},{24,28},{28,24},{1,5},{5... | collective-permute-start | bytes 3538952 | tf_op jit(solution)/shard_map/ppermute | solution.py:201
  61.6 2.4 %correlate.2 = f32[4,4,9,16,256]{4,3,2,1,0:T(8,128)S(1)} custom-call(bf16[2,128,128]{2,1,0:T(8,128)(2,1)S(1)} %get-tuple-element.31.pick, bf16[6,128,1024]{2,1,0:T(8,128)(2,1)S(1)} %get-tuple-element.32.stations, bf16[2048,512]{1,0:T(8,128)(2,1)S(1)} %get-tuple-element.33.table, bf16[1024,128]{1,0:T(8,128)(2,1)S(1)} %get-tuple-element.34.edge), custom_call_target="tpu_custom_call" | custom-call | tf_op jit(solution)/shard_map/correlate/pallas_call | solution.py:189
  64.0 0.4 collective-permute-done.4
  64.4 0.4 add_convert_fusion
  64.8 23.4 %all_to_all.17 = bf16[16,9,16,256]{3,2,1,0:T(8,128)(2,1)S(1)} all-to-all(bf16[16,9,16,256]{3,2,1,0:T(8,128)(2,1)S(1)} %bitcast.22), channel_id=1, replica_groups={{0,1,2,3,8,9,10,11,16,17,18,19,24,25,26,27},{4,5,6,7,12,13,14,15,20,21,..., dimensions={0} | all-to-all | bytes 2359296 | tf_op jit(solution)/shard_map/all_to_all | solution.py:204
  88.2 0.2 reduce_sum.12
  88.4 12.5 %all_gather.11.x_ref = bf16[9,16,1024]{2,1,0:T(8,128)(2,1)S(1)} all-gather(bf16[9,16,256]{2,1,0:T(8,128)(2,1)S(1)} %reduce_sum.12), channel_id=1, replica_groups=mesh['sta'=16,'grp'=8,'hr'=4] {'hr'}, dimensions={2}, use_global_device_ids=true | all-gather | bytes 368640 | tf_op jit(solution)/shard_map/all_gather | solution.py:206
  100.9 1.1 %unfold.1 = f32[9,16,1024]{2,1,0:T(8,128)} custom-call(f32[1,1024]{1,0:T(1,128)S(1)} %subtract_multiply_fusion.scale_ref, bf16[9,16,1024]{2,1,0:T(8,128)(2,1)S(1)} %all_gather.11.x_ref), custom_call_target="tpu_custom_call" | custom-call | tf_op jit(solution)/shard_map/unfold/pallas_call | solution.py:207
  (3 shorter events, 0.0 us)
Async XLA Ops:
  0.0 1.4 %copy-start = (bf16[1,8,6,8192]{3,1,2,0:T(8,128)(2,1)S(1)}, bf16[1,8,6,8192]{3,1,2,0:T(8,128)(2,1)}, u32[]{:S(2)}) copy-start(bf16[1,8,6,8192]{3,1,2,0:T(8,128)(2,1)} %param.4) | copy-start | bytes 2359300
  31.9 23.7 %collective-permute-start = (bf16[4,6,8,1024]{3,2,1,0:T(8,128)(2,1)S(1)}, bf16[4,6,8,1024]{3,2,1,0:T(8,128)(2,1)S(1)}, u32[]{:S(2)}, u32[]{:S(2)}) collective-permute-start(bf16[4,6,8,1024]{3,2,1,0:T(8,128)(2,1)S(1)} %bitcast.18), channel_id=1, source_target_pairs={{0,32},{4,484},{8,40},{12,492},{16,48},{20,500},{24,56},{28,508},{... | collective-permute-start | bytes 1179656 | tf_op jit(solution)/shard_map/ppermute | solution.py:157
  34.4 21.2 %collective-permute-start.1 = (bf16[4,6,8,1024]{3,2,1,0:T(8,128)(2,1)S(1)}, bf16[4,6,8,1024]{3,2,1,0:T(8,128)(2,1)S(1)}, u32[]{:S(2)}, u32[]{:S(2)}) collective-permute-start(bf16[4,6,8,1024]{3,2,1,0:T(8,128)(2,1)S(1)} %bitcast.19), channel_id=1, source_target_pairs={{0,480},{4,36},{8,488},{12,44},{16,496},{20,52},{24,504},{28,60},{... | collective-permute-start | bytes 1179656 | tf_op jit(solution)/shard_map/ppermute | solution.py:157
  39.0 16.6 %collective-permute-start.2 = (bf16[2,6,8,1024]{3,2,1,0:T(8,128)(2,1)S(1)}, bf16[2,6,8,1024]{3,2,1,0:T(8,128)(2,1)S(1)}, u32[]{:S(2)}, u32[]{:S(2)}) collective-permute-start(bf16[2,6,8,1024]{3,2,1,0:T(8,128)(2,1)S(1)} %bitcast.24), channel_id=1, source_target_pairs={{0,64},{4,452},{8,72},{12,460},{16,80},{20,468},{24,88},{28,476},{... | collective-permute-start | bytes 589832 | tf_op jit(solution)/shard_map/ppermute | solution.py:157
  40.9 14.7 %collective-permute-start.3 = (bf16[2,6,8,1024]{3,2,1,0:T(8,128)(2,1)S(1)}, bf16[2,6,8,1024]{3,2,1,0:T(8,128)(2,1)S(1)}, u32[]{:S(2)}, u32[]{:S(2)}) collective-permute-start(bf16[2,6,8,1024]{3,2,1,0:T(8,128)(2,1)S(1)} %bitcast.23), channel_id=1, source_target_pairs={{0,448},{4,68},{8,456},{12,76},{16,464},{20,84},{24,472},{28,92},{... | collective-permute-start | bytes 589832 | tf_op jit(solution)/shard_map/ppermute | solution.py:157
  47.0 8.7 %all-to-all-start = ((s32[8,1,16]{2,1,0:T(1,128)}), s32[8,1,16]{2,1,0:T(1,128)S(1)}, u32[]{:S(2)}, u32[]{:S(2)}) async-start(s32[8,1,16]{2,1,0:T(1,128)} %bitcast.25), calls=%async_computation | async-start | bytes 8192 | tf_op jit(solution)/shard_map/all_to_all | solution.py:165
  59.7 4.7 %collective-permute-start.4 = (bf16[4,4,9,16,256]{4,3,2,1,0:T(8,128)(2,1)S(1)}, bf16[4,4,9,16,256]{4,3,2,1,0:T(8,128)(2,1)S(1)}, u32[]{:S(2)}, u32[]{:S(2)}) collective-permute-start(bf16[4,4,9,16,256]{4,3,2,1,0:T(8,128)(2,1)S(1)} %correlate.3), channel_id=1, source_target_pairs={{0,4},{4,0},{8,12},{12,8},{16,20},{20,16},{24,28},{28,24},{1,5},{5... | collective-permute-start | bytes 3538952 | tf_op jit(solution)/shard_map/ppermute | solution.py:201

commit v14 on v13

--- a/solution.py
+++ b/solution.py
@@ -17,7 +17,7 @@
 FINE = 32
 HALF = NY * PD
 CH = 128
-PC = 256
+PC = 512
 TN = LAGS // 2
 TA = TN + CH
 TW = LAGS // NX

time: 102 us -> 102 us (level)
  no operation moved by 1% of the time
where the time goes in v14:
time: 102 us
  blocking collectives  66.4 us (65%)
  starting transfers between devices  21.8 us (21%)
  Pallas kernels  9.15 us (9%)
  waiting for transfers between devices  3.89 us (4%)
    all_gather x1, blocking collectives, body(): near = lax.all_gather(mine, 'sta', axis=0, axis_index_groups=planes)  30.5 us
    all_to_all x1, blocking collectives, body(): lax.all_to_all(part, ('grp', 'hr'), 0, 0, axis_index_groups=chips, tiled=...  23.4 us
    ppermute x4, starting transfers between devices, neighbour(): return lax.ppermute(x, ('sta', 'grp'), perm)  15 us
    all_gather x1, blocking collectives, body(): total = lax.all_gather(total, 'hr', axis=2, tiled=True)  12.5 us
    pallas_call x2, Pallas kernels, lags(): pl.pallas_call(functools.partial(correlate, half), out_shape=jax.ShapeDty...  5.03 us
    all_to_all x1, starting transfers between devices, body(): code = lax.all_to_all(code, 'grp', 0, 0, tiled=True)  4.93 us
    all_to_all x1, waiting for transfers between devices, body(): code = lax.all_to_all(code, 'grp', 0, 0, tiled=True)  3.59 us
  transfers between devices with their start and end apart: 6, of which 2 were waited for; matrix products, arithmetic and copies ran while one was open for 0% of the time, Pallas kernels for 2%

profile of v14, /device:TPU:8, one launch (start us, length us, event | category | flops | bytes accessed | tf_op | source)
XLA Modules:
  0.0 102.2 jit_solution(9288487827126406508)
XLA Ops:
  0.0 1.4 %codes.1 = s32[8,16]{1,0:T(8,128)} custom-call(s32[1]{0:T(128)} %bitcast.plane_ref, s32[1,16]{1,0:T(1,128)} %bitcast.26, s32[1,16]{1,0:T(1,128)} %bitcast.27, s32[1,16]{1,0:T(1,128)} %bitcast.28), custom_call_target="tpu_custom_call" | custom-call | tf_op jit(solution)/shard_map/codes/pallas_call | solution.py:141
  1.4 0.0 copy-done
  1.4 30.5 %all-gather = bf16[24,8,1024]{2,1,0:T(8,128)(2,1)S(1)} all-gather(bf16[6,8,1024]{2,1,0:T(8,128)(2,1)S(1)} %dynamic-slice_bitcast_fusion), channel_id=2, replica_groups={{0,128,256,384},{32,160,288,416},{64,192,320,448},{96,224,352,480},{1,1..., dimensions={0}, use_global_device_ids=true | all-gather | bytes 491520 | tf_op jit(solution)/shard_map/all_gather | solution.py:152
  31.9 2.5 %collective-permute-start = (bf16[4,6,8,1024]{3,2,1,0:T(8,128)(2,1)S(1)}, bf16[4,6,8,1024]{3,2,1,0:T(8,128)(2,1)S(1)}, u32[]{:S(2)}, u32[]{:S(2)}) collective-permute-start(bf16[4,6,8,1024]{3,2,1,0:T(8,128)(2,1)S(1)} %bitcast.18), channel_id=1, source_target_pairs={{0,32},{4,484},{8,40},{12,492},{16,48},{20,500},{24,56},{28,508},{... | collective-permute-start | bytes 1179656 | tf_op jit(solution)/shard_map/ppermute | solution.py:157
  34.4 4.5 %collective-permute-start.1 = (bf16[4,6,8,1024]{3,2,1,0:T(8,128)(2,1)S(1)}, bf16[4,6,8,1024]{3,2,1,0:T(8,128)(2,1)S(1)}, u32[]{:S(2)}, u32[]{:S(2)}) collective-permute-start(bf16[4,6,8,1024]{3,2,1,0:T(8,128)(2,1)S(1)} %bitcast.19), channel_id=1, source_target_pairs={{0,480},{4,36},{8,488},{12,44},{16,496},{20,52},{24,504},{28,60},{... | collective-permute-start | bytes 1179656 | tf_op jit(solution)/shard_map/ppermute | solution.py:157
  39.0 1.9 %collective-permute-start.2 = (bf16[2,6,8,1024]{3,2,1,0:T(8,128)(2,1)S(1)}, bf16[2,6,8,1024]{3,2,1,0:T(8,128)(2,1)S(1)}, u32[]{:S(2)}, u32[]{:S(2)}) collective-permute-start(bf16[2,6,8,1024]{3,2,1,0:T(8,128)(2,1)S(1)} %bitcast.24), channel_id=1, source_target_pairs={{0,64},{4,452},{8,72},{12,460},{16,80},{20,468},{24,88},{28,476},{... | collective-permute-start | bytes 589832 | tf_op jit(solution)/shard_map/ppermute | solution.py:157
  40.9 6.0 %collective-permute-start.3 = (bf16[2,6,8,1024]{3,2,1,0:T(8,128)(2,1)S(1)}, bf16[2,6,8,1024]{3,2,1,0:T(8,128)(2,1)S(1)}, u32[]{:S(2)}, u32[]{:S(2)}) collective-permute-start(bf16[2,6,8,1024]{3,2,1,0:T(8,128)(2,1)S(1)} %bitcast.23), channel_id=1, source_target_pairs={{0,448},{4,68},{8,456},{12,76},{16,464},{20,84},{24,472},{28,92},{... | collective-permute-start | bytes 589832 | tf_op jit(solution)/shard_map/ppermute | solution.py:157
  47.0 4.9 %all-to-all-start = ((s32[8,1,16]{2,1,0:T(1,128)}), s32[8,1,16]{2,1,0:T(1,128)S(1)}, u32[]{:S(2)}, u32[]{:S(2)}) async-start(s32[8,1,16]{2,1,0:T(1,128)} %bitcast.25), calls=%async_computation | async-start | bytes 8192 | tf_op jit(solution)/shard_map/all_to_all | solution.py:165
  51.9 0.1 subtract_multiply_fusion.scale_ref
  52.0 3.6 %all-to-all-done = s32[8,1,16]{2,1,0:T(1,128)S(1)} async-done(((s32[8,1,16]{2,1,0:T(1,128)}), s32[8,1,16]{2,1,0:T(1,128)S(1)}, u32[]{:S(2)}, u32[]{:S(2)}) %all-to-all-start) | async-done | bytes 544 | tf_op jit(solution)/shard_map/all_to_all | solution.py:165
  55.6 0.0 collective-permute-done.2.third_ref
  55.6 0.0 collective-permute-done.3.fourth_ref
  55.6 0.0 collective-permute-done.first_ref
  55.6 0.0 collective-permute-done.1.second_ref
  55.6 1.6 %stage.1 = (bf16[2048,512]{1,0:T(8,128)(2,1)S(1)}, bf16[1024,128]{1,0:T(8,128)(2,1)S(1)}, bf16[6,128,1024]{2,1,0:T(8,128)(2,1)S(1)}, bf16[2,128,128]{2,1,0:T(8,128)(2,1)S(1)}) custom-call(s32[1]{0:T(128)} %bitcast.12.grp_ref, s32[8,16]{1,0:T(8,128)S(1)} %bitcast.21, bf16[4,6,8,1024]{3,2,1,0:T(8,128)(2,1)S(1)} %bitcast.20, ...), custom_call_target="tpu_custom_call" | custom-call | tf_op jit(solution)/shard_map/stage/pallas_call | solution.py:169
  57.3 2.5 %correlate.3 = bf16[4,4,9,16,256]{4,3,2,1,0:T(8,128)(2,1)S(1)} custom-call(bf16[2,128,128]{2,1,0:T(8,128)(2,1)S(1)} %get-tuple-element.31.pick, bf16[6,128,1024]{2,1,0:T(8,128)(2,1)S(1)} %get-tuple-element.32.stations, bf16[2048,512]{1,0:T(8,128)(2,1)S(1)} %get-tuple-element.33.table, bf16[1024,128]{1,0:T(8,128)(2,1)S(1)} %get-tuple-element.34.edge), custom_call_target="tpu_custom_call" | custom-call | tf_op jit(solution)/shard_map/correlate/pallas_call | solution.py:189
  59.8 1.9 %collective-permute-start.4 = (bf16[4,4,9,16,256]{4,3,2,1,0:T(8,128)(2,1)S(1)}, bf16[4,4,9,16,256]{4,3,2,1,0:T(8,128)(2,1)S(1)}, u32[]{:S(2)}, u32[]{:S(2)}) collective-permute-start(bf16[4,4,9,16,256]{4,3,2,1,0:T(8,128)(2,1)S(1)} %correlate.3), channel_id=1, source_target_pairs={{0,4},{4,0},{8,12},{12,8},{16,20},{20,16},{24,28},{28,24},{1,5},{5... | collective-permute-start | bytes 3538952 | tf_op jit(solution)/shard_map/ppermute | solution.py:201
  61.7 2.5 %correlate.2 = f32[4,4,9,16,256]{4,3,2,1,0:T(8,128)S(1)} custom-call(bf16[2,128,128]{2,1,0:T(8,128)(2,1)S(1)} %get-tuple-element.31.pick, bf16[6,128,1024]{2,1,0:T(8,128)(2,1)S(1)} %get-tuple-element.32.stations, bf16[2048,512]{1,0:T(8,128)(2,1)S(1)} %get-tuple-element.33.table, bf16[1024,128]{1,0:T(8,128)(2,1)S(1)} %get-tuple-element.34.edge), custom_call_target="tpu_custom_call" | custom-call | tf_op jit(solution)/shard_map/correlate/pallas_call | solution.py:189
  64.3 0.3 collective-permute-done.4
  64.5 0.4 add_convert_fusion
  65.0 23.4 %all_to_all.17 = bf16[16,9,16,256]{3,2,1,0:T(8,128)(2,1)S(1)} all-to-all(bf16[16,9,16,256]{3,2,1,0:T(8,128)(2,1)S(1)} %bitcast.22), channel_id=1, replica_groups={{0,1,2,3,8,9,10,11,16,17,18,19,24,25,26,27},{4,5,6,7,12,13,14,15,20,21,..., dimensions={0} | all-to-all | bytes 2359296 | tf_op jit(solution)/shard_map/all_to_all | solution.py:204
  88.4 0.2 reduce_sum.12
  88.6 12.5 %all_gather.11.x_ref = bf16[9,16,1024]{2,1,0:T(8,128)(2,1)S(1)} all-gather(bf16[9,16,256]{2,1,0:T(8,128)(2,1)S(1)} %reduce_sum.12), channel_id=1, replica_groups=mesh['sta'=16,'grp'=8,'hr'=4] {'hr'}, dimensions={2}, use_global_device_ids=true | all-gather | bytes 368640 | tf_op jit(solution)/shard_map/all_gather | solution.py:206
  101.0 1.1 %unfold.1 = f32[9,16,1024]{2,1,0:T(8,128)} custom-call(f32[1,1024]{1,0:T(1,128)S(1)} %subtract_multiply_fusion.scale_ref, bf16[9,16,1024]{2,1,0:T(8,128)(2,1)S(1)} %all_gather.11.x_ref), custom_call_target="tpu_custom_call" | custom-call | tf_op jit(solution)/shard_map/unfold/pallas_call | solution.py:207
  (3 shorter events, 0.0 us)
Async XLA Ops:
  0.0 1.4 %copy-start = (bf16[1,8,6,8192]{3,1,2,0:T(8,128)(2,1)S(1)}, bf16[1,8,6,8192]{3,1,2,0:T(8,128)(2,1)}, u32[]{:S(2)}) copy-start(bf16[1,8,6,8192]{3,1,2,0:T(8,128)(2,1)} %param.4) | copy-start | bytes 2359300
  31.9 23.7 %collective-permute-start = (bf16[4,6,8,1024]{3,2,1,0:T(8,128)(2,1)S(1)}, bf16[4,6,8,1024]{3,2,1,0:T(8,128)(2,1)S(1)}, u32[]{:S(2)}, u32[]{:S(2)}) collective-permute-start(bf16[4,6,8,1024]{3,2,1,0:T(8,128)(2,1)S(1)} %bitcast.18), channel_id=1, source_target_pairs={{0,32},{4,484},{8,40},{12,492},{16,48},{20,500},{24,56},{28,508},{... | collective-permute-start | bytes 1179656 | tf_op jit(solution)/shard_map/ppermute | solution.py:157
  34.4 21.2 %collective-permute-start.1 = (bf16[4,6,8,1024]{3,2,1,0:T(8,128)(2,1)S(1)}, bf16[4,6,8,1024]{3,2,1,0:T(8,128)(2,1)S(1)}, u32[]{:S(2)}, u32[]{:S(2)}) collective-permute-start(bf16[4,6,8,1024]{3,2,1,0:T(8,128)(2,1)S(1)} %bitcast.19), channel_id=1, source_target_pairs={{0,480},{4,36},{8,488},{12,44},{16,496},{20,52},{24,504},{28,60},{... | collective-permute-start | bytes 1179656 | tf_op jit(solution)/shard_map/ppermute | solution.py:157
  39.0 16.6 %collective-permute-start.2 = (bf16[2,6,8,1024]{3,2,1,0:T(8,128)(2,1)S(1)}, bf16[2,6,8,1024]{3,2,1,0:T(8,128)(2,1)S(1)}, u32[]{:S(2)}, u32[]{:S(2)}) collective-permute-start(bf16[2,6,8,1024]{3,2,1,0:T(8,128)(2,1)S(1)} %bitcast.24), channel_id=1, source_target_pairs={{0,64},{4,452},{8,72},{12,460},{16,80},{20,468},{24,88},{28,476},{... | collective-permute-start | bytes 589832 | tf_op jit(solution)/shard_map/ppermute | solution.py:157
  40.9 14.7 %collective-permute-start.3 = (bf16[2,6,8,1024]{3,2,1,0:T(8,128)(2,1)S(1)}, bf16[2,6,8,1024]{3,2,1,0:T(8,128)(2,1)S(1)}, u32[]{:S(2)}, u32[]{:S(2)}) collective-permute-start(bf16[2,6,8,1024]{3,2,1,0:T(8,128)(2,1)S(1)} %bitcast.23), channel_id=1, source_target_pairs={{0,448},{4,68},{8,456},{12,76},{16,464},{20,84},{24,472},{28,92},{... | collective-permute-start | bytes 589832 | tf_op jit(solution)/shard_map/ppermute | solution.py:157
  47.0 8.7 %all-to-all-start = ((s32[8,1,16]{2,1,0:T(1,128)}), s32[8,1,16]{2,1,0:T(1,128)S(1)}, u32[]{:S(2)}, u32[]{:S(2)}) async-start(s32[8,1,16]{2,1,0:T(1,128)} %bitcast.25), calls=%async_computation | async-start | bytes 8192 | tf_op jit(solution)/shard_map/all_to_all | solution.py:165
  59.8 4.7 %collective-permute-start.4 = (bf16[4,4,9,16,256]{4,3,2,1,0:T(8,128)(2,1)S(1)}, bf16[4,4,9,16,256]{4,3,2,1,0:T(8,128)(2,1)S(1)}, u32[]{:S(2)}, u32[]{:S(2)}) collective-permute-start(bf16[4,4,9,16,256]{4,3,2,1,0:T(8,128)(2,1)S(1)} %correlate.3), channel_id=1, source_target_pairs={{0,4},{4,0},{8,12},{12,8},{16,20},{20,16},{24,28},{28,24},{1,5},{5... | collective-permute-start | bytes 3538952 | tf_op jit(solution)/shard_map/ppermute | solution.py:201
